TPU v7x, 32 devices: a whole 2x2x4 slice. The times are simulated.
32 devices in a mesh: dp: 8 (over y, x, core), tensor: 4 (over z).
Axes of the slice: x: 2, y: 2, z: 4, core: 2. Of those that a mesh axis runs over, the one named last changes fastest.
Arguments:
- layer_input: bfloat16 [16384, 1024], P('dp'), may hold values from -6 to 6
- output_grad: bfloat16 [16384, 1024], P('dp'), may hold values from -6 to 6
- segments: int32 [8, 2048], P('dp'), may hold values from 0 to 15, never falling along the last dimension, each value on 1 to 1024 neighbouring positions
- adapter_ids: int32 [8, 1], P('dp'), may hold values from 0 to 7
- ln_gain: float32 [2, 1024], replicated, may hold values from 0.5 to 1.5
- ln_bias: float32 [2, 1024], replicated, may hold values from -3 to 3
- w_qkv: bfloat16 [3, 1024, 1024], P(None, None, 'tensor'), may hold values from -0.1875 to 0.1875
- w_out: bfloat16 [1024, 1024], P('tensor'), may hold values from -1 to 1
- w_gate_up: bfloat16 [2, 1024, 4096], P(None, None, 'tensor'), may hold values from -0.1875 to 0.1875
- w_down: bfloat16 [4096, 1024], P('tensor'), may hold values from -0.09375 to 0.09375
- qkv_a: bfloat16 [8, 48, 1024], replicated, may hold values from -0.1875 to 0.1875
- qkv_b: bfloat16 [8, 48, 1024], P(None, None, 'tensor'), may hold values from -0.75 to 0.75
- out_a: bfloat16 [8, 16, 1024], P(None, None, 'tensor'), may hold values from -1 to 1
- out_b: bfloat16 [8, 16, 1024], replicated, may hold values from -0.75 to 0.75
- ffn_a: bfloat16 [8, 32, 1024], replicated, may hold values from -0.1875 to 0.1875
- ffn_b: bfloat16 [8, 32, 4096], P(None, None, 'tensor'), may hold values from -0.75 to 0.75
- down_a: bfloat16 [8, 16, 4096], P(None, None, 'tensor'), may hold values from -0.09375 to 0.09375
- down_b: bfloat16 [8, 16, 1024], replicated, may hold values from -0.75 to 0.75
Outputs:
- layer_output: bfloat16 [16384, 1024], P('dp')
- input_grad: float32 [16384, 1024], P('dp')
- qkv_a_grad: float32 [8, 48, 1024], replicated
- qkv_b_grad: float32 [8, 48, 1024], P(None, None, 'tensor')
- out_a_grad: float32 [8, 16, 1024], P(None, None, 'tensor')
- out_b_grad: float32 [8, 16, 1024], replicated
- ffn_a_grad: float32 [8, 32, 1024], replicated
- ffn_b_grad: float32 [8, 32, 4096], P(None, None, 'tensor')
- down_a_grad: float32 [8, 16, 4096], P(None, None, 'tensor')
- down_b_grad: float32 [8, 16, 1024], replicated
Inputs may be any that keep to these rules, and one draw needn't show every extreme that they name: In each sequence segment numbers never fall; each of the 16 segments holds 1 to 1024 tokens, and one holds exactly 1024. `adapter_ids`: every adapter is named by some sequence.
All inputs are finite; a program needn't handle non-finite values.
Results may differ from a plain program's by a relative error of at most 0.022.
Values may be sent and summed in bfloat16 or wider, within the bound.
No kernel may reach another device: no remote copies, remote signals or barrier semaphores. Data moves between devices by JAX's collectives and lax.ppermute only.
A program may use at most 256 MiB of HBM per device.

v0:
```python
import jax
import jax.numpy as jnp
from jax import lax
from jax.sharding import PartitionSpec as P

HEAD_DIM = 64


def widen(latent, one_hot):
    widened = one_hot[:, :, None] * latent[:, None, :]
    return widened.reshape(latent.shape[0], -1)


def reduce_rank(rows, stack, one_hot):
    full = jnp.einsum("ti,aki->tak", rows, stack, preferred_element_type=jnp.float32)
    return jnp.sum(full * one_hot.astype(jnp.float32)[:, :, None], axis=1)


def expand_rank(latent, stack, one_hot):
    return jnp.dot(
        widen(latent, one_hot),
        stack.reshape(-1, stack.shape[2]),
        preferred_element_type=jnp.float32,
    )


def rank_grad(grads, stack, one_hot):
    full = jnp.einsum("to,ako->tak", grads, stack, preferred_element_type=jnp.float32)
    return jnp.sum(full * one_hot.astype(jnp.float32)[:, :, None], axis=1)


def stack_grad(latent, one_hot, grads):
    product = jnp.einsum(
        "tk,to->ko", widen(latent, one_hot), grads, preferred_element_type=jnp.float32
    )
    return product.reshape(one_hot.shape[1], latent.shape[1], grads.shape[1])


def norm_forward(rows, gain, shift):
    centre = jnp.mean(rows, axis=-1, keepdims=True)
    centred = rows - centre
    spread = jnp.mean(centred * centred, axis=-1, keepdims=True)
    inverse = lax.rsqrt(spread + 1e-12)
    normed = centred * inverse
    return (normed * gain + shift, normed, inverse)


def norm_backward(grads, normed, inverse, gain):
    scaled = grads * gain
    first_mean = jnp.mean(scaled, axis=-1, keepdims=True)
    second_mean = jnp.mean(scaled * normed, axis=-1, keepdims=True)
    return inverse * (scaled - first_mean - normed * second_mean)


def rope_tables(total, length, head_dim):
    half_dim = head_dim // 2
    positions = (jnp.arange(total, dtype=jnp.int32) % length).astype(jnp.float32)
    freq = 10000.0 ** (-(2.0 * jnp.arange(half_dim, dtype=jnp.float32)) / head_dim)
    angle = positions[:, None] * freq[None, :]
    return (jnp.cos(angle)[:, None, :], jnp.sin(angle)[:, None, :])


def rotate(values, cosine, sine):
    half_dim = values.shape[-1] // 2
    first_half = values[..., :half_dim]
    second_half = values[..., half_dim:]
    return jnp.concatenate(
        [first_half * cosine - second_half * sine, second_half * cosine + first_half * sine],
        axis=-1,
    )


def rotate_back(grads, cosine, sine):
    half_dim = grads.shape[-1] // 2
    first_half = grads[..., :half_dim]
    second_half = grads[..., half_dim:]
    return jnp.concatenate(
        [first_half * cosine + second_half * sine, second_half * cosine - first_half * sine],
        axis=-1,
    )


def body(
    layer_input,
    output_grad,
    segments,
    adapter_ids,
    ln_gain,
    ln_bias,
    w_qkv,
    w_out,
    w_gate_up,
    w_down,
    qkv_a,
    qkv_b,
    out_a,
    out_b,
    ffn_a,
    ffn_b,
    down_a,
    down_b,
):
    seq_count, length = segments.shape
    total = layer_input.shape[0]
    rank = out_b.shape[1]
    adapter_count = qkv_a.shape[0]
    head_dim = HEAD_DIM
    local_width = w_qkv.shape[2]
    local_heads = local_width // head_dim
    shard_rows = total // lax.axis_size("tensor")
    row_start = lax.axis_index("tensor") * shard_rows
    block = min(512, length)
    count = length // block
    scale = head_dim ** (-0.5)
    seq_hot = (
        adapter_ids[:, 0][:, None] == jnp.arange(adapter_count, dtype=jnp.int32)[None, :]
    ).astype(jnp.bfloat16)
    row_hot = jnp.repeat(seq_hot, length, axis=0)
    shard_hot = lax.dynamic_slice_in_dim(row_hot, row_start, shard_rows, 0)
    input_shard_b = lax.dynamic_slice_in_dim(layer_input, row_start, shard_rows, 0)
    input_shard = input_shard_b.astype(jnp.float32)
    latent_qkv = reduce_rank(layer_input, qkv_a, row_hot).astype(jnp.bfloat16)
    projected = jnp.einsum("ti,pio->pto", layer_input, w_qkv, preferred_element_type=jnp.float32)
    cosine, sine = rope_tables(total, length, head_dim)

    def part_value(part):
        piece = latent_qkv[:, part * rank : (part + 1) * rank]
        return projected[part] + expand_rank(
            piece, qkv_b[:, part * rank : (part + 1) * rank, :], row_hot
        )

    query_b = rotate(part_value(0).reshape(total, local_heads, head_dim), cosine, sine).astype(
        jnp.bfloat16
    )
    keys_b = rotate(part_value(1).reshape(total, local_heads, head_dim), cosine, sine).astype(
        jnp.bfloat16
    )
    values_b = part_value(2).astype(jnp.bfloat16)

    def to_heads(array):
        return array.reshape(seq_count, length, local_heads, head_dim).transpose(0, 2, 1, 3)

    def from_heads(array):
        return array.transpose(0, 2, 1, 3).reshape(total, local_heads, head_dim)

    query_heads = to_heads(query_b)
    keys_heads = to_heads(keys_b)
    values_heads = to_heads(values_b)

    def forward_sequence(item):
        rows_all, keys, values, labels = item

        def one_block(index):
            start = index * block
            rows = lax.dynamic_slice_in_dim(rows_all, start, block, 1)
            row_labels = lax.dynamic_slice_in_dim(labels, start, block, 0)
            scores = (
                jnp.einsum("hqd,hkd->hqk", rows, keys, preferred_element_type=jnp.float32) * scale
            )
            same = row_labels[:, None] == labels[None, :]
            scores = jnp.where(same[None], scores, -1e30)
            top = jnp.max(scores, axis=-1, keepdims=True)
            expo = jnp.exp(scores - top)
            weight_sum = jnp.sum(expo, axis=-1, keepdims=True)
            weights = (expo / weight_sum).astype(jnp.bfloat16)
            mixed = jnp.einsum(
                "hqk,hkd->hqd", weights, values, preferred_element_type=jnp.float32
            ).astype(jnp.bfloat16)
            return (mixed, top[..., 0] + jnp.log(weight_sum[..., 0]))

        return lax.map(one_block, jnp.arange(count, dtype=jnp.int32))

    mixed_blocks, log_sums = lax.map(
        forward_sequence, (query_heads, keys_heads, values_heads, segments)
    )
    mixed_b = mixed_blocks.transpose(0, 1, 3, 2, 4).reshape(total, local_width)
    partial_out = jnp.dot(mixed_b, w_out, preferred_element_type=jnp.float32)
    latent_part = reduce_rank(mixed_b, out_a, row_hot)
    attn_total, latent_total = (
        lax.psum_scatter(partial_out, "tensor", scatter_dimension=0, tiled=True),
        lax.psum_scatter(latent_part, "tensor", scatter_dimension=0, tiled=True),
    )
    latent_out_b = latent_total.astype(jnp.bfloat16)
    branch = attn_total + expand_rank(latent_out_b, out_b, shard_hot)
    hidden, normed_one, inverse_one = norm_forward(input_shard + branch, ln_gain[0], ln_bias[0])
    hidden_b = hidden.astype(jnp.bfloat16)
    hidden_all = lax.all_gather(hidden_b, "tensor", axis=0, tiled=True)
    latent_ffn = reduce_rank(hidden_all, ffn_a, row_hot).astype(jnp.bfloat16)
    gate = jnp.dot(hidden_all, w_gate_up[0], preferred_element_type=jnp.float32) + expand_rank(
        latent_ffn[:, :rank], ffn_b[:, :rank, :], row_hot
    )
    upward = jnp.dot(hidden_all, w_gate_up[1], preferred_element_type=jnp.float32) + expand_rank(
        latent_ffn[:, rank:], ffn_b[:, rank:, :], row_hot
    )
    sigma = jax.nn.sigmoid(gate)
    swish = gate * sigma
    active_b = (swish * upward).astype(jnp.bfloat16)
    partial_ffn = jnp.dot(active_b, w_down, preferred_element_type=jnp.float32)
    latent_down_part = reduce_rank(active_b, down_a, row_hot)
    ffn_total, latent_down_total = (
        lax.psum_scatter(partial_ffn, "tensor", scatter_dimension=0, tiled=True),
        lax.psum_scatter(latent_down_part, "tensor", scatter_dimension=0, tiled=True),
    )
    latent_down_b = latent_down_total.astype(jnp.bfloat16)
    branch_ffn = ffn_total + expand_rank(latent_down_b, down_b, shard_hot)
    result, normed_two, inverse_two = norm_forward(hidden + branch_ffn, ln_gain[1], ln_bias[1])
    output = lax.all_gather(result.astype(jnp.bfloat16), "tensor", axis=0, tiled=True)
    cotangent_shard = lax.dynamic_slice_in_dim(output_grad, row_start, shard_rows, 0).astype(
        jnp.float32
    )
    grad_mid = norm_backward(cotangent_shard, normed_two, inverse_two, ln_gain[1])
    grad_ffn_b = grad_mid.astype(jnp.bfloat16)
    down_b_part = stack_grad(latent_down_b, shard_hot, grad_ffn_b)
    latent_down_grad = rank_grad(grad_ffn_b, down_b, shard_hot).astype(jnp.bfloat16)
    grad_all, latent_down_all = (
        lax.all_gather(grad_ffn_b, "tensor", axis=0, tiled=True),
        lax.all_gather(latent_down_grad, "tensor", axis=0, tiled=True),
    )
    down_a_grad = stack_grad(latent_down_all, row_hot, active_b)
    grad_active = jnp.einsum(
        "to,fo->tf", grad_all, w_down, preferred_element_type=jnp.float32
    ) + expand_rank(latent_down_all, down_a, row_hot)
    grad_gate = (grad_active * upward * sigma * (1.0 + gate * (1.0 - sigma))).astype(jnp.bfloat16)
    grad_up = (grad_active * swish).astype(jnp.bfloat16)
    ffn_b_grad = jnp.concatenate(
        [
            stack_grad(latent_ffn[:, :rank], row_hot, grad_gate),
            stack_grad(latent_ffn[:, rank:], row_hot, grad_up),
        ],
        axis=1,
    )
    grad_hidden_part = jnp.einsum(
        "tf,if->ti", grad_gate, w_gate_up[0], preferred_element_type=jnp.float32
    ) + jnp.einsum("tf,if->ti", grad_up, w_gate_up[1], preferred_element_type=jnp.float32)
    latent_ffn_part = jnp.concatenate(
        [
            rank_grad(grad_gate, ffn_b[:, :rank, :], row_hot),
            rank_grad(grad_up, ffn_b[:, rank:, :], row_hot),
        ],
        axis=1,
    )
    hidden_total, latent_ffn_total = (
        lax.psum_scatter(grad_hidden_part, "tensor", scatter_dimension=0, tiled=True),
        lax.psum_scatter(latent_ffn_part, "tensor", scatter_dimension=0, tiled=True),
    )
    latent_ffn_grad = latent_ffn_total.astype(jnp.bfloat16)
    grad_hidden = grad_mid + hidden_total + expand_rank(latent_ffn_grad, ffn_a, shard_hot)
    ffn_a_part = stack_grad(latent_ffn_grad, shard_hot, hidden_b)
    grad_first = norm_backward(grad_hidden, normed_one, inverse_one, ln_gain[0])
    grad_branch_b = grad_first.astype(jnp.bfloat16)
    out_b_part = stack_grad(latent_out_b, shard_hot, grad_branch_b)
    latent_out_grad = rank_grad(grad_branch_b, out_b, shard_hot).astype(jnp.bfloat16)
    branch_all, latent_out_all = (
        lax.all_gather(grad_branch_b, "tensor", axis=0, tiled=True),
        lax.all_gather(latent_out_grad, "tensor", axis=0, tiled=True),
    )
    out_a_grad = stack_grad(latent_out_all, row_hot, mixed_b)
    grad_mixed = (
        jnp.einsum("to,io->ti", branch_all, w_out, preferred_element_type=jnp.float32)
        + expand_rank(latent_out_all, out_a, row_hot)
    ).astype(jnp.bfloat16)
    grad_heads = to_heads(grad_mixed)

    def backward_sequence(item):
        rows_all, keys, values, grads_all, labels, logs = item

        def split_blocks(array):
            return array.reshape(local_heads, count, block, head_dim).transpose(1, 0, 2, 3)

        def step(carry, piece):
            grad_keys, grad_values = carry
            rows, grads, row_labels, log_rows = piece
            scores = (
                jnp.einsum("hqd,hkd->hqk", rows, keys, preferred_element_type=jnp.float32) * scale
            )
            same = row_labels[:, None] == labels[None, :]
            scores = jnp.where(same[None], scores, -1e30)
            prob = jnp.exp(scores - log_rows[:, :, None])
            grad_prob = jnp.einsum(
                "hqd,hkd->hqk", grads, values, preferred_element_type=jnp.float32
            )
            delta = jnp.sum(prob * grad_prob, axis=-1, keepdims=True)
            grad_score = (prob * (grad_prob - delta) * scale).astype(jnp.bfloat16)
            grad_rows = jnp.einsum(
                "hqk,hkd->hqd", grad_score, keys, preferred_element_type=jnp.float32
            )
            grad_keys = grad_keys + jnp.einsum(
                "hqk,hqd->hkd", grad_score, rows, preferred_element_type=jnp.float32
            )
            grad_values = grad_values + jnp.einsum(
                "hqk,hqd->hkd", prob.astype(jnp.bfloat16), grads, preferred_element_type=jnp.float32
            )
            return ((grad_keys, grad_values), grad_rows)

        zeros = jnp.zeros(keys.shape, jnp.float32)
        label_blocks = labels.reshape(count, block)
        (grad_keys, grad_values), grad_blocks = lax.scan(
            step,
            (zeros, zeros),
            (split_blocks(rows_all), split_blocks(grads_all), label_blocks, logs),
        )
        grad_query = grad_blocks.transpose(1, 0, 2, 3).reshape(keys.shape)
        return (grad_query, grad_keys, grad_values)

    grad_query_h, grad_keys_h, grad_values_h = lax.map(
        backward_sequence, (query_heads, keys_heads, values_heads, grad_heads, segments, log_sums)
    )
    grad_query = rotate_back(from_heads(grad_query_h).astype(jnp.bfloat16), cosine, sine).astype(
        jnp.bfloat16
    )
    grad_keys = rotate_back(from_heads(grad_keys_h).astype(jnp.bfloat16), cosine, sine).astype(
        jnp.bfloat16
    )
    grad_values = from_heads(grad_values_h).astype(jnp.bfloat16)
    grad_parts = jnp.stack(
        [
            grad_query.reshape(total, local_width),
            grad_keys.reshape(total, local_width),
            grad_values.reshape(total, local_width),
        ]
    )
    qkv_b_grad = jnp.concatenate(
        [
            stack_grad(latent_qkv[:, part * rank : (part + 1) * rank], row_hot, grad_parts[part])
            for part in range(3)
        ],
        axis=1,
    )
    grad_input_part = jnp.einsum(
        "pto,pio->ti", grad_parts, w_qkv, preferred_element_type=jnp.float32
    )
    latent_qkv_part = jnp.concatenate(
        [
            rank_grad(grad_parts[part], qkv_b[:, part * rank : (part + 1) * rank, :], row_hot)
            for part in range(3)
        ],
        axis=1,
    )
    input_total, latent_qkv_total = (
        lax.psum_scatter(
            grad_input_part.astype(jnp.bfloat16), "tensor", scatter_dimension=0, tiled=True
        ).astype(jnp.float32),
        lax.psum_scatter(
            latent_qkv_part.astype(jnp.bfloat16), "tensor", scatter_dimension=0, tiled=True
        ).astype(jnp.float32),
    )
    latent_qkv_grad = latent_qkv_total.astype(jnp.bfloat16)
    grad_input = grad_first + input_total + expand_rank(latent_qkv_grad, qkv_a, shard_hot)
    qkv_a_part = stack_grad(latent_qkv_grad, shard_hot, input_shard_b)
    grad_whole = lax.all_gather(
        grad_input.astype(jnp.bfloat16), "tensor", axis=0, tiled=True
    ).astype(grad_input.dtype)
    shared = lax.psum((qkv_a_part, out_b_part, ffn_a_part, down_b_part), ("dp", "tensor"))
    sharded = (
        lax.psum(qkv_b_grad.astype(jnp.bfloat16), "dp").astype(jnp.float32),
        lax.psum(out_a_grad.astype(jnp.bfloat16), "dp").astype(jnp.float32),
        lax.psum(ffn_b_grad.astype(jnp.bfloat16), "dp").astype(jnp.float32),
        lax.psum(down_a_grad.astype(jnp.bfloat16), "dp").astype(jnp.float32),
    )
    return (
        output,
        grad_whole,
        shared[0],
        sharded[0],
        sharded[1],
        shared[1],
        shared[2],
        sharded[2],
        sharded[3],
        shared[3],
    )


def solution(mesh):
    in_specs = (
        P("dp", None),
        P("dp", None),
        P("dp", None),
        P("dp", None),
        P(),
        P(),
        P(None, None, "tensor"),
        P("tensor", None),
        P(None, None, "tensor"),
        P("tensor", None),
        P(),
        P(None, None, "tensor"),
        P(None, None, "tensor"),
        P(),
        P(),
        P(None, None, "tensor"),
        P(None, None, "tensor"),
        P(),
    )
    out_specs = (
        P("dp", None),
        P("dp", None),
        P(),
        P(None, None, "tensor"),
        P(None, None, "tensor"),
        P(),
        P(),
        P(None, None, "tensor"),
        P(None, None, "tensor"),
        P(),
    )
    return jax.shard_map(body, mesh=mesh, in_specs=in_specs, out_specs=out_specs, check_vma=False)
```

profile of v0, /device:TPU:0, one launch (start us, length us, event | category | flops | bytes accessed | tf_op | source)
XLA Modules:
  0.0 1741.0 jit_solution(5210742664421289885)
XLA Ops:
  8.1 4.4 multiply_reduce_fusion.1
  26.9 69.5 %while.47 = (s32[]{:T(128)}, bf16[4,4,512,64]{2,3,1,0:T(8,128)(2,1)}, f32[4,4,512]{2,1,0:T(4,128)}, s32[4]{0:T(128)S(1)}, s32[2048]{0:T(1024)S(1)}, /*index=5*/b...) while((s32[]{:T(128)}, ...), condition=%wide.region_4.5_spmd, body=%wide.region_1.4_spmd.sunk | while | flops 1125251072 | bytes 61422800 | solution.py:171
  29.2 4.4 fusion.326
  33.6 4.3 fusion.327
  38.6 5.9 fusion.328
  46.5 4.4 fusion.326
  50.9 4.3 fusion.327
  55.9 5.9 fusion.328
  63.8 4.4 fusion.326
  68.2 4.3 fusion.327
  73.2 5.9 fusion.328
  81.1 4.4 fusion.326
  85.5 4.3 fusion.327
  90.5 5.9 fusion.328
  101.1 6.0 fusion.252
  107.9 15.5 reduce-scatter.11.cloned.1.call-done
  124.2 145.0 %reduce-scatter.9.cloned.1.call-done = f32[512,1024]{1,0:T(8,128)} async-done(((f32[2048,1024]{1,0:T(8,128)}), f32[512,1024]{1,0:T(8,128)}) %reduce-scatter.9.cloned.1.call-update) | async-done | bytes 2097168 | tf_op jit(solution)/shard_map/reduce_scatter | solution.py:180
  275.0 80.9 %all-gather.6.cloned.1.call-done = bf16[2048,1024]{1,0:T(8,128)(2,1)} async-done(((bf16[512,1024]{1,0:T(8,128)(2,1)}), bf16[2048,1024]{1,0:T(8,128)(2,1)}) %all-gather.6.cloned.1.call-update) | async-done | bytes 4194320 | tf_op jit(solution)/shard_map/all_gather | solution.py:187
  360.6 4.5 fusion.134
  366.6 4.5 fusion.130
  371.1 4.9 multiply_convert_fusion.3
  380.3 9.0 fusion.253
  389.3 9.0 reduce-scatter.15.cloned.1.call-done
  399.1 144.3 %reduce-scatter.13.cloned.1.call-done = f32[512,1024]{1,0:T(8,128)} async-done(((f32[2048,1024]{1,0:T(8,128)}), f32[512,1024]{1,0:T(8,128)}) %reduce-scatter.13.cloned.1.call-update) | async-done | bytes 2097168 | tf_op jit(solution)/shard_map/reduce_scatter | solution.py:201
  551.8 14.3 all_gather.24
  566.1 65.6 %all-gather.10.cloned.1.call-done = bf16[2048,1024]{1,0:T(8,128)(2,1)} async-done(((bf16[512,1024]{1,0:T(8,128)(2,1)}), bf16[2048,1024]{1,0:T(8,128)(2,1)}) %all-gather.10.cloned.1.call-update) | async-done | bytes 4194320 | tf_op jit(solution)/shard_map/all_gather | solution.py:216
  631.7 9.2 fusion.254
  640.9 10.6 multiply_convert_fusion.1
  651.6 6.9 fusion.132
  662.7 13.3 convolution_add_fusion
  676.1 4.9 reduce-scatter.19.cloned.1.call-done
  681.8 144.9 %reduce-scatter.17.cloned.1.call-done = f32[512,1024]{1,0:T(8,128)} async-done(((f32[2048,1024]{1,0:T(8,128)}), f32[512,1024]{1,0:T(8,128)}) %reduce-scatter.17.cloned.1.call-update) | async-done | bytes 2097168 | tf_op jit(solution)/shard_map/reduce_scatter | solution.py:243
  837.8 15.3 all_gather.26
  853.0 62.0 %all-gather.12.cloned.1.call-done = bf16[2048,1024]{1,0:T(8,128)(2,1)} async-done(((bf16[512,1024]{1,0:T(8,128)(2,1)}), bf16[2048,1024]{1,0:T(8,128)(2,1)}) %all-gather.12.cloned.1.call-update) | async-done | bytes 4194320 | tf_op jit(solution)/shard_map/all_gather | solution.py:254
  923.1 326.9 %while.48 = (s32[]{:T(128)}, f32[4,2048,64]{1,2,0:T(8,128)}, f32[4,2048,64]{1,2,0:T(8,128)}, bf16[4,4,512,64]{2,3,1,0:T(8,128)(2,1)}, s32[4,512]{1,0:T(4,128)S(1...) while((s32[]{:T(128)}, f32[4,2048,64]{1,2,0:T(8,128)}, ...), condition=%wide.region_28.29_spmd.clone, body=%wide.region_26.28_spmd.clone.sunk | while | flops 2796560384 | bytes 204022416 | solution.py:297
  923.3 9.1 fusion.340
  932.4 9.1 fusion.339
  942.8 25.5 %fusion.341 = f32[4,2048,64]{1,2,0:T(8,128)} fusion(f32[4,512,2048]{2,1,0:T(8,128)} %fusion.339, f32[4,512,2048]{2,1,0:T(8,128)} %fusion.340, f32[4,512]{1,0:T(4,128)S(1)} %dynamic-slice_bitcast_fusion.2, pred[512,2048]{1,0:T(8,128)(4,1)S(1)} %broadcast_compare_fusion.5, f32[4,2048,64]{1,2,0:T(8,128)} %get-tuple-element.486, pred[]{:T(512)S(6)} %compare.4, ...), kind=kOutput, calls=%fused_computation.35.clone.1 | convolution fusion | flops 584060928 | bytes 73679360 | tf_op jit(solution)/shard_map/while/body/eval_jaxpr/while/body/eval_jaxpr/hqk,hqd->hkd/dot_general | solution.py:287
  968.3 24.0 %fusion.343 = bf16[4,4,512,64]{2,3,1,0:T(8,128)(2,1)} fusion(bf16[4,4,512,64]{2,3,1,0:T(8,128)(2,1)} %get-tuple-element.488, s32[]{:T(128)} %get-tuple-element.485, bf16[4,2048,64]{1,2,0:T(8,128)(2,1)S(1)} %get-tuple-element.505, f32[4,512,2048]{2,1,0:T(8,128)} %fusion.339, f32[4,512,2048]{2,1,0:T(8,128)} %fusion.340, ...), kind=kOutput, calls=%fused_computation.38.clone.1 | convolution fusion | flops 583012352 | bytes 70795776 | tf_op jit(solution)/shard_map/while/body/eval_jaxpr/while/body/eval_jaxpr/hqk,hkd->hqd/dot_general | solution.py:284
  992.3 11.8 fusion.342
  1004.0 9.1 fusion.340
  1013.1 9.1 fusion.339
  1023.6 26.0 %fusion.341 = f32[4,2048,64]{1,2,0:T(8,128)} fusion(f32[4,512,2048]{2,1,0:T(8,128)} %fusion.339, f32[4,512,2048]{2,1,0:T(8,128)} %fusion.340, f32[4,512]{1,0:T(4,128)S(1)} %dynamic-slice_bitcast_fusion.2, pred[512,2048]{1,0:T(8,128)(4,1)S(1)} %broadcast_compare_fusion.5, f32[4,2048,64]{1,2,0:T(8,128)} %get-tuple-element.486, pred[]{:T(512)S(6)} %compare.4, ...), kind=kOutput, calls=%fused_computation.35.clone.1 | convolution fusion | flops 584060928 | bytes 73679360 | tf_op jit(solution)/shard_map/while/body/eval_jaxpr/while/body/eval_jaxpr/hqk,hqd->hkd/dot_general | solution.py:287
  1049.6 24.0 %fusion.343 = bf16[4,4,512,64]{2,3,1,0:T(8,128)(2,1)} fusion(bf16[4,4,512,64]{2,3,1,0:T(8,128)(2,1)} %get-tuple-element.488, s32[]{:T(128)} %get-tuple-element.485, bf16[4,2048,64]{1,2,0:T(8,128)(2,1)S(1)} %get-tuple-element.505, f32[4,512,2048]{2,1,0:T(8,128)} %fusion.339, f32[4,512,2048]{2,1,0:T(8,128)} %fusion.340, ...), kind=kOutput, calls=%fused_computation.38.clone.1 | convolution fusion | flops 583012352 | bytes 70795776 | tf_op jit(solution)/shard_map/while/body/eval_jaxpr/while/body/eval_jaxpr/hqk,hkd->hqd/dot_general | solution.py:284
  1073.6 12.4 fusion.342
  1086.0 9.1 fusion.340
  1095.1 9.1 fusion.339
  1105.5 26.0 %fusion.341 = f32[4,2048,64]{1,2,0:T(8,128)} fusion(f32[4,512,2048]{2,1,0:T(8,128)} %fusion.339, f32[4,512,2048]{2,1,0:T(8,128)} %fusion.340, f32[4,512]{1,0:T(4,128)S(1)} %dynamic-slice_bitcast_fusion.2, pred[512,2048]{1,0:T(8,128)(4,1)S(1)} %broadcast_compare_fusion.5, f32[4,2048,64]{1,2,0:T(8,128)} %get-tuple-element.486, pred[]{:T(512)S(6)} %compare.4, ...), kind=kOutput, calls=%fused_computation.35.clone.1 | convolution fusion | flops 584060928 | bytes 73679360 | tf_op jit(solution)/shard_map/while/body/eval_jaxpr/while/body/eval_jaxpr/hqk,hqd->hkd/dot_general | solution.py:287
  1131.6 24.0 %fusion.343 = bf16[4,4,512,64]{2,3,1,0:T(8,128)(2,1)} fusion(bf16[4,4,512,64]{2,3,1,0:T(8,128)(2,1)} %get-tuple-element.488, s32[]{:T(128)} %get-tuple-element.485, bf16[4,2048,64]{1,2,0:T(8,128)(2,1)S(1)} %get-tuple-element.505, f32[4,512,2048]{2,1,0:T(8,128)} %fusion.339, f32[4,512,2048]{2,1,0:T(8,128)} %fusion.340, ...), kind=kOutput, calls=%fused_computation.38.clone.1 | convolution fusion | flops 583012352 | bytes 70795776 | tf_op jit(solution)/shard_map/while/body/eval_jaxpr/while/body/eval_jaxpr/hqk,hkd->hqd/dot_general | solution.py:284
  1155.5 12.4 fusion.342
  1167.9 9.1 fusion.340
  1177.0 9.1 fusion.339
  1187.5 26.1 %fusion.341 = f32[4,2048,64]{1,2,0:T(8,128)} fusion(f32[4,512,2048]{2,1,0:T(8,128)} %fusion.339, f32[4,512,2048]{2,1,0:T(8,128)} %fusion.340, f32[4,512]{1,0:T(4,128)S(1)} %dynamic-slice_bitcast_fusion.2, pred[512,2048]{1,0:T(8,128)(4,1)S(1)} %broadcast_compare_fusion.5, f32[4,2048,64]{1,2,0:T(8,128)} %get-tuple-element.486, pred[]{:T(512)S(6)} %compare.4, ...), kind=kOutput, calls=%fused_computation.35.clone.1 | convolution fusion | flops 584060928 | bytes 73679360 | tf_op jit(solution)/shard_map/while/body/eval_jaxpr/while/body/eval_jaxpr/hqk,hqd->hkd/dot_general | solution.py:287
  1213.5 24.0 %fusion.343 = bf16[4,4,512,64]{2,3,1,0:T(8,128)(2,1)} fusion(bf16[4,4,512,64]{2,3,1,0:T(8,128)(2,1)} %get-tuple-element.488, s32[]{:T(128)} %get-tuple-element.485, bf16[4,2048,64]{1,2,0:T(8,128)(2,1)S(1)} %get-tuple-element.505, f32[4,512,2048]{2,1,0:T(8,128)} %fusion.339, f32[4,512,2048]{2,1,0:T(8,128)} %fusion.340, ...), kind=kOutput, calls=%fused_computation.38.clone.1 | convolution fusion | flops 583012352 | bytes 70795776 | tf_op jit(solution)/shard_map/while/body/eval_jaxpr/while/body/eval_jaxpr/hqk,hkd->hqd/dot_general | solution.py:284
  1237.5 12.4 fusion.342
  1261.2 7.6 bitcast_convert_fusion
  1279.8 74.3 %reduce-scatter.21.cloned.1.call-done = bf16[512,1024]{1,0:T(8,128)(2,1)} async-done(((bf16[2048,1024]{1,0:T(8,128)(2,1)}), bf16[512,1024]{1,0:T(8,128)(2,1)}) %reduce-scatter.21.cloned.1.call-update) | async-done | bytes 1048592 | tf_op jit(solution)/shard_map/reduce_scatter | solution.py:340
  1354.1 4.0 fusion.126
  1365.9 70.9 %all-gather.8.cloned.1.call-done = bf16[2048,1024]{1,0:T(8,128)(2,1)} async-done(((bf16[512,1024]{1,0:T(8,128)(2,1)}), bf16[2048,1024]{1,0:T(8,128)(2,1)}) %all-gather.8.cloned.1.call-update) | async-done | bytes 4194320 | tf_op jit(solution)/shard_map/all_gather | solution.py:207
  1436.8 60.1 %all-reduce.7.cloned.1.call-done = (bf16[8,48,256]{2,1,0:T(8,128)(2,1)}, bf16[8,16,256]{2,1,0:T(8,128)(2,1)}, bf16[8,32,1024]{2,1,0:T(8,128)(2,1)}, bf16[8,16,1024]{2,1,0:T(8,128)(2,1)}) async-done(((bf16[8,48,256]{2,1,0:T(8,128)(2,1)}, bf16[8,16,256]{2,1,0:T(8,128)(2,1)}, bf16[8,32,1024]{2,1,0:T(8,128)(2,1)}, bf16[8,16,1024]{2,1,0:T(8,128)(2,1)}), (bf16[8,48,256]{2,1,0:T(8,128)(2,1)}, ...) | async-done | bytes 1048592 | tf_op jit(solution)/shard_map/psum | solution.py:355
  1504.1 74.9 %all-gather.14.cloned.1.call-done = bf16[2048,1024]{1,0:T(8,128)(2,1)} async-done(((bf16[512,1024]{1,0:T(8,128)(2,1)}), bf16[2048,1024]{1,0:T(8,128)(2,1)}) %all-gather.14.cloned.1.call-update) | async-done | bytes 4194320 | tf_op jit(solution)/shard_map/all_gather | solution.py:350
  1578.9 6.6 convert_element_type.342
  1585.6 140.0 %all-reduce.5.cloned.1.call-done = (f32[8,48,1024]{2,1,0:T(8,128)}, f32[8,16,1024]{2,1,0:T(8,128)}, f32[8,32,1024]{2,1,0:T(8,128)}, f32[8,16,1024]{2,1,0:T(8,128)}) async-done(((f32[8,48,1024]{2,1,0:T(8,128)}, f32[8,16,1024]{2,1,0:T(8,128)}, f32[8,32,1024]{2,1,0:T(8,128)}, f32[8,16,1024]{2,1,0:T(8,128)}), (f32[8,48,1024]{2,1,0:T(8,128)}, f32[8,16,1024]{2,1,0:T(8,128)}, f32[8,32,1024]{2,1,0:T(8,128)}, ...) | async-done | bytes 3670032 | tf_op jit(solution)/shard_map/psum | solution.py:353
  1725.5 4.8 copy.107
  (333 shorter events, 123.3 us)
Async XLA Ops:
  7.2 373.1 %copy-start = (bf16[1024,1024]{1,0:T(8,128)(2,1)S(1)}, bf16[1024,1024]{1,0:T(8,128)(2,1)}, u32[]{:S(2)}) copy-start(bf16[1024,1024]{1,0:T(8,128)(2,1)} %param.31) | copy-start | bytes 6291460
  7.2 116.2 %reduce-scatter.11.cloned.1.call-start = ((), (), s32[]{:S(2)}) async-start(), calls=%async_computation.9 | async-start | bytes 163840 | tf_op jit(solution)/shard_map/reduce_scatter | solution.py:181
  8.1 4.4 copy-start.77
  8.1 11.7 copy-start.63
  8.1 4.5 copy-start.51
  8.1 4.4 copy-start.71
  12.6 5.4 copy-start.36
  12.6 7.2 copy-start.40
  33.6 5.0 copy-start.4
  50.9 5.0 copy-start.4
  68.2 5.0 copy-start.4
  85.5 5.0 copy-start.4
  96.4 4.7 copy-start.2
  96.4 3.7 copy-start.56
  96.4 3.7 copy-start.78
  101.1 168.1 %reduce-scatter.9.cloned.1.call-start = ((), (), s32[]{:S(2)}) async-start(), calls=%async_computation.8 | async-start | bytes 10485760 | tf_op jit(solution)/shard_map/reduce_scatter | solution.py:180
  107.2 162.0 %copy-start.64 = (bf16[8]{0:T(256)(128)(2,1)S(1)}, bf16[8]{0:T(256)(128)(2,1)}, u32[]{:S(2)}) copy-start(bf16[8]{0:T(256)(128)(2,1)} %copy-done.63) | copy-start | bytes 52
  107.2 162.0 %copy-start.76 = (bf16[8,16,1024]{2,1,0:T(8,128)(2,1)S(1)}, bf16[8,16,1024]{2,1,0:T(8,128)(2,1)}, u32[]{:S(2)}) copy-start(bf16[8,16,1024]{2,1,0:T(8,128)(2,1)} %param.35) | copy-start | bytes 786436
  107.2 248.7 %all-gather.6.cloned.1.call-start = ((), (), s32[]{:S(2)}) async-start(), calls=%async_computation.10 | async-start | bytes 5242880 | tf_op jit(solution)/shard_map/all_gather | solution.py:187
  124.2 147.5 %copy-start.58 = (bf16[512,16]{0,1:T(8,128)(2,1)}, bf16[512,16]{0,1:T(8,128)(2,1)S(1)}, u32[]{:S(2)}) copy-start(bf16[512,16]{0,1:T(8,128)(2,1)S(1)} %convert_element_type.300) | copy-start | bytes 49156
  271.7 84.2 %copy-start.73 = (bf16[8,32,1024]{2,1,0:T(8,128)(2,1)S(1)}, bf16[8,32,1024]{2,1,0:T(8,128)(2,1)}, u32[]{:S(2)}) copy-start(bf16[8,32,1024]{2,1,0:T(8,128)(2,1)} %param.36) | copy-start | bytes 1572868
  274.4 123.9 %reduce-scatter.15.cloned.1.call-start = ((), (), s32[]{:S(2)}) async-start(), calls=%async_computation.12 | async-start | bytes 163840 | tf_op jit(solution)/shard_map/reduce_scatter | solution.py:202
  355.9 3.7 copy-start.68
  355.9 4.7 copy-start.70
  360.6 4.5 copy-start.47
  360.6 10.5 copy-start.49
  360.6 4.5 copy-start.72
  366.6 4.6 copy-start.80
  371.1 6.9 copy-start.74
  380.2 163.1 %reduce-scatter.13.cloned.1.call-start = ((), (), s32[]{:S(2)}) async-start(), calls=%async_computation.11 | async-start | bytes 10485760 | tf_op jit(solution)/shard_map/reduce_scatter | solution.py:201
  389.2 242.5 %all-gather.10.cloned.1.call-start = ((), (), s32[]{:S(2)}) async-start(), calls=%async_computation.14 | async-start | bytes 5242880 | tf_op jit(solution)/shard_map/all_gather | solution.py:216
  399.0 147.6 %copy-start.60 = (bf16[512,16]{0,1:T(8,128)(2,1)}, bf16[512,16]{0,1:T(8,128)(2,1)S(1)}, u32[]{:S(2)}) copy-start(bf16[512,16]{0,1:T(8,128)(2,1)S(1)} %convert_element_type.304) | copy-start | bytes 49156
  543.3 3.7 copy-start.33
  550.0 130.9 %reduce-scatter.19.cloned.1.call-start = ((), (), s32[]{:S(2)}) async-start(), calls=%async_computation.16 | async-start | bytes 327680 | tf_op jit(solution)/shard_map/reduce_scatter | solution.py:244
  566.1 74.8 %copy-start.45 = (bf16[2048,16]{0,1:T(8,128)(2,1)}, bf16[2048,16]{0,1:T(8,128)(2,1)S(1)}, u32[]{:S(2)}) copy-start(bf16[2048,16]{0,1:T(8,128)(2,1)S(1)} %all_gather.24) | copy-start | bytes 196612
  631.7 9.2 copy-start.75
  640.9 10.6 copy-start.69
  651.5 6.9 copy-start.22
  651.5 8.5 copy-start.20
  662.3 164.4 %reduce-scatter.17.cloned.1.call-start = ((), (), s32[]{:S(2)}) async-start(), calls=%async_computation.15 | async-start | bytes 10485760 | tf_op jit(solution)/shard_map/reduce_scatter | solution.py:243
  676.0 150.7 %copy-start.7 = (f32[512,1024]{1,0:T(8,128)S(1)}, f32[512,1024]{1,0:T(8,128)}, u32[]{:S(2)}) copy-start(f32[512,1024]{1,0:T(8,128)} %copy-done.6) | copy-start | bytes 6291460
  676.0 239.0 %all-gather.12.cloned.1.call-start = ((), (), s32[]{:S(2)}) async-start(), calls=%async_computation.17 | async-start | bytes 5242880 | tf_op jit(solution)/shard_map/all_gather | solution.py:254
  681.8 148.8 %copy-start.54 = (bf16[512,32]{0,1:T(8,128)(2,1)}, bf16[512,32]{0,1:T(8,128)(2,1)S(1)}, u32[]{:S(2)}) copy-start(bf16[512,32]{0,1:T(8,128)(2,1)S(1)} %convert_element_type.311) | copy-start | bytes 98308
  826.7 3.9 copy-start.9
  833.0 446.8 %reduce-scatter.23.cloned.1.call-start = ((), (), s32[]{:S(2)}) async-start(), calls=%async_computation.19 | async-start | bytes 245760 | tf_op jit(solution)/shard_map/reduce_scatter | solution.py:343
  833.9 81.2 %copy-start.42 = (bf16[256,1024]{1,0:T(8,128)(2,1)S(1)}, bf16[256,1024]{1,0:T(8,128)(2,1)}, u32[]{:S(2)}) copy-start(bf16[256,1024]{1,0:T(8,128)(2,1)} %param.29) | copy-start | bytes 1572868
  837.7 80.8 %copy-start.57 = (bf16[8,16,256]{2,1,0:T(8,128)(2,1)S(1)}, bf16[8,16,256]{2,1,0:T(8,128)(2,1)}, u32[]{:S(2)}) copy-start(bf16[8,16,256]{2,1,0:T(8,128)(2,1)} %param.34) | copy-start | bytes 196612
  853.0 66.1 %copy-start.38 = (bf16[2048,16]{0,1:T(8,128)(2,1)}, bf16[2048,16]{0,1:T(8,128)(2,1)S(1)}, u32[]{:S(2)}) copy-start(bf16[2048,16]{0,1:T(8,128)(2,1)S(1)} %all_gather.26) | copy-start | bytes 196612
  918.6 4.6 copy-start.3
  918.6 4.6 copy-start.5
  1258.0 96.1 %reduce-scatter.21.cloned.1.call-start = ((), (), s32[]{:S(2)}) async-start(), calls=%async_computation.18 | async-start | bytes 5242880 | tf_op jit(solution)/shard_map/reduce_scatter | solution.py:340
  1268.9 167.9 %all-gather.8.cloned.1.call-start = ((), (), s32[]{:S(2)}) async-start(), calls=%async_computation.13 | async-start | bytes 5242880 | tf_op jit(solution)/shard_map/all_gather | solution.py:207
  1269.4 227.5 %all-reduce.7.cloned.1.call-start = ((), (), s32[]{:S(2)}) async-start(), calls=%async_computation.22 | async-start | bytes 2097152 | tf_op jit(solution)/shard_map/psum | solution.py:355
  1279.7 299.2 %all-gather.14.cloned.1.call-start = ((), (), s32[]{:S(2)}) async-start(), calls=%async_computation.20 | async-start | bytes 5242880 | tf_op jit(solution)/shard_map/all_gather | solution.py:350
  1354.1 4.7 copy-start.59
  1354.1 4.7 copy-start.61
  1354.1 4.8 copy-start.15
  1354.1 5.9 copy-start.55
  1354.1 6.0 copy-start.12
  1358.2 4.5 copy-start.62
  1358.2 367.3 %all-reduce.5.cloned.1.call-start = ((), (), s32[]{:S(2)}) async-start(), calls=%async_computation.21 | async-start | bytes 7340032 | tf_op jit(solution)/shard_map/psum | solution.py:353
  1725.5 4.8 copy-start.29
  1725.5 6.0 copy-start.44
  1725.5 8.5 copy-start.1
  (35 other events, 70.2 us)
Sparse Core Ops, SparseCore 0:
  101.2 22.1 reduce-scatter.10
  126.3 142.8 reduce-scatter.8
  274.5 81.3 all-gather.5
  380.3 17.9 reduce-scatter.14
  400.5 142.8 reduce-scatter.12
  550.1 81.5 all-gather.9
  662.4 18.4 reduce-scatter.18
  683.9 142.8 reduce-scatter.16
  833.1 81.9 all-gather.11
  1258.1 17.9 reduce-scatter.22
  1279.0 75.0 reduce-scatter.20
  1355.5 81.2 all-gather.7
  1441.4 55.5 all-reduce.6
  1498.9 79.9 all-gather.13
  1585.9 139.5 all-reduce.4
where the time goes:
time: 1750 us; the launch traced here: 1740 us
  waiting for transfers between devices  1090 us (62%)
  matrix products  499 us (29%)
  other arithmetic  61.2 us (3%)
  local copies, waits for them, and re-layouts  36.3 us (2%)
  blocking collectives  29.5 us (2%)
    reduce_scatter x1, waiting for transfers between devices, body(): lax.psum_scatter(partial_out, 'tensor', scatter_dimension=0, tiled=True)  145 us
    reduce_scatter x1, waiting for transfers between devices, body(): lax.psum_scatter(grad_hidden_part, 'tensor', scatter_dimension=0, tiled=T...  145 us
    reduce_scatter x1, waiting for transfers between devices, body(): lax.psum_scatter(partial_ffn, 'tensor', scatter_dimension=0, tiled=True)  144 us
    psum x1, waiting for transfers between devices, body(): lax.psum((qkv_a_part, out_b_part, ffn_a_part, down_b_part), ('dp', 'tenso...  140 us
    dot_general x4, matrix products, step(): jnp.einsum('hqk,hqd->hkd', grad_score, rows, preferred_element_type=jnp.f...  104 us
    dot_general x4, matrix products, step(): jnp.einsum('hqk,hkd->hqd', grad_score, keys, preferred_element_type=jnp.f...  95.9 us
    all_gather x1, waiting for transfers between devices, body(): hidden_all = lax.all_gather(hidden_b, 'tensor', axis=0, tiled=True)  80.9 us
    all_gather x1, waiting for transfers between devices, body(): lax.all_gather(grad_input.astype(jnp.bfloat16), 'tensor', axis=0, tiled=T...  74.9 us
  transfers between devices with their start and end apart: 15, of which 14 were waited for; matrix products, arithmetic and copies ran while one was open for 5% of the time, Pallas kernels for 0%

commit v1 on v0

v1 whole, which is shorter than its diff:
```python
import jax
import jax.numpy as jnp
import numpy as np
from jax import lax
from jax.experimental import pallas as pl
from jax.experimental.pallas import tpu as pltpu
from jax.sharding import Mesh
from jax.sharding import PartitionSpec as P

HEAD_DIM = 64
LANES = 128
DP = ("yx", "core")
ALL = ("tensor", "yx", "core")
F32 = jnp.float32
BF16 = jnp.bfloat16


def nt(left, right):
    return lax.dot_general(left, right, (((1,), (1,)), ((), ())), preferred_element_type=F32)


def tn(left, right):
    return lax.dot_general(left, right, (((0,), (0,)), ((), ())), preferred_element_type=F32)


def nn(left, right):
    return jnp.dot(left, right, preferred_element_type=F32)


def roll_rows(rows, shift, count, dtype):
    length, width = rows.shape
    block = LANES
    blocks = length // block
    shift = lax.rem(shift + length, length)
    first = shift // block
    scalars = jnp.stack([first, shift - first * block]).astype(jnp.int32)

    def kernel(scalar_ref, low_ref, high_ref, out_ref):
        offset = scalar_ref[1]
        row = lax.broadcasted_iota(jnp.int32, (block, block), 0)
        column = lax.broadcasted_iota(jnp.int32, (block, block), 1)
        low = jnp.where(column == row + offset, 1.0, 0.0).astype(BF16)
        high = jnp.where(column + block == row + offset, 1.0, 0.0).astype(BF16)
        out_ref[...] = (nn(low, low_ref[...]) + nn(high, high_ref[...])).astype(dtype)

    return pl.pallas_call(
        kernel,
        grid_spec=pltpu.PrefetchScalarGridSpec(
            num_scalar_prefetch=1,
            grid=(count // block,),
            in_specs=[
                pl.BlockSpec((block, width), lambda i, s: (lax.rem(s[0] + i, blocks), 0)),
                pl.BlockSpec((block, width), lambda i, s: (lax.rem(s[0] + i + 1, blocks), 0)),
            ],
            out_specs=pl.BlockSpec((block, width), lambda i, s: (i, 0)),
        ),
        out_shape=jax.ShapeDtypeStruct((count, width), dtype),
        cost_estimate=pl.CostEstimate(
            flops=4 * count * block * width, bytes_accessed=8 * count * width, transcendentals=0
        ),
        name="roll_rows",
    )(scalars, rows, rows)


def spin(values, cosine, sine):
    lane = lax.broadcasted_iota(jnp.int32, (1, LANES), 1)
    first = lax.rem(lane, HEAD_DIM) < HEAD_DIM // 2
    parts = []
    for start in range(0, values.shape[1], LANES):
        piece = values[:, start : start + LANES]
        ahead = pltpu.roll(piece, LANES - HEAD_DIM // 2, 1)
        behind = pltpu.roll(piece, HEAD_DIM // 2, 1)
        parts.append(piece * cosine + jnp.where(first, ahead, behind) * sine)
    return parts[0] if len(parts) == 1 else jnp.concatenate(parts, axis=1)


def project_qkv(group, own, weights, latent, latent_own, factors, tables, tables_own):
    shards, _, width, local = weights.shape
    count, total = own.shape[0], group.shape[0]
    rank = latent.shape[1] // 3
    scale = HEAD_DIM ** (-0.5)

    def kernel(x_ref, o_ref, w_ref, l_ref, lo_ref, f_ref, c_ref, s_ref, co_ref, so_ref, q_ref, k_ref, v_ref):
        x = x_ref[...]
        lat = l_ref[...]
        factor = f_ref[...]
        query = nn(o_ref[...], w_ref[0, 0]) + nn(lo_ref[...][:, :rank], factor[:rank])
        q_ref[...] = (spin(query, co_ref[...], so_ref[...]).astype(BF16) * scale).astype(BF16)
        key = nn(x, w_ref[0, 1]) + nn(lat[:, rank : 2 * rank], factor[rank : 2 * rank])
        k_ref[...] = spin(key, c_ref[...], s_ref[...]).astype(BF16)
        value = nn(x, w_ref[0, 2]) + nn(lat[:, 2 * rank :], factor[2 * rank :])
        v_ref[...] = value.astype(BF16)

    def whole(array):
        return pl.BlockSpec(array.shape, lambda i: (0,) * array.ndim)

    def columns(rows):
        return pl.BlockSpec((rows, local), lambda i: (0, i))

    cosine, sine = tables
    cosine_own, sine_own = tables_own
    return pl.pallas_call(
        kernel,
        grid=(shards,),
        in_specs=[
            whole(group),
            whole(own),
            pl.BlockSpec((1, 3, width, local), lambda i: (i, 0, 0, 0)),
            whole(latent),
            whole(latent_own),
            columns(factors.shape[0]),
            whole(cosine),
            whole(sine),
            whole(cosine_own),
            whole(sine_own),
        ],
        out_specs=[columns(count), columns(total), columns(total)],
        out_shape=[
            jax.ShapeDtypeStruct((count, width), BF16),
            jax.ShapeDtypeStruct((total, width), BF16),
            jax.ShapeDtypeStruct((total, width), BF16),
        ],
        cost_estimate=pl.CostEstimate(
            flops=2 * width * width * (count + 2 * total),
            bytes_accessed=2 * (4 * width * width + 6 * total * width),
            transcendentals=0,
        ),
        name="project_qkv",
    )(group, own, weights, latent, latent_own, factors, cosine, sine, cosine_own, sine_own)


def head_lanes():
    return lax.broadcasted_iota(jnp.int32, (1, LANES), 1) // HEAD_DIM


def attend(query, keys, values, labels_own, labels):
    count, width = query.shape
    total = keys.shape[0]
    pairs = width // LANES

    def kernel(q_ref, k_ref, v_ref, own_ref, all_ref, out_ref, log_ref):
        q = q_ref[...]
        k = k_ref[...]
        flipped = v_ref[...].astype(F32).T
        same = all_ref[...] == own_ref[...]
        lanes = head_lanes()
        sides = lax.broadcasted_iota(jnp.int32, (LANES, 1), 0) // HEAD_DIM
        outs = []
        logs = []
        for head in range(2):
            masked = jnp.where(lanes == head, q, jnp.zeros_like(q))
            scores = jnp.where(same, nt(k, masked), -1e30)
            top = jnp.max(scores, axis=0, keepdims=True)
            expo = jnp.exp(scores - top).astype(BF16)
            stacked = jnp.where(sides == head, flipped, 1.0).astype(BF16)
            product = nn(stacked, expo)
            other = (1 - head) * HEAD_DIM
            weight_sum = product[other : other + 1]
            outs.append(product[head * HEAD_DIM : (head + 1) * HEAD_DIM] / weight_sum)
            logs.append(top + jnp.log(weight_sum))
        out_ref[...] = jnp.concatenate(outs, axis=0).T.astype(BF16)
        log_ref[0, 0:1] = logs[0]
        log_ref[0, 1:2] = logs[1]

    pair = lambda rows: pl.BlockSpec((rows, LANES), lambda i: (0, i))
    return pl.pallas_call(
        kernel,
        grid=(pairs,),
        in_specs=[
            pair(count),
            pair(total),
            pair(total),
            pl.BlockSpec((1, count), lambda i: (0, 0)),
            pl.BlockSpec((total, 1), lambda i: (0, 0)),
        ],
        out_specs=[pair(count), pl.BlockSpec((1, 8, count), lambda i: (i, 0, 0))],
        out_shape=[
            jax.ShapeDtypeStruct((count, width), BF16),
            jax.ShapeDtypeStruct((pairs, 8, count), F32),
        ],
        cost_estimate=pl.CostEstimate(
            flops=16 * count * total * width,
            bytes_accessed=4 * (count + total) * width,
            transcendentals=2 * pairs * count * total,
        ),
        name="attend",
    )(query, keys, values, labels_own[None, :], labels[:, None])


def attend_back(query, keys, values, mixed, grads, logs, labels_own, labels, tables, tables_own):
    count, width = query.shape
    total = keys.shape[0]
    pairs = width // LANES
    scale = HEAD_DIM ** (-0.5)
    cosine, sine = tables
    cosine_own, sine_own = tables_own

    def kernel(q_ref, k_ref, v_ref, m_ref, g_ref, log_ref, own_ref, all_ref, c_ref, s_ref, co_ref, so_ref, dq_ref, dk_ref, dv_ref):
        q = q_ref[...]
        k = k_ref[...]
        v = v_ref[...]
        g = g_ref[...]
        same = all_ref[...] == own_ref[...]
        lanes = head_lanes()
        sides = lax.broadcasted_iota(jnp.int32, (LANES, 1), 0) // HEAD_DIM
        k_flipped = k.astype(F32).T
        product = g.astype(F32) * m_ref[...].astype(F32)
        high = product.astype(BF16)
        low = (product - high.astype(F32)).astype(BF16)
        picks = (
            lax.broadcasted_iota(jnp.int32, (8, LANES), 1) // HEAD_DIM
            == lax.broadcasted_iota(jnp.int32, (8, LANES), 0)
        ).astype(F32).astype(BF16)
        delta = nt(picks, high) + nt(picks, low)
        dq = jnp.zeros((LANES, count), F32)
        dk = jnp.zeros((total, LANES), F32)
        dv = jnp.zeros((total, LANES), F32)
        for head in range(2):
            q_masked = jnp.where(lanes == head, q, jnp.zeros_like(q))
            g_masked = jnp.where(lanes == head, g, jnp.zeros_like(g))
            scores = jnp.where(same, nt(k, q_masked), -1e30)
            prob = jnp.exp(scores - log_ref[0, head : head + 1])
            grad_prob = nt(v, g_masked)
            grad_score = (prob * (grad_prob - delta[head : head + 1])).astype(BF16)
            dv = dv + nn(prob.astype(BF16), g_masked)
            dk = dk + nn(grad_score, q_masked)
            k_side = jnp.where(sides == head, k_flipped, 0.0).astype(BF16)
            dq = dq + nn(k_side, grad_score)
        dq_ref[...] = spin(dq.T * scale, co_ref[...], -so_ref[...]).astype(BF16)
        dk_ref[...] = spin(dk, c_ref[...], -s_ref[...]).astype(BF16)
        dv_ref[...] = dv.astype(BF16)

    pair = lambda rows: pl.BlockSpec((rows, LANES), lambda i: (0, i))

    def whole(array):
        return pl.BlockSpec(array.shape, lambda i: (0,) * array.ndim)

    labels_own = labels_own[None, :]
    labels = labels[:, None]
    return pl.pallas_call(
        kernel,
        grid=(pairs,),
        in_specs=[
            pair(count),
            pair(total),
            pair(total),
            pair(count),
            pair(count),
            pl.BlockSpec((1, 8, count), lambda i: (i, 0, 0)),
            whole(labels_own),
            whole(labels),
            whole(cosine),
            whole(sine),
            whole(cosine_own),
            whole(sine_own),
        ],
        out_specs=[pair(count), pair(total), pair(total)],
        out_shape=[
            jax.ShapeDtypeStruct((count, width), BF16),
            jax.ShapeDtypeStruct((total, width), BF16),
            jax.ShapeDtypeStruct((total, width), BF16),
        ],
        cost_estimate=pl.CostEstimate(
            flops=40 * count * total * width,
            bytes_accessed=2 * (5 * count + 4 * total) * width,
            transcendentals=2 * pairs * count * total,
        ),
        name="attend_back",
    )(query, keys, values, mixed, grads, logs, labels_own, labels, cosine, sine, cosine_own, sine_own)


def norm_forward(rows, gain, shift):
    centre = jnp.mean(rows, axis=-1, keepdims=True)
    centred = rows - centre
    spread = jnp.mean(centred * centred, axis=-1, keepdims=True)
    inverse = lax.rsqrt(spread + 1e-12)
    normed = centred * inverse
    return (normed * gain + shift, normed, inverse)


def norm_backward(grads, normed, inverse, gain):
    scaled = grads * gain
    first_mean = jnp.mean(scaled, axis=-1, keepdims=True)
    second_mean = jnp.mean(scaled * normed, axis=-1, keepdims=True)
    return inverse * (scaled - first_mean - normed * second_mean)


def rope_tables(length, extra):
    half = HEAD_DIM // 2
    step = 64
    freq = 10000.0 ** (-(2.0 * np.arange(half)) / HEAD_DIM)
    freq = np.tile(freq, LANES // half)
    sign = np.where(np.arange(LANES) % HEAD_DIM < half, -1.0, 1.0)
    coarse = ((np.arange(length + extra) % length)[::step, None] * freq).astype(np.float64)
    fine = np.arange(step)[:, None] * freq
    f = lambda array: jnp.asarray(array, F32)
    cos_c, sin_c = f(np.cos(coarse))[:, None], f(np.sin(coarse))[:, None]
    cos_f, sin_f = f(np.cos(fine))[None], f(np.sin(fine))[None]
    cosine = (cos_c * cos_f - sin_c * sin_f).reshape(-1, LANES)
    sine = ((sin_c * cos_f + cos_c * sin_f) * f(sign)).reshape(-1, LANES)
    return cosine, sine


def window(array, start, count):
    return lax.dynamic_slice_in_dim(array, start, count, 0)


def gather_weight(local, parts, part):
    rows = local.shape[0] // parts
    piece = window(local, part * rows, rows)
    return lax.all_gather(piece, ALL, axis=0, tiled=True)


def gather_small(rows, shards, place):
    return lax.all_gather(rows, "tensor", axis=0)


def by_shard(array, shards):
    rows, width = array.shape
    return array.reshape(rows, shards, width // shards).transpose(1, 0, 2)


def reduce_grads(shared, split, hot, unit):
    shards = lax.axis_size("tensor")
    adapters = hot.shape[0]
    pieces = [by_shard(array, shards).reshape(shards, -1, unit) for array in shared + split]
    flag = jnp.zeros((shards, 16, unit), F32).at[:, 0, :adapters].set(hot.astype(F32) / shards)
    packed = jnp.concatenate(pieces + [flag], axis=1).astype(BF16)
    part = lax.psum_scatter(packed, "tensor", scatter_dimension=0, tiled=False)
    every = lax.all_gather(part, DP, axis=0).astype(F32)
    hots = every[:, -16, :adapters]
    placed = jnp.einsum("sj,srn->jrn", hots, every[:, :-16], precision=lax.Precision.HIGHEST)
    sizes = [piece.shape[1] for piece in pieces]
    offsets = np.concatenate([[0], np.cumsum(sizes)])
    cut = offsets[len(shared)]
    outs = []
    if shared:
        whole = lax.all_gather(placed[:, :cut].astype(BF16), "tensor", axis=2, tiled=True).astype(F32)
        for i, array in enumerate(shared):
            outs.append(whole[:, offsets[i] : offsets[i + 1]])
    for i, array in enumerate(split):
        j = len(shared) + i
        outs.append(
            placed[:, offsets[j] : offsets[j + 1]].reshape(adapters, array.shape[0], -1)
        )
    return outs


def body(
    layer_input,
    output_grad,
    segments,
    adapter_ids,
    ln_gain,
    ln_bias,
    w_qkv,
    w_out,
    w_gate_up,
    w_down,
    qkv_a,
    qkv_b,
    out_a,
    out_b,
    ffn_a,
    ffn_b,
    down_a,
    down_b,
):
    seq_count, length = segments.shape
    assert seq_count == 1
    width = layer_input.shape[1]
    shards = lax.axis_size("tensor")
    parts = lax.axis_size(DP)
    place = lax.axis_index("tensor")
    part = lax.axis_index(DP)
    members = shards // 2
    half = length // 2
    count = length // shards
    group = place // members
    member = lax.rem(place, members)
    local = w_qkv.shape[2]
    units = w_down.shape[0]
    rank = out_b.shape[1]

    qkv_all = gather_weight(w_qkv.reshape(3 * width, local), parts, part)
    qkv_all = qkv_all.reshape(shards, 3, width, local)
    out_all = gather_weight(w_out, parts, part)
    up_all = gather_weight(w_gate_up.reshape(2 * width, units), parts, part)
    up_all = up_all.reshape(shards, 2, width, units)
    down_all = gather_weight(w_down, parts, part).reshape(shards, units, width)

    adapter = adapter_ids[0, 0]
    pick = lambda stack: lax.dynamic_index_in_dim(stack, adapter, 0, keepdims=False)
    qa, ob, fa, db = pick(qkv_a), pick(out_b), pick(ffn_a), pick(down_b)
    small = jnp.concatenate(
        [
            pick(qkv_b),
            pick(out_a),
            pick(ffn_b).reshape(-1, local),
            pick(down_a).reshape(-1, local),
        ],
        axis=0,
    )
    small = gather_small(small, shards, place)
    cuts = np.cumsum([3 * rank, rank, 2 * rank * (units // local)])
    rejoin = lambda piece: piece.transpose(1, 0, 2).reshape(piece.shape[1], -1)
    qb = rejoin(small[:, : cuts[0]])
    oa = rejoin(small[:, cuts[0] : cuts[1]])
    fb = small[:, cuts[1] : cuts[2]].reshape(shards, 2 * rank, units)
    da = small[:, cuts[2] :].reshape(shards, rank, units)

    labels = segments[0]
    long = labels[: length - half + 1] == labels[half - 1 :]
    start = jnp.sum(jnp.where(long, jnp.arange(length - half + 1, dtype=jnp.int32), 0))
    group_start = start + group * half
    own_start = start + place * count
    x_group = roll_rows(layer_input, group_start, half, BF16)
    x_own_b = window(x_group, member * count, count)
    x_own = x_own_b.astype(F32)
    cotangent = roll_rows(output_grad, own_start, count, F32)
    labels_twice = jnp.concatenate([labels, labels[:half]])
    labels_group = window(labels_twice, group_start, half)
    labels_own = window(labels_group, member * count, count)
    cosine, sine = rope_tables(length, half)
    tables = (window(cosine, group_start, half), window(sine, group_start, half))
    tables_own = tuple(window(table, member * count, count) for table in tables)

    latent_qkv = nt(x_group, qa).astype(BF16)
    latent_own = window(latent_qkv, member * count, count)
    query, keys, values = project_qkv(
        x_group, x_own_b, qkv_all, latent_qkv, latent_own, qb, tables, tables_own
    )
    mixed, logs = attend(query, keys, values, labels_own, labels_group)
    latent_out = nt(mixed, oa).astype(BF16)
    branch = nn(mixed, out_all) + nn(latent_out, ob)
    hidden, normed_one, inverse_one = norm_forward(x_own + branch, ln_gain[0], ln_bias[0])
    hidden_b = hidden.astype(BF16)

    latent_ffn = nt(hidden_b, fa).astype(BF16)
    gates, ups, actives = [], [], []
    ffn_out = None
    latent_down = None
    for k in range(shards):
        gate = nn(hidden_b, up_all[k, 0]) + nn(latent_ffn[:, :rank], fb[k, :rank])
        up = nn(hidden_b, up_all[k, 1]) + nn(latent_ffn[:, rank:], fb[k, rank:])
        active = (gate * jax.nn.sigmoid(gate) * up).astype(BF16)
        term = nn(active, down_all[k])
        lat = nt(active, da[k])
        ffn_out = term if ffn_out is None else ffn_out + term
        latent_down = lat if latent_down is None else latent_down + lat
        gates.append(gate)
        ups.append(up)
        actives.append(active)
    latent_down = latent_down.astype(BF16)
    ffn_out = ffn_out + nn(latent_down, db)
    result, normed_two, inverse_two = norm_forward(hidden + ffn_out, ln_gain[1], ln_bias[1])
    rolled = lax.all_gather(result.astype(BF16), "tensor", axis=0, tiled=True)
    output = roll_rows(rolled, -start, length, BF16)

    grad_mid = norm_backward(cotangent, normed_two, inverse_two, ln_gain[1])
    grad_ffn = grad_mid.astype(BF16)
    down_b_part = tn(latent_down, grad_ffn)
    latent_down_grad = nt(grad_ffn, db).astype(BF16)
    grad_hidden = grad_mid
    gate_grads, up_grads, down_a_parts = [], [], []
    latent_gate_grad = None
    latent_up_grad = None
    for k in range(shards):
        grad_active = nt(grad_ffn, down_all[k]) + nn(latent_down_grad, da[k])
        sigma = jax.nn.sigmoid(gates[k])
        grad_gate = (grad_active * ups[k] * sigma * (1.0 + gates[k] * (1.0 - sigma))).astype(BF16)
        grad_up = (grad_active * (gates[k] * sigma)).astype(BF16)
        down_a_parts.append(tn(latent_down_grad, actives[k]))
        gate_grads.append(tn(latent_ffn[:, :rank], grad_gate))
        up_grads.append(tn(latent_ffn[:, rank:], grad_up))
        grad_hidden = grad_hidden + nt(grad_gate, up_all[k, 0]) + nt(grad_up, up_all[k, 1])
        one = nt(grad_gate, fb[k, :rank])
        two = nt(grad_up, fb[k, rank:])
        latent_gate_grad = one if latent_gate_grad is None else latent_gate_grad + one
        latent_up_grad = two if latent_up_grad is None else latent_up_grad + two
    latent_ffn_grad = jnp.concatenate([latent_gate_grad, latent_up_grad], axis=1).astype(BF16)
    grad_hidden = grad_hidden + nn(latent_ffn_grad, fa)
    down_a_part = jnp.concatenate(down_a_parts, axis=1)
    ffn_b_part = jnp.concatenate(
        [jnp.concatenate(gate_grads, axis=1), jnp.concatenate(up_grads, axis=1)], axis=0
    )
    ffn_a_part = tn(latent_ffn_grad, hidden_b)
    grad_first = norm_backward(grad_hidden, normed_one, inverse_one, ln_gain[0])
    grad_branch = grad_first.astype(BF16)
    out_b_part = tn(latent_out, grad_branch)
    latent_out_grad = nt(grad_branch, ob).astype(BF16)
    out_a_part = tn(latent_out_grad, mixed)
    grad_mixed = (nt(grad_branch, out_all) + nn(latent_out_grad, oa)).astype(BF16)

    hot = (adapter == jnp.arange(qkv_a.shape[0], dtype=jnp.int32)).astype(F32)
    out_b_grad, ffn_a_grad, down_b_grad, out_a_grad, ffn_b_grad, down_a_grad = reduce_grads(
        [out_b_part, ffn_a_part, down_b_part], [out_a_part, ffn_b_part, down_a_part], hot, local
    )

    dq, dk, dv = attend_back(
        query, keys, values, mixed, grad_mixed, logs, labels_own, labels_group, tables, tables_own
    )
    qb_q, qb_k, qb_v = qb[:rank], qb[rank : 2 * rank], qb[2 * rank :]
    lat_q = nt(dq, qb_q).astype(BF16)
    lat_k = nt(dk, qb_k).astype(BF16)
    lat_v = nt(dv, qb_v).astype(BF16)
    back = nn(lat_k, qa[rank : 2 * rank]) + nn(lat_v, qa[2 * rank :])
    back_own = nn(lat_q, qa[:rank])
    for k in range(shards):
        cols = slice(k * local, (k + 1) * local)
        back = back + nt(dk[:, cols], qkv_all[k, 1]) + nt(dv[:, cols], qkv_all[k, 2])
        back_own = back_own + nt(dq[:, cols], qkv_all[k, 0])
    qkv_b_part = jnp.concatenate(
        [
            tn(latent_own[:, :rank], dq),
            tn(latent_qkv[:, rank : 2 * rank], dk),
            tn(latent_qkv[:, 2 * rank :], dv),
        ],
        axis=0,
    )
    qkv_a_part = jnp.concatenate([tn(lat_q, x_own_b), tn(lat_k, x_group), tn(lat_v, x_group)], axis=0)
    back_b = back.astype(BF16)
    grad_input = grad_first + back_own + window(back, member * count, count)
    for d in range(1, members):
        target = lax.rem(member + d, members)
        sent = window(back_b, target * count, count)
        links = [
            (g * members + i, g * members + (i + d) % members)
            for g in range(2)
            for i in range(members)
        ]
        grad_input = grad_input + lax.ppermute(sent, "tensor", links).astype(F32)
    grad_rolled = lax.all_gather(grad_input.astype(BF16), "tensor", axis=0, tiled=True)
    grad_whole = roll_rows(grad_rolled, -start, length, F32)
    qkv_a_grad, qkv_b_grad = reduce_grads([qkv_a_part], [qkv_b_part], hot, local)
    return (
        output,
        grad_whole,
        qkv_a_grad,
        qkv_b_grad,
        out_a_grad,
        out_b_grad,
        ffn_a_grad,
        ffn_b_grad,
        down_a_grad,
        down_b_grad,
    )


def solution(mesh):
    devices = mesh.devices
    mesh = Mesh(
        devices.reshape(devices.shape[0] // 2, 2, devices.shape[1]), ("yx", "core", "tensor")
    )
    in_specs = (
        P(DP, None),
        P(DP, None),
        P(DP, None),
        P(DP, None),
        P(),
        P(),
        P(None, None, "tensor"),
        P("tensor", None),
        P(None, None, "tensor"),
        P("tensor", None),
        P(),
        P(None, None, "tensor"),
        P(None, None, "tensor"),
        P(),
        P(),
        P(None, None, "tensor"),
        P(None, None, "tensor"),
        P(),
    )
    out_specs = (
        P(DP, None),
        P(DP, None),
        P(),
        P(None, None, "tensor"),
        P(None, None, "tensor"),
        P(),
        P(),
        P(None, None, "tensor"),
        P(None, None, "tensor"),
        P(),
    )
    return jax.shard_map(body, mesh=mesh, in_specs=in_specs, out_specs=out_specs, check_vma=False)
```

time: 1750 us -> 750 us (0.43)
  waiting for transfers between devices: 1090 us -> 326 us
  matrix products: 499 us -> 166 us
  Pallas kernels: 0 us -> 98.7 us
  other arithmetic: 61.2 us -> 8.85 us
  blocking collectives: 29.5 us -> 60.5 us
  local copies, waits for them, and re-layouts: 36.3 us -> 59.5 us
    reduce_scatter x8 -> x2, waiting for transfers between devices: 538 us -> 0.01 us  [reduce_grads(): part = lax.psum_scatter(packed, 'tensor', scatter_dimension=0, tiled=False)]
    dot_general x71 -> x101, matrix products: 499 us -> 166 us  [the longest x45 82.2 us: nt(): lax.dot_general(left, right, (((1,), (1,)), ((), ())), preferred_element_...]
    psum x2 -> x0, waiting for transfers between devices: 200 us -> none  [the longest x1 140 us: body(): lax.psum((qkv_a_part, out_b_part, ffn_a_part, down_b_part), ('dp', 'tenso...]
    pallas_call x0 -> x7, Pallas kernels: none -> 98.7 us  [the longest x4 40.6 us: roll_rows(): pl.pallas_call(kernel, grid_spec=pltpu.PrefetchScalarGridSpec(num_scalar_...]
    all_gather x5 -> x8, waiting for transfers between devices: 354 us -> 270 us  [the longest x4 198 us: gather_weight(): return lax.all_gather(piece, ALL, axis=0, tiled=True)]
    ppermute x0 -> x1, waiting for transfers between devices: none -> 55.8 us  [body(): grad_input = grad_input + lax.ppermute(sent, 'tensor', links).astype(F32)]
    all_gather x2 -> x3, blocking collectives: 29.5 us -> 60.5 us  [the longest x1 29.7 us: reduce_grads(): lax.all_gather(placed[:, :cut].astype(BF16), 'tensor', axis=2, tiled=True)]
    convert_element_type x17 -> x2, other arithmetic: 24.2 us -> 2.21 us  [the longest x1 1.81 us: body(): grad_ffn = grad_mid.astype(BF16)]
  transfers between devices with their start and end apart: 15 -> 11, of which waited for: 14 -> 7; matrix products, arithmetic and copies ran while one was open for 5% -> 19% of each run, Pallas kernels for 0% -> 11%
where the time goes in v1:
time: 750 us; the launch traced here: 741 us
  waiting for transfers between devices  326 us (43%)
  matrix products  166 us (22%)
  Pallas kernels  98.7 us (13%)
  blocking collectives  60.5 us (8%)
  local copies, waits for them, and re-layouts  59.5 us (8%)
  between operations  18.7 us (2%)
  other arithmetic  8.85 us (1%)
    all_gather x4, waiting for transfers between devices, gather_weight(): return lax.all_gather(piece, ALL, axis=0, tiled=True)  198 us
    dot_general x45, matrix products, nt(): lax.dot_general(left, right, (((1,), (1,)), ((), ())), preferred_element_...  82.2 us
    dot_general x32, matrix products, nn(): return jnp.dot(left, right, preferred_element_type=F32)  66.9 us
    ppermute x1, waiting for transfers between devices, body(): grad_input = grad_input + lax.ppermute(sent, 'tensor', links).astype(F32)  55.8 us
    all_gather x1, waiting for transfers between devices, body(): lax.all_gather(grad_input.astype(BF16), 'tensor', axis=0, tiled=True)  55.5 us
    pallas_call x4, Pallas kernels, roll_rows(): pl.pallas_call(kernel, grid_spec=pltpu.PrefetchScalarGridSpec(num_scalar_...  40.6 us
    all_gather x1, blocking collectives, reduce_grads(): lax.all_gather(placed[:, :cut].astype(BF16), 'tensor', axis=2, tiled=True)  29.7 us
    pallas_call x1, Pallas kernels, attend_back(): pl.pallas_call(kernel, grid=(pairs,), in_specs=[pair(count), pair(total),...  28.1 us
  transfers between devices with their start and end apart: 11, of which 7 were waited for; matrix products, arithmetic and copies ran while one was open for 19% of the time, Pallas kernels for 11%

profile of v1, /device:TPU:0, one launch (start us, length us, event | category | flops | bytes accessed | tf_op | source)
XLA Modules:
  0.0 741.1 jit_solution(12038327637001139814)
XLA Ops:
  7.3 1.8 constant_dynamic-slice_fusion.10
  10.6 1.9 constant_dynamic-slice_fusion.1
  19.5 21.1 %all-gather = bf16[1024,256]{1,0:T(8,128)(2,1)S(1)} all-gather(bf16[256,256]{1,0:T(8,128)(2,1)S(1)} %pad_maximum_fusion.1), channel_id=2, replica_groups=mesh['yx'=4,'core'=2,'tensor'=4] {'tensor'}, dimensions={0}, use_global_device_ids=true | all-gather | bytes 655360 | tf_op jit(solution)/shard_map/all_gather | solution.py:315
  46.4 4.9 roll_rows.6
  51.9 7.7 %roll_rows.4.x_ref = bf16[1024,1024]{1,0:T(8,128)(2,1)} custom-call(s32[2]{0:T(128)} %pad_add_fusion.1.scalar_ref, bf16[2048,1024]{1,0:T(8,128)(2,1)} %high_ref.2, bf16[2048,1024]{1,0:T(8,128)(2,1)} %high_ref.2), custom_call_target="tpu_custom_call" | custom-call | flops 536870912 | bytes 8388608 | tf_op jit(solution)/shard_map/roll_rows/pallas_call | solution.py:46
  60.9 2.6 convolution_convert_fusion.l_ref
  69.2 15.8 %all-gather.10.cloned.1.call-done = bf16[12288,256]{1,0:T(8,128)(2,1)} async-done(((bf16[384,256]{1,0:T(8,128)(2,1)}), bf16[12288,256]{1,0:T(8,128)(2,1)}) %all-gather.10.cloned.1.call-update) | async-done | bytes 6291472 | tf_op jit(solution)/shard_map/all_gather | solution.py:311
  85.1 11.9 %project_qkv.1 = (bf16[512,1024]{1,0:T(8,128)(2,1)}, bf16[1024,1024]{1,0:T(8,128)(2,1)}, bf16[1024,1024]{1,0:T(8,128)(2,1)}) custom-call(bf16[1024,1024]{1,0:T(8,128)(2,1)} %roll_rows.4.x_ref, bf16[512,1024]{1,0:T(8,128)(2,1)} %constant_dynamic-slice_fusion.11.o_ref, bf16[4,3,1024,256]{3,2,1,0:T(8,128)(2,1)} %bitcast.352, bf16[1024,48]{1,0:T(8,128)(2,1)} %copy-done.27, ...), custom_call_target="tpu_custom_call" | custom-call | flops 5368709120 | bytes 20971520 | tf_op jit(solution)/shard_map/project_qkv/pallas_call | solution.py:102
  97.0 18.1 %attend.1 = (bf16[512,1024]{1,0:T(8,128)(2,1)}, f32[8,8,512]{2,1,0:T(8,128)}) custom-call(bf16[512,1024]{1,0:T(8,128)(2,1)} %get-tuple-element.38.q_ref, bf16[1024,1024]{1,0:T(8,128)(2,1)} %get-tuple-element.39.k_ref, bf16[1024,1024]{1,0:T(8,128)(2,1)} %get-tuple-element.40.v_ref, s32[1,512]{1,0:T(1,128)} %bitcast.402, s32[1024,1]{1,0:T(8,128)} %copy.76.all_ref), custom_call_target="tpu_custom_call" | custom-call | flops 8589934592 | bytes 6291456 | tf_op jit(solution)/shard_map/attend/pallas_call | solution.py:166
  115.1 1.6 convolution_convert_fusion.29
  116.7 26.0 %all-gather.12.cloned.1.call-done = bf16[1024,1024]{1,0:T(8,128)(2,1)} async-done(((bf16[32,1024]{1,0:T(8,128)(2,1)}), bf16[1024,1024]{1,0:T(8,128)(2,1)}) %all-gather.12.cloned.1.call-update) | async-done | bytes 2097168 | tf_op jit(solution)/shard_map/all_gather | solution.py:311
  142.7 3.2 fusion.135
  150.2 108.6 %all-gather.14.cloned.1.call-done = bf16[8192,1024]{1,0:T(8,128)(2,1)} async-done(((bf16[256,1024]{1,0:T(8,128)(2,1)}), bf16[8192,1024]{1,0:T(8,128)(2,1)}) %all-gather.14.cloned.1.call-update) | async-done | bytes 16777232 | tf_op jit(solution)/shard_map/all_gather | solution.py:311
  258.8 3.2 fusion.6
  263.2 3.7 fusion.8
  266.9 2.0 multiply_convert_fusion.11
  269.3 2.4 copy-done.67
  274.8 2.0 multiply_convert_fusion.10
  280.3 2.0 multiply_convert_fusion.9
  285.9 2.0 multiply_convert_fusion.8
  289.3 47.5 %all-gather.16.cloned.1.call-done = bf16[4096,1024]{1,0:T(8,128)(2,1)} async-done(((bf16[128,1024]{1,0:T(8,128)(2,1)}), bf16[4096,1024]{1,0:T(8,128)(2,1)}) %all-gather.16.cloned.1.call-update) | async-done | bytes 8388624 | tf_op jit(solution)/shard_map/all_gather | solution.py:311
  336.8 3.3 fusion.23
  340.1 3.2 fusion.27
  345.9 1.9 fusion.134
  350.1 1.8 fusion.128
  356.3 1.6 multiply_convert_fusion.7
  364.8 2.9 fusion.17
  368.5 2.9 fusion.19
  375.7 2.9 fusion.13
  379.5 2.9 fusion.15
  386.8 2.9 fusion.11
  390.6 2.9 fusion.9
  393.5 2.9 fusion.5
  396.4 2.9 fusion.7
  403.4 2.6 fusion.127
  410.1 1.7 copy.91
  421.7 2.9 fusion.125
  426.0 28.1 %attend_back.1 = (bf16[512,1024]{1,0:T(8,128)(2,1)}, bf16[1024,1024]{1,0:T(8,128)(2,1)}, bf16[1024,1024]{1,0:T(8,128)(2,1)}) custom-call(bf16[512,1024]{1,0:T(8,128)(2,1)} %get-tuple-element.38.q_ref, bf16[1024,1024]{1,0:T(8,128)(2,1)} %get-tuple-element.39.k_ref, bf16[1024,1024]{1,0:T(8,128)(2,1)} %get-tuple-element.40.v_ref, ...), custom_call_target="tpu_custom_call" | custom-call | flops 21474836480 | bytes 13631488 | tf_op jit(solution)/shard_map/attend_back/pallas_call | solution.py:240
  454.1 1.6 convolution_convert_fusion.26
  455.7 2.3 convolution_convert_fusion.21
  458.3 2.1 convolution_convert_fusion.18
  464.8 16.0 %all-gather.22.cloned.1.call-done = bf16[8,288,256]{2,1,0:T(8,128)(2,1)} async-done(((bf16[1,288,256]{2,1,0:T(8,128)(2,1)}), bf16[8,288,256]{2,1,0:T(8,128)(2,1)}) %all-gather.22.cloned.1.call-update) | async-done | bytes 1179664 | tf_op jit(solution)/shard_map/all_gather | solution.py:330
  486.5 1.9 fusion.43
  488.5 3.7 fusion.80
  492.2 1.9 fusion.44
  494.1 3.8 fusion.45
  497.9 3.9 fusion.46
  501.8 3.8 fusion.47
  505.6 3.8 fusion.48
  509.4 3.8 fusion.49
  513.2 3.8 fusion.42
  517.0 12.7 %add_add_fusion = f32[1024,1024]{1,0:T(8,128)} fusion(f32[1024,1024]{1,0:T(8,128)} %fusion.42, f32[1024,1024]{1,0:T(8,128)S(1)} %fusion.43, f32[1024,1024]{1,0:T(8,128)S(1)} %fusion.44, f32[1024,1024]{1,0:T(8,128)} %fusion.45, f32[1024,1024]{1,0:T(8,128)} %fusion.46, f32[1024,1024]{1,0:T(8,128)} %fusion.47, f32[1024,1024]{1,0:T(8,128)} %fusion.48, ...), kind=kOutput, calls=%fused_computation | convolution fusion | flops 42991616 | bytes 42008584 | tf_op jit(solution)/shard_map/dot_general | solution.py:27
  529.7 1.7 dynamic-slice_convert_fusion
  531.4 1.5 collective-permute-start
  535.7 1.7 fusion.51
  538.9 55.8 %collective-permute-done = bf16[512,1024]{1,0:T(8,128)(2,1)S(1)} collective-permute-done((bf16[512,1024]{1,0:T(8,128)(2,1)S(1)}, bf16[512,1024]{1,0:T(8,128)(2,1)S(1)}, u32[]{:S(2)}, u32[]{:S(2)}) %collective-permute-start) | collective-permute-done | bytes 1048608 | tf_op jit(solution)/shard_map/ppermute | solution.py:532
  594.6 2.8 add_convert_fusion
  598.8 9.6 %all_gather.44 = bf16[8,112,256]{2,1,0:T(8,128)(2,1)S(1)} all-gather(bf16[1,112,256]{2,1,0:T(8,128)(2,1)} %reduce-scatter.3.cloned.1.call-done), channel_id=1, replica_groups=mesh['yx'=4,'core'=2,'tensor'=4] {'yx','core'}, dimensions={0}, use_global_device_ids=true | all-gather | bytes 516096 | tf_op jit(solution)/shard_map/all_gather | solution.py:330
  608.9 29.7 %all_gather.45 = bf16[8,48,1024]{2,0,1:T(8,128)(2,1)S(1)} all-gather(bf16[8,48,256]{2,0,1:T(8,128)(2,1)S(1)} %slice.667), channel_id=1, replica_groups=mesh['yx'=4,'core'=2,'tensor'=4] {'tensor'}, dimensions={2}, use_global_device_ids=true | all-gather | bytes 983040 | tf_op jit(solution)/shard_map/all_gather | solution.py:338
  638.6 1.6 copy.98
  646.3 1.6 copy.102
  650.2 13.6 %roll_rows.5 = bf16[2048,1024]{1,0:T(8,128)(2,1)} custom-call(s32[2]{0:T(128)} %pad_add_fusion.scalar_ref, bf16[2048,1024]{1,0:T(8,128)(2,1)} %all-gather.18.cloned.1.call-done.low_ref.high_ref, bf16[2048,1024]{1,0:T(8,128)(2,1)} %all-gather.18.cloned.1.call-done.low_ref.high_ref), custom_call_target="tpu_custom_call" | custom-call | flops 1073741824 | bytes 16777216 | tf_op jit(solution)/shard_map/roll_rows/pallas_call | solution.py:46
  663.8 55.5 %all-gather.20.cloned.1.call-done.low_ref.high_ref = bf16[2048,1024]{1,0:T(8,128)(2,1)} async-done(((bf16[512,1024]{1,0:T(8,128)(2,1)}), bf16[2048,1024]{1,0:T(8,128)(2,1)}) %all-gather.20.cloned.1.call-update) | async-done | bytes 4194320 | tf_op jit(solution)/shard_map/all_gather | solution.py:533
  719.3 14.4 %roll_rows.7 = f32[2048,1024]{1,0:T(8,128)} custom-call(s32[2]{0:T(128)} %pad_add_fusion.scalar_ref, bf16[2048,1024]{1,0:T(8,128)(2,1)} %all-gather.20.cloned.1.call-done.low_ref.high_ref, bf16[2048,1024]{1,0:T(8,128)(2,1)} %all-gather.20.cloned.1.call-done.low_ref.high_ref), custom_call_target="tpu_custom_call" | custom-call | flops 1073741824 | bytes 16777216 | tf_op jit(solution)/shard_map/roll_rows/pallas_call | solution.py:46
  (331 shorter events, 107.6 us)
Async XLA Ops:
  7.2 5.4 copy-start
  7.2 6.2 copy-start.54
  7.2 77.9 %all-gather.10.cloned.1.call-start = ((), (), s32[]{:S(2)}) async-start(), calls=%async_computation.2 | async-start | bytes 6488064 | tf_op jit(solution)/shard_map/all_gather | solution.py:311
  9.0 133.7 %all-gather.12.cloned.1.call-start = ((), (), s32[]{:S(2)}) async-start(), calls=%async_computation.3 | async-start | bytes 2162688 | tf_op jit(solution)/shard_map/all_gather | solution.py:311
  10.6 248.2 %all-gather.14.cloned.1.call-start = ((), (), s32[]{:S(2)}) async-start(), calls=%async_computation.4 | async-start | bytes 17301504 | tf_op jit(solution)/shard_map/all_gather | solution.py:311
  12.5 324.3 %all-gather.16.cloned.1.call-start = ((), (), s32[]{:S(2)}) async-start(), calls=%async_computation.5 | async-start | bytes 8650752 | tf_op jit(solution)/shard_map/all_gather | solution.py:311
  13.3 444.6 %reduce-scatter.5.cloned.1.call-start = ((), (), s32[]{:S(2)}) async-start(), calls=%async_computation.9 | async-start | bytes 737280 | tf_op jit(solution)/shard_map/reduce_scatter | solution.py:329
  42.5 72.6 %copy-start.37 = (bf16[4,2,8,256]{3,2,0,1:T(8,128)(2,1)}, bf16[4,2,8,256]{3,2,0,1:T(8,128)(2,1)S(1)}, u32[]{:S(2)}) copy-start(bf16[4,2,8,256]{3,2,0,1:T(8,128)(2,1)S(1)} %copy.120) | copy-start | bytes 98308
  59.6 4.6 copy-start.59
  59.6 4.6 copy-start.60
  59.6 4.6 copy-start.61
  59.6 4.6 copy-start.62
  64.7 1.8 copy-start.4
  66.5 2.1 copy-start.64
  66.5 2.1 copy-start.65
  69.2 78.4 %copy-start.57 = (f32[1,1024]{1,0:T(1,128)}, f32[1,1024]{1,0:T(1,128)S(1)}, u32[]{:S(2)}) copy-start(f32[1,1024]{1,0:T(1,128)S(1)} %get-tuple-element.117) | copy-start | bytes 12292
  116.7 29.2 %copy-start.13 = (bf16[512,1024]{1,0:T(8,128)(2,1)S(1)}, bf16[512,1024]{1,0:T(8,128)(2,1)}, u32[]{:S(2)}) copy-start(bf16[512,1024]{1,0:T(8,128)(2,1)} %constant_dynamic-slice_fusion.11.o_ref) | copy-start | bytes 3145732
  263.2 3.7 copy-start.33
  263.2 8.5 %copy-start.67 = (bf16[8192,1024]{1,0:T(8,128)(2,1)S(1)}, bf16[8192,1024]{1,0:T(8,128)(2,1)}, u32[]{:S(2)}) copy-start(bf16[8192,1024]{1,0:T(8,128)(2,1)} %all-gather.14.cloned.1.call-done) | copy-start | bytes 50331652
  266.9 2.0 copy-start.52
  268.9 4.1 copy-start.19
  276.8 1.7 copy-start.21
  282.2 1.9 copy-start.23
  285.9 3.0 copy-start.50
  336.8 3.3 copy-start.24
  336.8 6.5 copy-start.68
  340.1 3.2 copy-start.22
  347.8 1.6 copy-start.10
  350.1 2.9 copy-start.26
  354.1 1.6 copy-start.34
  354.1 1.6 copy-start.53
  354.1 2.2 copy-start.71
  360.5 1.6 copy-start.36
  360.5 1.6 copy-start.51
  360.5 2.3 copy-start.72
  371.4 1.6 copy-start.32
  371.4 2.2 copy-start.70
  382.4 1.6 copy-start.30
  382.4 2.2 copy-start.69
  400.9 1.6 copy-start.16
  406.5 2.4 copy-start.2
  407.6 1.5 copy-start.45
  409.3 12.4 %copy-start.3 = (f32[512,1024]{1,0:T(8,128)S(1)}, f32[512,1024]{1,0:T(8,128)}, u32[]{:S(2)}) copy-start(f32[512,1024]{1,0:T(8,128)} %copy-done.2) | copy-start | bytes 6291460
  413.0 7.7 %copy-start.55 = (bf16[16,256]{1,0:T(8,128)(2,1)S(1)}, bf16[16,256]{1,0:T(8,128)(2,1)}, u32[]{:S(2)}) copy-start(bf16[16,256]{1,0:T(8,128)(2,1)} %pad_convert_fusion) | copy-start | bytes 24580
  421.4 3.2 copy-start.38
  421.4 59.4 %all-gather.22.cloned.1.call-start = ((), (), s32[]{:S(2)}) async-start(), calls=%async_computation.10 | async-start | bytes 1327104 | tf_op jit(solution)/shard_map/all_gather | solution.py:330
  426.0 28.1 %copy-start.49 = (bf16[4,2,8,256]{3,2,0,1:T(8,128)(2,1)S(1)}, bf16[4,2,8,256]{3,2,0,1:T(8,128)(2,1)}, u32[]{:S(2)}) copy-start(bf16[4,2,8,256]{3,2,0,1:T(8,128)(2,1)} %copy.121) | copy-start | bytes 98308
  426.0 29.7 %copy-start.40 = (bf16[4,2,8,256]{3,2,0,1:T(8,128)(2,1)S(1)}, bf16[4,2,8,256]{3,2,0,1:T(8,128)(2,1)}, u32[]{:S(2)}) copy-start(bf16[4,2,8,256]{3,2,0,1:T(8,128)(2,1)} %copy.123) | copy-start | bytes 98308
  458.0 2.5 copy-start.39
  458.0 140.8 %reduce-scatter.3.cloned.1.call-start = ((), (), s32[]{:S(2)}) async-start(), calls=%async_computation.8 | async-start | bytes 286720 | tf_op jit(solution)/shard_map/reduce_scatter | solution.py:329
  458.1 2.4 copy-start.8
  458.3 2.8 copy-start.5
  461.2 1.7 copy-start.6
  464.7 180.3 %all-gather.24.cloned.1.call-start = ((), (), s32[]{:S(2)}) async-start(), calls=%async_computation.11 | async-start | bytes 1310720 | tf_op jit(solution)/shard_map/all_gather | solution.py:338
  485.5 164.8 %all-gather.18.cloned.1.call-start = ((), (), s32[]{:S(2)}) async-start(), calls=%async_computation.6 | async-start | bytes 5242880 | tf_op jit(solution)/shard_map/all_gather | solution.py:457
  486.2 233.1 %all-gather.20.cloned.1.call-start = ((), (), s32[]{:S(2)}) async-start(), calls=%async_computation.7 | async-start | bytes 5242880 | tf_op jit(solution)/shard_map/all_gather | solution.py:533
  488.5 3.7 copy-start.7
  492.2 1.9 copy-start.9
  531.4 63.2 %collective-permute-start = (bf16[512,1024]{1,0:T(8,128)(2,1)S(1)}, bf16[512,1024]{1,0:T(8,128)(2,1)S(1)}, u32[]{:S(2)}, u32[]{:S(2)}) collective-permute-start(bf16[512,1024]{1,0:T(8,128)(2,1)S(1)} %dynamic-slice_convert_fusion), channel_id=1, source_target_pairs={{0,1},{1,0},{2,3},{3,2},{4,5},{5,4},{6,7},{7,6},{8,9},{9,8},{10,11... | collective-permute-start | bytes 3145736 | tf_op jit(solution)/shard_map/ppermute | solution.py:532
  535.7 59.0 %copy-start.11 = (f32[1024,1024]{1,0:T(8,128)S(1)}, f32[1024,1024]{1,0:T(8,128)}, u32[]{:S(2)}) copy-start(f32[1024,1024]{1,0:T(8,128)} %add_add_fusion) | copy-start | bytes 12582916
  641.6 1.6 slice-start.1
  641.9 2.4 slice-start.2
  645.0 2.9 copy-start.18
  719.3 14.4 %copy-start.1 = (bf16[1024,1024]{1,0:T(8,128)(2,1)S(1)}, bf16[1024,1024]{1,0:T(8,128)(2,1)}, u32[]{:S(2)}) copy-start(bf16[1024,1024]{1,0:T(8,128)(2,1)} %param.36) | copy-start | bytes 6291460
  (23 other events, 30.3 us)
Sparse Core Ops, SparseCore 0:
  11.4 73.5 all-gather.9
  87.9 54.7 all-gather.11
  145.6 113.1 all-gather.13
  261.5 75.2 all-gather.15
  421.5 20.7 reduce-scatter.4
  458.1 22.6 all-gather.21
  483.6 19.8 reduce-scatter.2
  505.6 28.3 all-gather.23
  535.6 97.4 all-gather.17
  635.1 84.2 all-gather.19

commit v2 on v1

v2 whole, which is shorter than its diff:
```python
import jax
import jax.numpy as jnp
import numpy as np
from jax import lax
from jax.experimental import pallas as pl
from jax.experimental.pallas import tpu as pltpu
from jax.sharding import Mesh
from jax.sharding import PartitionSpec as P


HEAD_DIM = 64
LANES = 128
DP = ("yx", "core")
ALL = ("tensor", "yx", "core")
F32 = jnp.float32
BF16 = jnp.bfloat16


def nt(left, right):
    return lax.dot_general(left, right, (((1,), (1,)), ((), ())), preferred_element_type=F32)


def tn(left, right):
    return lax.dot_general(left, right, (((0,), (0,)), ((), ())), preferred_element_type=F32)


def nn(left, right):
    return jnp.dot(left, right, preferred_element_type=F32)


def roll_rows(pieces, place, shift, count, dtype):
    number = len(pieces)
    size, width = pieces[0].shape
    length = number * size
    unit = LANES
    units = length // unit
    block = min(512, count)
    shift = lax.rem(shift + length, length)
    first = shift // unit
    scalars = jnp.stack([first, shift - first * unit, place]).astype(jnp.int32)

    def kernel(scalar_ref, *refs):
        out_ref = refs[number]
        step = pl.program_id(0)
        if number > 1:
            rows_ref = refs[number + 1]

            @pl.when(step == 0)
            def _():
                for k in range(number):
                    member = lax.rem(scalar_ref[2] + (number - k), number)
                    rows_ref[pl.ds(pl.multiple_of(member * size, size), size)] = refs[k][...]
        else:
            rows_ref = refs[0]
        offset = scalar_ref[1]
        row = lax.broadcasted_iota(jnp.int32, (unit, 2 * unit), 0)
        column = lax.broadcasted_iota(jnp.int32, (unit, 2 * unit), 1)
        move = jnp.where(column == row + offset, 1.0, 0.0).astype(BF16)
        for s in range(block // unit):
            base = scalar_ref[0] + step * (block // unit) + s
            low = rows_ref[pl.ds(pl.multiple_of(lax.rem(base, units) * unit, unit), unit)]
            high = rows_ref[pl.ds(pl.multiple_of(lax.rem(base + 1, units) * unit, unit), unit)]
            pair = jnp.concatenate([low, high], axis=0)
            out_ref[s * unit : (s + 1) * unit] = nn(move, pair).astype(dtype)

    return pl.pallas_call(
        kernel,
        grid_spec=pltpu.PrefetchScalarGridSpec(
            num_scalar_prefetch=1,
            grid=(count // block,),
            in_specs=[pl.BlockSpec((size, width), lambda i, s: (0, 0))] * number,
            out_specs=pl.BlockSpec((block, width), lambda i, s: (i, 0)),
            scratch_shapes=[pltpu.VMEM((length, width), BF16)] if number > 1 else [],
        ),
        out_shape=jax.ShapeDtypeStruct((count, width), dtype),
        cost_estimate=pl.CostEstimate(
            flops=4 * count * unit * width,
            bytes_accessed=2 * length * width + 4 * count * width,
            transcendentals=0,
        ),
        name="roll_rows",
    )(scalars, *pieces)


def spin(values, cosine, sine):
    lane = lax.broadcasted_iota(jnp.int32, (1, LANES), 1)
    first = lax.rem(lane, HEAD_DIM) < HEAD_DIM // 2
    parts = []
    for start in range(0, values.shape[1], LANES):
        piece = values[:, start : start + LANES]
        ahead = pltpu.roll(piece, LANES - HEAD_DIM // 2, 1)
        behind = pltpu.roll(piece, HEAD_DIM // 2, 1)
        parts.append(piece * cosine + jnp.where(first, ahead, behind) * sine)
    return parts[0] if len(parts) == 1 else jnp.concatenate(parts, axis=1)


def project_qkv(group, own, weights, latent, latent_own, factors, tables, tables_own):
    shards, _, width, local = weights.shape
    count, total = own.shape[0], group.shape[0]
    rank = latent.shape[1] // 3
    scale = HEAD_DIM ** (-0.5)

    def kernel(x_ref, o_ref, w_ref, l_ref, lo_ref, f_ref, c_ref, s_ref, co_ref, so_ref, q_ref, k_ref, v_ref):
        x = x_ref[...]
        lat = l_ref[...]
        factor = f_ref[...]
        query = nn(o_ref[...], w_ref[0, 0]) + nn(lo_ref[...][:, :rank], factor[:rank])
        q_ref[...] = (spin(query, co_ref[...], so_ref[...]).astype(BF16) * scale).astype(BF16)
        key = nn(x, w_ref[0, 1]) + nn(lat[:, rank : 2 * rank], factor[rank : 2 * rank])
        k_ref[...] = spin(key, c_ref[...], s_ref[...]).astype(BF16)
        value = nn(x, w_ref[0, 2]) + nn(lat[:, 2 * rank :], factor[2 * rank :])
        v_ref[...] = value.astype(BF16)

    def whole(array):
        return pl.BlockSpec(array.shape, lambda i: (0,) * array.ndim)

    def columns(rows):
        return pl.BlockSpec((rows, local), lambda i: (0, i))

    cosine, sine = tables
    cosine_own, sine_own = tables_own
    return pl.pallas_call(
        kernel,
        grid=(shards,),
        in_specs=[
            whole(group),
            whole(own),
            pl.BlockSpec((1, 3, width, local), lambda i: (i, 0, 0, 0)),
            whole(latent),
            whole(latent_own),
            columns(factors.shape[0]),
            whole(cosine),
            whole(sine),
            whole(cosine_own),
            whole(sine_own),
        ],
        out_specs=[columns(count), columns(total), columns(total)],
        out_shape=[
            jax.ShapeDtypeStruct((count, width), BF16),
            jax.ShapeDtypeStruct((total, width), BF16),
            jax.ShapeDtypeStruct((total, width), BF16),
        ],
        cost_estimate=pl.CostEstimate(
            flops=2 * width * width * (count + 2 * total),
            bytes_accessed=2 * (4 * width * width + 6 * total * width),
            transcendentals=0,
        ),
        name="project_qkv",
    )(group, own, weights, latent, latent_own, factors, cosine, sine, cosine_own, sine_own)


def head_lanes():
    return lax.broadcasted_iota(jnp.int32, (1, LANES), 1) // HEAD_DIM


def attend(query, keys, values, labels_own, labels):
    count, width = query.shape
    total = keys.shape[0]
    pairs = width // LANES

    def kernel(q_ref, k_ref, v_ref, own_ref, all_ref, out_ref, log_ref):
        q = q_ref[...]
        k = k_ref[...]
        flipped = v_ref[...].astype(F32).T
        same = all_ref[...] == own_ref[...]
        lanes = head_lanes()
        sides = lax.broadcasted_iota(jnp.int32, (LANES, 1), 0) // HEAD_DIM
        outs = []
        logs = []
        for head in range(2):
            masked = jnp.where(lanes == head, q, jnp.zeros_like(q))
            scores = jnp.where(same, nt(k, masked), -1e30)
            top = jnp.max(scores, axis=0, keepdims=True)
            expo = jnp.exp(scores - top).astype(BF16)
            stacked = jnp.where(sides == head, flipped, 1.0).astype(BF16)
            product = nn(stacked, expo)
            other = (1 - head) * HEAD_DIM
            weight_sum = product[other : other + 1]
            outs.append(product[head * HEAD_DIM : (head + 1) * HEAD_DIM] / weight_sum)
            logs.append(top + jnp.log(weight_sum))
        out_ref[...] = jnp.concatenate(outs, axis=0).T.astype(BF16)
        log_ref[0, 0:1] = logs[0]
        log_ref[0, 1:2] = logs[1]

    pair = lambda rows: pl.BlockSpec((rows, LANES), lambda i: (0, i))
    return pl.pallas_call(
        kernel,
        grid=(pairs,),
        in_specs=[
            pair(count),
            pair(total),
            pair(total),
            pl.BlockSpec((1, count), lambda i: (0, 0)),
            pl.BlockSpec((total, 1), lambda i: (0, 0)),
        ],
        out_specs=[pair(count), pl.BlockSpec((1, 8, count), lambda i: (i, 0, 0))],
        out_shape=[
            jax.ShapeDtypeStruct((count, width), BF16),
            jax.ShapeDtypeStruct((pairs, 8, count), F32),
        ],
        cost_estimate=pl.CostEstimate(
            flops=16 * count * total * width,
            bytes_accessed=4 * (count + total) * width,
            transcendentals=2 * pairs * count * total,
        ),
        name="attend",
    )(query, keys, values, labels_own[None, :], labels[:, None])


def attend_back(query, keys, values, mixed, grads, logs, labels_own, labels, tables, tables_own, block, before, last):
    count, width = query.shape
    pairs = width // LANES
    scale = HEAD_DIM ** (-0.5)
    cosine, sine = tables
    cosine_own, sine_own = tables_own
    chained = before is not None

    def kernel(block_ref, q_ref, k_ref, v_ref, m_ref, g_ref, log_ref, own_ref, all_ref, c_ref, s_ref, co_ref, so_ref, *rest):
        before_ref = rest[0] if chained else None
        dq_ref, dk_ref, dv_ref = rest[-3:]
        q = q_ref[...]
        k = k_ref[...]
        v = v_ref[...]
        g = g_ref[...]
        same = all_ref[...] == own_ref[...]
        lanes = head_lanes()
        sides = lax.broadcasted_iota(jnp.int32, (LANES, 1), 0) // HEAD_DIM
        k_flipped = k.astype(F32).T
        product = g.astype(F32) * m_ref[...].astype(F32)
        high = product.astype(BF16)
        low = (product - high.astype(F32)).astype(BF16)
        picks = (
            lax.broadcasted_iota(jnp.int32, (8, LANES), 1) // HEAD_DIM
            == lax.broadcasted_iota(jnp.int32, (8, LANES), 0)
        ).astype(F32).astype(BF16)
        delta = nt(picks, high) + nt(picks, low)
        dq = jnp.zeros((LANES, count), F32)
        dk = jnp.zeros((count, LANES), F32)
        dv = jnp.zeros((count, LANES), F32)
        for head in range(2):
            q_masked = jnp.where(lanes == head, q, jnp.zeros_like(q))
            g_masked = jnp.where(lanes == head, g, jnp.zeros_like(g))
            scores = jnp.where(same, nt(k, q_masked), -1e30)
            prob = jnp.exp(scores - log_ref[0, head : head + 1])
            grad_prob = nt(v, g_masked)
            grad_score = (prob * (grad_prob - delta[head : head + 1])).astype(BF16)
            dv = dv + nn(prob.astype(BF16), g_masked)
            dk = dk + nn(grad_score, q_masked)
            k_side = jnp.where(sides == head, k_flipped, 0.0).astype(BF16)
            dq = dq + nn(k_side, grad_score)
        dq = dq.T * scale
        if chained:
            dq = dq + before_ref[...]
        dq_ref[...] = spin(dq, co_ref[...], -so_ref[...]).astype(BF16) if last else dq
        dk_ref[...] = spin(dk, c_ref[...], -s_ref[...]).astype(BF16)
        dv_ref[...] = dv.astype(BF16)

    pair = pl.BlockSpec((count, LANES), lambda i, s: (0, i))
    chosen = pl.BlockSpec((count, LANES), lambda i, s: (s[0], i))
    rows = lambda array: pl.BlockSpec((count, array.shape[1]), lambda i, s: (s[0], 0))
    whole = lambda array: pl.BlockSpec(array.shape, lambda i, s: (0,) * array.ndim)
    labels_own = labels_own[None, :]
    labels = labels[:, None]
    operands = [query, keys, values, mixed, grads, logs, labels_own, labels, cosine, sine, cosine_own, sine_own]
    specs = [
        pair,
        chosen,
        chosen,
        pair,
        pair,
        pl.BlockSpec((1, 8, count), lambda i, s: (i, 0, 0)),
        whole(labels_own),
        rows(labels),
        rows(cosine),
        rows(sine),
        whole(cosine_own),
        whole(sine_own),
    ]
    if chained:
        operands.append(before)
        specs.append(pair)
    return pl.pallas_call(
        kernel,
        grid_spec=pltpu.PrefetchScalarGridSpec(
            num_scalar_prefetch=1, grid=(pairs,), in_specs=specs, out_specs=[pair] * 3
        ),
        out_shape=[
            jax.ShapeDtypeStruct((count, width), BF16 if last else F32),
            jax.ShapeDtypeStruct((count, width), BF16),
            jax.ShapeDtypeStruct((count, width), BF16),
        ],
        cost_estimate=pl.CostEstimate(
            flops=40 * count * count * width,
            bytes_accessed=2 * 9 * count * width,
            transcendentals=2 * pairs * count * count,
        ),
        name="attend_back",
    )(jnp.reshape(block, (1,)), *operands)


def project_back(grads, first, weights, factors, outer, latent, rows, block, base, before):
    shards, _, width, local = weights.shape
    count = grads[0].shape[0]
    rank = factors.shape[0] // 3
    number = len(grads)
    based = base is not None
    added = before is not None
    depth = number * rank

    def kernel(block_ref, w_ref, f_ref, a_ref, l_ref, x_ref, *rest):
        g_refs = rest[:number]
        base_ref = rest[number] if based else None
        before_ref = rest[number + based] if added else None
        out_ref, part_ref, acc_ref, lat_ref, b_ref = rest[-5:]
        step = pl.program_id(0)

        @pl.when(step == 0)
        def _():
            acc_ref[...] = base_ref[...] if based else jnp.zeros_like(acc_ref)
            lat_ref[...] = jnp.zeros_like(lat_ref)

        total = acc_ref[...]
        lats = []
        parts = []
        for j in range(number):
            p = first + j
            g = g_refs[j][...]
            total = total + nt(g, w_ref[0, p])
            lats.append(nt(g, f_ref[p * rank : (p + 1) * rank]))
            parts.append(tn(l_ref[:, p * rank : (p + 1) * rank], g))
        acc_ref[...] = total
        lat_ref[...] += jnp.concatenate(lats, axis=1)
        b_ref[step] = jnp.concatenate(parts, axis=0)

        @pl.when(step == shards - 1)
        def _():
            lat = lat_ref[...].astype(BF16)
            final = acc_ref[...] + nn(lat, a_ref[first * rank :])
            out_ref[...] = final.astype(out_ref.dtype)
            part = jnp.concatenate([b_ref[t] for t in range(shards)], axis=1)
            part = jnp.concatenate([part, tn(lat, x_ref[...])], axis=0)
            if added:
                other = before_ref[...]
                none = jnp.zeros((rank, width), F32)
                size = depth - rank
                part = part + jnp.concatenate([none, other[:size], none, other[size:]], axis=0)
            part_ref[...] = part.astype(part_ref.dtype)

    whole = lambda array: pl.BlockSpec(array.shape, lambda i, s: (0,) * array.ndim)
    chosen = lambda array: pl.BlockSpec((count, array.shape[1]), lambda i, s: (s[0], 0))
    columns = lambda size: pl.BlockSpec((size, local), lambda i, s: (0, i))
    fixed = lambda size: pl.BlockSpec((size, width), lambda i, s: (0, 0))
    operands = [weights, factors, outer, latent, rows, *grads]
    specs = [
        pl.BlockSpec((1, 3, width, local), lambda i, s: (i, 0, 0, 0)),
        columns(3 * rank),
        whole(outer),
        chosen(latent),
        chosen(rows),
        *[columns(count) for _ in grads],
    ]
    if based:
        operands.append(base)
        specs.append(fixed(count))
    if added:
        operands.append(before)
        specs.append(whole(before))
    return pl.pallas_call(
        kernel,
        grid_spec=pltpu.PrefetchScalarGridSpec(
            num_scalar_prefetch=1,
            grid=(shards,),
            in_specs=specs,
            out_specs=[fixed(count), fixed(2 * depth)],
            scratch_shapes=[
                pltpu.VMEM((count, width), F32),
                pltpu.VMEM((count, depth), F32),
                pltpu.VMEM((shards, depth, local), F32),
            ],
        ),
        out_shape=[
            jax.ShapeDtypeStruct((count, width), F32 if based else BF16),
            jax.ShapeDtypeStruct((2 * depth, width), BF16 if based else F32),
        ],
        cost_estimate=pl.CostEstimate(
            flops=2 * number * count * width * width,
            bytes_accessed=6 * width * width + 2 * (number + 4) * count * width,
            transcendentals=0,
        ),
        name="project_back",
    )(jnp.reshape(block, (1,)), *operands)


def out_forward(mixed, weights, outer, factors, rows, gain, shift, next_factors):
    count, width = mixed.shape
    rank = factors.shape[0]

    def kernel(m_ref, w_ref, a_ref, b_ref, x_ref, g_ref, s_ref, f_ref, hid_ref, hidb_ref, n_ref, i_ref, lo_ref, lf_ref):
        m = m_ref[...]
        latent = nt(m, a_ref[...]).astype(BF16)
        total = x_ref[...].astype(F32) + nn(m, w_ref[...]) + nn(latent, b_ref[...])
        hidden, normed, inverse = norm_forward(total, g_ref[...], s_ref[...])
        hid_ref[...] = hidden
        hidden_b = hidden.astype(BF16)
        hidb_ref[...] = hidden_b
        n_ref[...] = normed
        i_ref[...] = inverse
        lo_ref[...] = latent
        lf_ref[...] = nt(hidden_b, f_ref[...]).astype(BF16)

    full = lambda array: pl.BlockSpec(array.shape, lambda i: (0,) * array.ndim)
    block = min(256, count)
    part = lambda size: pl.BlockSpec((block, size), lambda i: (i, 0))
    operands = [mixed, weights, outer, factors, rows, gain, shift, next_factors]
    return pl.pallas_call(
        kernel,
        grid=(count // block,),
        in_specs=[
            part(width),
            full(weights),
            full(outer),
            full(factors),
            part(width),
            full(gain),
            full(shift),
            full(next_factors),
        ],
        out_specs=[part(width), part(width), part(width), part(1), part(rank), part(2 * rank)],
        out_shape=[
            jax.ShapeDtypeStruct((count, width), F32),
            jax.ShapeDtypeStruct((count, width), BF16),
            jax.ShapeDtypeStruct((count, width), F32),
            jax.ShapeDtypeStruct((count, 1), F32),
            jax.ShapeDtypeStruct((count, rank), BF16),
            jax.ShapeDtypeStruct((count, 2 * rank), BF16),
        ],
        cost_estimate=pl.CostEstimate(
            flops=2 * count * width * width,
            bytes_accessed=2 * width * width + 14 * count * width,
            transcendentals=count,
        ),
        name="out_forward",
    )(*operands)


def ffn_views(weights, width, sub):
    if len(weights) == 1:
        (packed,) = weights
        _, parts, rows, units = packed.shape
        low = units // parts
        high = rows - low
        specs = [
            pl.BlockSpec((1, parts, high, sub), lambda t, b: (t, 0, 0, b)),
            pl.BlockSpec((1, sub // low, low, width), lambda t, b: (t, b, high // low, 0)),
        ]
        upper = lambda ref, i: ref[0, i * parts // 2 : (i + 1) * parts // 2].reshape(width, sub)
        lower = lambda ref: ref[0].reshape(sub, width)
        return [packed, packed], specs, upper, lower
    specs = [
        pl.BlockSpec((1, 2, width, sub), lambda t, b: (t, 0, 0, b)),
        pl.BlockSpec((1, sub, width), lambda t, b: (t, b, 0)),
    ]
    return list(weights), specs, lambda ref, i: ref[0, i], lambda ref: ref[0]


def ffn_forward(hidden, hidden_b, latent, weights, fb, da, db, gain, shift, cotangent):
    count, width = hidden.shape
    shards, _, units = fb.shape
    rank = db.shape[0]
    sub = min(512, units)
    arrays, views, upper, lower = ffn_views(weights, width, sub)
    inner = units // sub
    steps = shards * inner

    def kernel(h_ref, hb_ref, l_ref, w_ref, wd_ref, fb_ref, da_ref, db_ref, g_ref, s_ref, c_ref,
               pre_ref, res_ref, mid_ref, midb_ref, ld_ref, ldg_ref, acc_ref, lat_ref):
        step = pl.program_id(0) * inner + pl.program_id(1)

        @pl.when(step == 0)
        def _():
            acc_ref[...] = h_ref[...]
            lat_ref[...] = jnp.zeros_like(lat_ref)

        h = hb_ref[...]
        lat = l_ref[...]
        gate = nn(h, upper(w_ref, 0)) + nn(lat[:, :rank], fb_ref[0, :rank])
        up = nn(h, upper(w_ref, 1)) + nn(lat[:, rank:], fb_ref[0, rank:])
        pre_ref[0] = gate.astype(BF16)
        pre_ref[1] = up.astype(BF16)
        active = (gate * jax.nn.sigmoid(gate) * up).astype(BF16)
        acc_ref[...] += nn(active, lower(wd_ref))
        lat_ref[...] += nt(active, da_ref[0])

        @pl.when(step == steps - 1)
        def _():
            latent_down = lat_ref[...].astype(BF16)
            total = acc_ref[...] + nn(latent_down, db_ref[...])
            result, normed, inverse = norm_forward(total, g_ref[...], s_ref[...])
            res_ref[...] = result.astype(BF16)
            grad = norm_backward(c_ref[...], normed, inverse, g_ref[...])
            mid_ref[...] = grad
            grad_b = grad.astype(BF16)
            midb_ref[...] = grad_b
            ld_ref[...] = latent_down
            ldg_ref[...] = nt(grad_b, db_ref[...]).astype(BF16)

    full = lambda array: pl.BlockSpec(array.shape, lambda t, b: (0,) * array.ndim)
    fixed = lambda rows, size: pl.BlockSpec((rows, size), lambda t, b: (0, 0))
    operands = [hidden, hidden_b, latent, *arrays, fb, da, db, gain, shift, cotangent]
    return pl.pallas_call(
        kernel,
        grid=(shards, inner),
        in_specs=[
            full(hidden),
            full(hidden_b),
            full(latent),
            *views,
            pl.BlockSpec((1, 2 * rank, sub), lambda t, b: (t, 0, b)),
            pl.BlockSpec((1, rank, sub), lambda t, b: (t, 0, b)),
            full(db),
            full(gain),
            full(shift),
            full(cotangent),
        ],
        out_specs=[
            pl.BlockSpec((2, count, sub), lambda t, b: (0, 0, t * inner + b)),
            fixed(count, width),
            fixed(count, width),
            fixed(count, width),
            fixed(count, rank),
            fixed(count, rank),
        ],
        out_shape=[
            jax.ShapeDtypeStruct((2, count, shards * units), BF16),
            jax.ShapeDtypeStruct((count, width), BF16),
            jax.ShapeDtypeStruct((count, width), F32),
            jax.ShapeDtypeStruct((count, width), BF16),
            jax.ShapeDtypeStruct((count, rank), BF16),
            jax.ShapeDtypeStruct((count, rank), BF16),
        ],
        scratch_shapes=[pltpu.VMEM((count, width), F32), pltpu.VMEM((count, rank), F32)],
        cost_estimate=pl.CostEstimate(
            flops=6 * count * width * shards * units,
            bytes_accessed=6 * width * shards * units + 4 * count * shards * units,
            transcendentals=count * shards * units,
        ),
        name="ffn_forward",
    )(*operands)


def ffn_backward(
    grad_b, grad, pre, latent_down, latent_down_grad, latent_ffn, weights, fb, da, fa, hidden_b,
    normed, inverse, gain, latent_out, ob, oa, mixed, out_all,
):
    count, width = grad.shape
    shards, _, units = fb.shape
    rank = ob.shape[0]
    sub = min(512, units)
    inner = units // sub
    steps = shards * inner
    arrays, views, upper, lower = ffn_views(weights, width, sub)

    def kernel(gb_ref, g_ref, pre_ref, ld_ref, ldg_ref, lf_ref, w_ref, wd_ref, fb_ref, da_ref, fa_ref,
               hb_ref, n_ref, i_ref, gain_ref, lo_ref, ob_ref, oa_ref, m_ref, wo_ref,
               first_ref, mixed_ref, split_ref, common_ref, acc_ref, lat_ref):
        step = pl.program_id(0) * inner + pl.program_id(1)

        @pl.when(step == 0)
        def _():
            acc_ref[...] = g_ref[...]
            lat_ref[...] = jnp.zeros_like(lat_ref)

        ldg = ldg_ref[...]
        lf = lf_ref[...]
        grad_active = nt(gb_ref[...], lower(wd_ref)) + nn(ldg, da_ref[0])
        gate = pre_ref[0].astype(F32)
        up = pre_ref[1].astype(F32)
        sigma = jax.nn.sigmoid(gate)
        swish = gate * sigma
        active = (swish * up).astype(BF16)
        grad_gate = (grad_active * up * (sigma + swish * (1.0 - sigma))).astype(BF16)
        grad_up = (grad_active * swish).astype(BF16)
        split_ref[0] = jnp.concatenate(
            [tn(ldg, active), tn(lf[:, :rank], grad_gate), tn(lf[:, rank:], grad_up)], axis=0
        ).astype(BF16)
        acc_ref[...] += nt(grad_gate, upper(w_ref, 0)) + nt(grad_up, upper(w_ref, 1))
        lat_ref[...] += jnp.concatenate(
            [nt(grad_gate, fb_ref[0, :rank]), nt(grad_up, fb_ref[0, rank:])], axis=1
        )

        @pl.when(step == steps - 1)
        def _():
            lat = lat_ref[...].astype(BF16)
            total = acc_ref[...] + nn(lat, fa_ref[...])
            first = norm_backward(total, n_ref[...], i_ref[...], gain_ref[...])
            first_ref[...] = first
            branch = first.astype(BF16)
            log = nt(branch, ob_ref[...]).astype(BF16)
            common_ref[...] = jnp.concatenate(
                [
                    tn(ld_ref[...], gb_ref[...]),
                    tn(lat, hb_ref[...]),
                    tn(lo_ref[...], branch),
                    tn(log, m_ref[...]),
                ],
                axis=0,
            ).astype(BF16)
            mixed_ref[...] = (nt(branch, wo_ref[...]) + nn(log, oa_ref[...])).astype(BF16)

    full = lambda array: pl.BlockSpec(array.shape, lambda t, b: (0,) * array.ndim)
    fixed = lambda rows, size: pl.BlockSpec((rows, size), lambda t, b: (0, 0))
    head = [grad_b, grad, pre, latent_down, latent_down_grad, latent_ffn]
    rest = [fa, hidden_b, normed, inverse, gain, latent_out, ob, oa, mixed, out_all]
    specs = [full(array) for array in head]
    specs[2] = pl.BlockSpec((2, count, sub), lambda t, b: (0, 0, t * inner + b))
    specs += views
    specs += [
        pl.BlockSpec((1, 2 * rank, sub), lambda t, b: (t, 0, b)),
        pl.BlockSpec((1, rank, sub), lambda t, b: (t, 0, b)),
    ]
    specs += [full(array) for array in rest]
    return pl.pallas_call(
        kernel,
        grid=(shards, inner),
        in_specs=specs,
        out_specs=[
            fixed(count, width),
            fixed(count, width),
            pl.BlockSpec((1, 3 * rank, sub), lambda t, b: (t, 0, b)),
            fixed(5 * rank, width),
        ],
        out_shape=[
            jax.ShapeDtypeStruct((count, width), F32),
            jax.ShapeDtypeStruct((count, width), BF16),
            jax.ShapeDtypeStruct((shards, 3 * rank, units), BF16),
            jax.ShapeDtypeStruct((5 * rank, width), BF16),
        ],
        scratch_shapes=[pltpu.VMEM((count, width), F32), pltpu.VMEM((count, 2 * rank), F32)],
        cost_estimate=pl.CostEstimate(
            flops=6 * count * width * shards * units,
            bytes_accessed=6 * width * shards * units + 4 * count * shards * units,
            transcendentals=count * shards * units,
        ),
        name="ffn_backward",
    )(*head, *arrays, fb, da, *rest)


def norm_forward(rows, gain, shift):
    centre = jnp.mean(rows, axis=-1, keepdims=True)
    centred = rows - centre
    spread = jnp.mean(centred * centred, axis=-1, keepdims=True)
    inverse = lax.rsqrt(spread + 1e-12)
    normed = centred * inverse
    return (normed * gain + shift, normed, inverse)


def norm_backward(grads, normed, inverse, gain):
    scaled = grads * gain
    first_mean = jnp.mean(scaled, axis=-1, keepdims=True)
    second_mean = jnp.mean(scaled * normed, axis=-1, keepdims=True)
    return inverse * (scaled - first_mean - normed * second_mean)


def rope_tables(length, extra):
    half = HEAD_DIM // 2
    step = 64
    freq = 10000.0 ** (-(2.0 * np.arange(half)) / HEAD_DIM)
    freq = np.tile(freq, LANES // half)
    sign = np.where(np.arange(LANES) % HEAD_DIM < half, -1.0, 1.0)
    coarse = ((np.arange(length + extra) % length)[::step, None] * freq).astype(np.float64)
    fine = np.arange(step)[:, None] * freq
    f = lambda array: jnp.asarray(array, F32)
    cos_c, sin_c = f(np.cos(coarse))[:, None], f(np.sin(coarse))[:, None]
    cos_f, sin_f = f(np.cos(fine))[None], f(np.sin(fine))[None]
    cosine = (cos_c * cos_f - sin_c * sin_f).reshape(-1, LANES)
    sine = ((sin_c * cos_f + cos_c * sin_f) * f(sign)).reshape(-1, LANES)
    return cosine, sine


def window(array, start, count):
    return lax.dynamic_slice_in_dim(array, start, count, 0)


def gather_weight(local, parts, part):
    rows = local.shape[0] // parts
    piece = window(local, part * rows, rows)
    return lax.all_gather(piece, ALL, axis=0, tiled=True)


def gather_ffn(w_gate_up, w_down, parts, part):
    _, width, units = w_gate_up.shape
    upper = w_gate_up.reshape(2 * width, units)
    if units == width and width % (128 * parts // 8) == 0 and parts == 8:
        high, low = 2 * width // parts, units // parts
        piece = jnp.concatenate(
            [window(upper, part * high, high), window(w_down, part * low, low)], axis=0
        )
        whole = lax.all_gather(piece, ALL, axis=0, tiled=True)
        return (whole.reshape(-1, parts, high + low, units),)
    return (
        gather_weight(upper, parts, part).reshape(-1, 2, width, units),
        gather_weight(w_down, parts, part).reshape(-1, units, width),
    )


def flip(bit):
    return [(i, i ^ bit) for i in range(4)]


def send_round(piece):
    shards = lax.axis_size("tensor")
    return [lax.ppermute(piece, "tensor", cyclic(shards, k)) for k in range(1, shards)]


def spread_first(stack):
    return lax.ppermute(stack, "yx", flip(1)), lax.ppermute(stack, "yx", flip(2))


def spread_second(across, along):
    half = across.shape[0] // 2
    return (
        lax.ppermute(across[:half], "yx", flip(2)),
        lax.ppermute(along[half:], "yx", flip(1)),
    )


def swap_core(near):
    return lax.ppermute(near, "core", [(0, 1), (1, 0)])


def assemble(own, near, far, outs, store):
    shards = near.shape[1] + 1
    rows, cols = own.shape[1:]
    scalars = jnp.stack(
        [lax.axis_index("tensor"), lax.axis_index("yx"), lax.axis_index("core")]
    ).astype(jnp.int32)

    def behind(t, s):
        return lax.rem(s[0] - t + shards, shards)

    def kernel(scalar_ref, own_ref, near_ref, far_ref, *out_refs):
        mine = behind(pl.program_id(0), scalar_ref) == 0
        first = scalar_ref[2] == 0

        @pl.when(mine)
        def _():
            for j in range(8):
                store(own_ref[j], j, out_refs)

        for low_ref, high_ref, here in ((near_ref, far_ref, first), (far_ref, near_ref, jnp.logical_not(first))):

            @pl.when(jnp.logical_and(jnp.logical_not(mine), here))
            def _():
                for i in range(4):
                    side = lax.bitwise_xor(scalar_ref[1], i)
                    store(low_ref[side, 0], 2 * i, out_refs)
                    store(high_ref[side, 0], 2 * i + 1, out_refs)

    other = pl.BlockSpec(
        (4, 1, rows, cols), lambda t, s: (0, jnp.maximum(behind(t, s) - 1, 0), 0, 0)
    )
    return pl.pallas_call(
        kernel,
        grid_spec=pltpu.PrefetchScalarGridSpec(
            num_scalar_prefetch=1,
            grid=(shards,),
            in_specs=[pl.BlockSpec((8, rows, cols), lambda t, s: (0, 0, 0)), other, other],
            out_specs=[spec for _, spec in outs],
        ),
        out_shape=[jax.ShapeDtypeStruct(shape, BF16) for shape, _ in outs],
        cost_estimate=pl.CostEstimate(
            flops=0, bytes_accessed=32 * shards * rows * cols, transcendentals=0
        ),
    )(scalars, own, near, far)


def assemble_qkv(own, near, far, width, local):
    shards = near.shape[1] + 1
    size = width // 8
    short = local // 8
    head = 3 * size

    def store(piece, j, outs):
        for p in range(3):
            outs[0][0, p, j * size : (j + 1) * size] = piece[p * size : (p + 1) * size]
        for c in range(width // local):
            outs[1][j * short : (j + 1) * short, c * local : (c + 1) * local] = piece[
                head + c * short : head + (c + 1) * short
            ]

    outs = [
        (
            (shards, 3, width, local),
            pl.BlockSpec((1, 3, width, local), lambda t, s: (t, 0, 0, 0)),
        ),
        ((shards * local, width), pl.BlockSpec((local, width), lambda t, s: (t, 0))),
    ]
    return assemble(own, near, far, outs, store)


def in_order(blocks, place):
    shards = len(blocks)
    stack = jnp.stack(blocks)
    return jnp.stack(
        [
            lax.dynamic_index_in_dim(stack, lax.rem(place - t + shards, shards), 0, keepdims=False)
            for t in range(shards)
        ]
    )


def cyclic(size, step):
    return [(i, (i + step) % size) for i in range(size)]


def send_grads(share):
    shards = lax.axis_size("tensor")
    place = lax.axis_index("tensor")
    received = [share(place)]
    for step in range(1, shards):
        sent = share(lax.rem(place + step, shards))
        received.append(lax.ppermute(sent, "tensor", cyclic(shards, step)))
    return received


def add_all(blocks):
    total = blocks[0].astype(F32)
    for block in blocks[1:]:
        total = total + block.astype(F32)
    return total


def after(array, *marks):
    return lax.optimization_barrier((array, *marks))[0]


def layer(
    layer_input,
    output_grad,
    segments,
    adapter_ids,
    ln_gain,
    ln_bias,
    w_qkv,
    w_out,
    w_gate_up,
    w_down,
    qkv_a,
    qkv_b,
    out_a,
    out_b,
    ffn_a,
    ffn_b,
    down_a,
    down_b,
):
    seq_count, length = segments.shape
    assert seq_count == 1
    width = layer_input.shape[1]
    shards = lax.axis_size("tensor")
    parts = lax.axis_size(DP)
    place = lax.axis_index("tensor")
    part = lax.axis_index(DP)
    members = shards // 2
    half = length // 2
    count = length // shards
    group = place // members
    member = lax.rem(place, members)
    local = w_qkv.shape[2]
    units = w_down.shape[0]
    rank = out_b.shape[1]

    adapter = adapter_ids[0, 0]
    pick = lambda stack: lax.dynamic_index_in_dim(stack, adapter, 0, keepdims=False)
    qa, ob, fa, db = pick(qkv_a), pick(out_b), pick(ffn_a), pick(down_b)
    small = jnp.concatenate(
        [
            pick(qkv_b),
            pick(out_a),
            pick(ffn_b).reshape(-1, local),
            pick(down_a).reshape(-1, local),
        ],
        axis=0,
    )
    labels = segments[0]
    long = labels[: length - half + 1] == labels[half - 1 :]
    start = jnp.sum(jnp.where(long, jnp.arange(length - half + 1, dtype=jnp.int32), 0))
    group_start = start + group * half
    own_start = start + place * count
    x_group = roll_rows([layer_input], place, group_start, half, BF16)
    x_own_b = window(x_group, member * count, count)
    cotangent = roll_rows([output_grad], place, own_start, count, F32)
    labels_twice = jnp.concatenate([labels, labels[:half]])
    labels_group = window(labels_twice, group_start, half)
    labels_own = window(labels_group, member * count, count)
    cosine, sine = rope_tables(length, half)
    tables = (window(cosine, group_start, half), window(sine, group_start, half))
    tables_own = tuple(window(table, member * count, count) for table in tables)

    ffn_all = gather_ffn(w_gate_up, w_down, parts, part)
    if parts == 8:
        qkv_pieces = w_qkv.reshape(3, 8, width // 8, local).transpose(1, 0, 2, 3)
        out_pieces = w_out.reshape(8, local // 8, width // local, local).transpose(0, 2, 1, 3)
        pieces = jnp.concatenate(
            [
                qkv_pieces.reshape(8, 3 * width // 8, local),
                out_pieces.reshape(8, width // 8, local),
            ],
            axis=1,
        )
        piece = lax.dynamic_index_in_dim(pieces, part, 0, keepdims=False)
        joined = send_round(jnp.concatenate([piece, small], axis=0))
        size = piece.shape[0]
        small = in_order([small] + [block[size:] for block in joined], place)
        stack = jnp.concatenate([block[:size] for block in joined], axis=0)
        stack = after(stack, x_group, cotangent)
        across, along = spread_first(stack)
        corner = jnp.concatenate(spread_second(across, along), axis=0)
        near = jnp.stack([stack, across, along, corner]).reshape(4, shards - 1, size, local)
        far = swap_core(near)
        qkv_all, out_all = assemble_qkv(pieces, near, far, width, local)
    else:
        qkv_all = gather_weight(w_qkv.reshape(3 * width, local), parts, part)
        qkv_all = qkv_all.reshape(shards, 3, width, local)
        out_all = gather_weight(w_out, parts, part)
        small = lax.all_gather(small, "tensor", axis=0)
    cuts = np.cumsum([3 * rank, rank, 2 * rank * (units // local)])
    rejoin = lambda piece: piece.transpose(1, 0, 2).reshape(piece.shape[1], -1)
    qb = rejoin(small[:, : cuts[0]])
    oa = rejoin(small[:, cuts[0] : cuts[1]])
    fb = small[:, cuts[1] : cuts[2]].reshape(shards, 2 * rank, units)
    da = small[:, cuts[2] :].reshape(shards, rank, units)

    latent_qkv = nt(x_group, qa).astype(BF16)
    latent_own = window(latent_qkv, member * count, count)
    query, keys, values = project_qkv(
        x_group, x_own_b, qkv_all, latent_qkv, latent_own, qb, tables, tables_own
    )
    mixed, logs = attend(query, keys, values, labels_own, labels_group)
    hidden, hidden_b, normed, inverse, latent_out, latent_ffn = out_forward(
        mixed, out_all, oa, ob, x_own_b, ln_gain[:1], ln_bias[:1], fa
    )

    pre, result, grad_mid, grad_ffn, latent_down, latent_down_grad = ffn_forward(
        hidden, hidden_b, latent_ffn, ffn_all, fb, da, db, ln_gain[1:], ln_bias[1:], cotangent
    )
    rolled = lax.all_gather(result, "tensor", axis=0, tiled=True)

    grad_first, grad_mixed, split, common = ffn_backward(
        grad_ffn, grad_mid, pre, latent_down, latent_down_grad, latent_ffn, ffn_all, fb, da, fa,
        hidden_b, normed, inverse, ln_gain[:1], latent_out, ob, oa, mixed, out_all,
    )

    dq = None
    received = []
    before = None
    for d in range(1, members):
        target = lax.rem(member + d, members)
        dq, dk, dv = attend_back(
            query, keys, values, mixed, grad_mixed, logs, labels_own, labels_group, tables,
            tables_own, target, dq, False,
        )
        sent, part_of = project_back(
            [dk, dv], 1, qkv_all, qb, qa, latent_qkv, x_group, target, None, None
        )
        before = part_of if before is None else before + part_of
        links = [
            (g * members + i, g * members + (i + d) % members)
            for g in range(2)
            for i in range(members)
        ]
        received.append(lax.ppermute(sent, "tensor", links))

    def early_share(target):
        mine = lax.dynamic_index_in_dim(split, target, 0, keepdims=False)
        return jnp.concatenate([common, mine.reshape(-1, width)], axis=0)

    common = after(common, sent)
    early = send_grads(early_share)
    dq, dk, dv = attend_back(
        query, keys, values, mixed, grad_mixed, logs, labels_own, labels_group, tables, tables_own,
        member, dq, True,
    )
    back, qkv_part = project_back(
        [dq, dk, dv], 0, qkv_all, qb, qa, latent_qkv, x_group, member, grad_first, before
    )
    for piece in received:
        back = back + after(piece, back).astype(F32)
    back = back.astype(BF16)
    blocks = [back] + send_round(back)
    qkv_part = after(qkv_part, back)
    late = send_grads(lambda target: qkv_part)

    adapters = qkv_a.shape[0]
    hot = (adapter == jnp.arange(adapters, dtype=jnp.int32)).astype(BF16)
    flag = jnp.zeros((16, width), BF16).at[0, :adapters].set(hot)
    early = [after(piece, back) for piece in early]
    sums = jnp.concatenate([add_all(early).astype(BF16), add_all(late).astype(BF16), flag], axis=0)
    every = lax.all_gather(sums, DP, axis=0)
    placed = jnp.einsum(
        "sj,srn->jrn", every[:, -16, :adapters], every[:, :-16], preferred_element_type=F32
    )
    own_columns = lambda rows: lax.dynamic_slice_in_dim(rows, place * local, local, 2)
    mark = 5 * rank
    down_b_grad = placed[:, :rank]
    ffn_a_grad = placed[:, rank : 3 * rank]
    out_b_grad = placed[:, 3 * rank : 4 * rank]
    out_a_grad = own_columns(placed[:, 4 * rank : mark])
    extent = 3 * rank * units // width
    own_split = placed[:, mark : mark + extent].reshape(adapters, 3 * rank, units)
    down_a_grad = own_split[:, :rank]
    ffn_b_grad = own_split[:, rank:]
    mark += extent
    qkv_b_grad = own_columns(placed[:, mark : mark + 3 * rank])
    qkv_a_grad = placed[:, mark + 3 * rank : mark + 6 * rank]

    output = roll_rows([after(rolled, back)], place, -start, length, BF16)
    blocks = [after(block, output, qkv_a_grad) for block in blocks]
    grad_whole = roll_rows(blocks, place, -start, length, F32)
    return (
        output,
        grad_whole,
        qkv_a_grad,
        qkv_b_grad,
        out_a_grad,
        out_b_grad,
        ffn_a_grad,
        ffn_b_grad,
        down_a_grad,
        down_b_grad,
    )


def solution(mesh):
    devices = mesh.devices
    mesh = Mesh(
        devices.reshape(devices.shape[0] // 2, 2, devices.shape[1]), ("yx", "core", "tensor")
    )
    in_specs = (
        P(DP, None),
        P(DP, None),
        P(DP, None),
        P(DP, None),
        P(),
        P(),
        P(None, None, "tensor"),
        P("tensor", None),
        P(None, None, "tensor"),
        P("tensor", None),
        P(),
        P(None, None, "tensor"),
        P(None, None, "tensor"),
        P(),
        P(),
        P(None, None, "tensor"),
        P(None, None, "tensor"),
        P(),
    )
    out_specs = (
        P(DP, None),
        P(DP, None),
        P(),
        P(None, None, "tensor"),
        P(None, None, "tensor"),
        P(),
        P(),
        P(None, None, "tensor"),
        P(None, None, "tensor"),
        P(),
    )
    return jax.shard_map(layer, mesh=mesh, in_specs=in_specs, out_specs=out_specs, check_vma=False)
```

time: 750 us -> 498 us (0.66)
  matrix products: 166 us -> 2.94 us
  waiting for transfers between devices: 326 us -> 195 us
  Pallas kernels: 98.7 us -> 185 us
  blocking collectives: 60.5 us -> 0 us
  starting transfers between devices: 2.41 us -> 27.2 us
  local copies, waits for them, and re-layouts: 59.5 us -> 45.1 us
    all_gather x8 -> x3, waiting for transfers between devices: 270 us -> 50.4 us  [the longest x1 25.4 us: gather_ffn(): whole = lax.all_gather(piece, ALL, axis=0, tiled=True)]
    pallas_call x1 -> x8, Pallas kernels: 28.1 us -> 131 us  [the longest x2 34.9 us: attend_back(): pl.pallas_call(kernel, grid_spec=pltpu.PrefetchScalarGridSpec(num_scalar_...]
    ppermute x1 -> x18, waiting for transfers between devices: 55.8 us -> 145 us  [the longest x6 83 us: send_round(): lax.ppermute(piece, 'tensor', cyclic(shards, k))]
    dot_general x56 -> x1, matrix products: 84.2 us -> 2.25 us  [layer(): jnp.einsum('sj,srn->jrn', every[:, -16, :adapters], every[:, :-16], prefe...]
    dot_general x45 -> x1, matrix products: 82.2 us -> 0.69 us  [nt(): lax.dot_general(left, right, (((1,), (1,)), ((), ())), preferred_element_...]
    all_gather x3 -> x0, blocking collectives: 60.5 us -> none  [the longest x1 29.7 us: reduce_grads(): lax.all_gather(placed[:, :cut].astype(BF16), 'tensor', axis=2, tiled=True)]
    ppermute x1 -> x18, starting transfers between devices: 1.54 us -> 27.1 us  [the longest x6 12.4 us: send_round(): lax.ppermute(piece, 'tensor', cyclic(shards, k))]
    pallas_call x4, Pallas kernels: 40.6 us -> 23.5 us  [roll_rows(): pl.pallas_call(kernel, grid_spec=pltpu.PrefetchScalarGridSpec(num_scalar_...]
  transfers between devices with their start and end apart: 11 -> 21, of which waited for: 7 -> 11; matrix products, arithmetic and copies ran while one was open for 19% -> 10% of each run, Pallas kernels for 11% -> 31%
where the time goes in v2:
time: 498 us; the launch traced here: 488 us
  waiting for transfers between devices  195 us (39%)
  Pallas kernels  185 us (37%)
  local copies, waits for them, and re-layouts  45.1 us (9%)
  starting transfers between devices  27.2 us (5%)
  between operations  17.3 us (3%)
  other arithmetic  15.8 us (3%)
    ppermute x6, waiting for transfers between devices, send_round(): lax.ppermute(piece, 'tensor', cyclic(shards, k))  83 us
    pallas_call x2, Pallas kernels, attend_back(): pl.pallas_call(kernel, grid_spec=pltpu.PrefetchScalarGridSpec(num_scalar_...  34.9 us
    pallas_call x1, Pallas kernels, ffn_backward(): pl.pallas_call(kernel, grid=(shards, inner), in_specs=specs, out_specs=[f...  34.7 us
    ppermute x1, waiting for transfers between devices, spread_first(): lax.ppermute(stack, 'yx', flip(1))  27.4 us
    pallas_call x1, Pallas kernels, ffn_forward(): pl.pallas_call(kernel, grid=(shards, inner), in_specs=[full(hidden), full...  26.9 us
    all_gather x1, waiting for transfers between devices, gather_ffn(): whole = lax.all_gather(piece, ALL, axis=0, tiled=True)  25.4 us
    all_gather x1, waiting for transfers between devices, layer(): every = lax.all_gather(sums, DP, axis=0)  24.9 us
    pallas_call x4, Pallas kernels, roll_rows(): pl.pallas_call(kernel, grid_spec=pltpu.PrefetchScalarGridSpec(num_scalar_...  23.5 us
  transfers between devices with their start and end apart: 21, of which 11 were waited for; matrix products, arithmetic and copies ran while one was open for 10% of the time, Pallas kernels for 31%

profile of v2, /device:TPU:0, one launch (start us, length us, event | category | flops | bytes accessed | tf_op | source)
XLA Modules:
  0.0 488.3 jit_solution(4226890330925452934)
XLA Ops:
  7.2 1.2 constant_dynamic-slice_fusion.3
  10.0 1.6 copy.52
  15.2 1.4 constant_dynamic-update-slice_fusion.3
  16.6 1.3 constant_dynamic-update-slice_fusion.2
  19.1 5.1 %collective-permute-start.2 = (bf16[768,256]{1,0:T(8,128)(2,1)}, bf16[768,256]{1,0:T(8,128)(2,1)S(1)}, u32[]{:S(2)}, u32[]{:S(2)}) collective-permute-start(bf16[768,256]{1,0:T(8,128)(2,1)} %constant_dynamic-update-slice_fusion), channel_id=1, source_target_pairs={{0,3},{1,0},{2,1},{3,2},{4,7},{5,4},{6,5},{7,6},{8,11},{9,8},{10,9... | collective-permute-start | bytes 1179656 | tf_op jit(solution)/shard_map/ppermute | solution.py:712
  24.2 1.0 collective-permute-start
  28.0 4.7 roll_rows.5.c_ref
  33.3 4.8 roll_rows.4.x_ref
  38.0 1.4 dynamic-slice_bitcast_fusion.7.b_ref.ob_ref
  39.4 28.1 %collective-permute-done = bf16[768,256]{1,0:T(8,128)(2,1)} collective-permute-done((bf16[768,256]{1,0:T(8,128)(2,1)}, bf16[768,256]{1,0:T(8,128)(2,1)}, u32[]{:S(2)}, u32[]{:S(2)}) %collective-permute-start) | collective-permute-done | bytes 393248 | tf_op jit(solution)/shard_map/ppermute | solution.py:712
  67.5 1.0 slice.142
  68.5 6.3 %collective-permute-done.1 = bf16[768,256]{1,0:T(8,128)(2,1)S(1)} collective-permute-done((bf16[768,256]{1,0:T(8,128)(2,1)}, bf16[768,256]{1,0:T(8,128)(2,1)S(1)}, u32[]{:S(2)}, u32[]{:S(2)}) %collective-permute-start.1) | collective-permute-done | bytes 393248 | tf_op jit(solution)/shard_map/ppermute | solution.py:712
  76.4 1.6 collective-permute-start.3
  77.9 1.5 collective-permute-start.4
  79.5 1.0 copy.56.all_ref
  80.6 1.4 dynamic-slice_bitcast_fusion.6.db_ref
  81.9 1.5 dynamic-slice_bitcast_fusion.5.f_ref.fa_ref
  85.8 27.4 %collective-permute-done.3 = bf16[1536,256]{1,0:T(8,128)(2,1)} collective-permute-done((bf16[1536,256]{1,0:T(8,128)(2,1)S(1)}, bf16[1536,256]{1,0:T(8,128)(2,1)}, u32[]{:S(2)}, u32[]{:S(2)}) %collective-permute-start.3) | collective-permute-done | bytes 786464 | tf_op jit(solution)/shard_map/ppermute | solution.py:716
  113.2 1.0 slice.145
  114.2 1.6 collective-permute-start.5
  115.8 1.1 slice.146
  116.9 1.5 collective-permute-start.6
  119.6 4.0 collective-permute-done.5
  123.6 2.3 collective-permute-done.6
  126.0 3.0 pad_maximum_fusion.near_ref
  130.6 1.1 constant_dynamic-slice_fusion.6
  131.7 1.0 constant_dynamic-slice_fusion.15.o_ref.x_ref
  132.7 1.5 pad_maximum_fusion.1.own_ref
  134.8 1.0 slice_bitcast_fusion
  135.8 1.0 slice_bitcast_fusion.1
  136.8 1.0 slice_bitcast_fusion.2
  140.8 8.4 %shard_map.294 = (bf16[4,3,1024,256]{3,2,1,0:T(8,128)(2,1)}, bf16[1024,1024]{1,0:T(8,128)(2,1)}) custom-call(s32[3]{0:T(128)} %pad_add_fusion.scalar_ref, bf16[8,512,256]{2,1,0:T(8,128)(2,1)} %pad_maximum_fusion.1.own_ref, bf16[4,3,512,256]{3,2,1,0:T(8,128)(2,1)} %pad_maximum_fusion.near_ref, bf16[4,3,512,256]{3,2,1,0:T(8,128)(2,1)} %collective-permute-done.7.far_ref), custom_call_target="tpu_custom_call" | custom-call | bytes 16777216 | tf_op jit(solution)/shard_map/pallas_call | solution.py:762
  149.3 12.1 %project_qkv.1 = (bf16[512,1024]{1,0:T(8,128)(2,1)}, bf16[1024,1024]{1,0:T(8,128)(2,1)}, bf16[1024,1024]{1,0:T(8,128)(2,1)}) custom-call(bf16[1024,1024]{1,0:T(8,128)(2,1)} %roll_rows.4.x_ref, bf16[512,1024]{1,0:T(8,128)(2,1)} %constant_dynamic-slice_fusion.15.o_ref.x_ref, bf16[4,3,1024,256]{3,2,1,0:T(8,128)(2,1)} %get-tuple-element.69.w_ref, ...), custom_call_target="tpu_custom_call" | custom-call | flops 5368709120 | bytes 20971520 | tf_op jit(solution)/shard_map/project_qkv/pallas_call | solution.py:122
  161.4 18.0 %attend.1 = (bf16[512,1024]{1,0:T(8,128)(2,1)}, f32[8,8,512]{2,1,0:T(8,128)}) custom-call(bf16[512,1024]{1,0:T(8,128)(2,1)} %get-tuple-element.70.q_ref, bf16[1024,1024]{1,0:T(8,128)(2,1)} %get-tuple-element.71.k_ref, bf16[1024,1024]{1,0:T(8,128)(2,1)} %get-tuple-element.72.v_ref, s32[1,512]{1,0:T(1,128)} %bitcast.110, s32[1024,1]{1,0:T(8,128)} %copy.56.all_ref), custom_call_target="tpu_custom_call" | custom-call | flops 8589934592 | bytes 6291456 | tf_op jit(solution)/shard_map/attend/pallas_call | solution.py:186
  179.3 6.9 %out_forward.1 = (f32[512,1024]{1,0:T(8,128)}, bf16[512,1024]{1,0:T(8,128)(2,1)}, f32[512,1024]{1,0:T(8,128)}, f32[512,1]{1,0:T(8,128)}, bf16[512,16]{1,0:T(8,128)(2,1)}, /*index=5*/bf16[512,32]{1,0:T(8,128)(2,1)}) custom-call(bf16[512,1024]{1,0:T(8,128)(2,1)} %get-tuple-element.73.m_ref, bf16[1024,1024]{1,0:T(8,128)(2,1)} %get-tuple-element.74.w_ref.wo_ref, ...), custom_call_target="tpu_custom_call" | custom-call | flops 1073741824 | bytes 9437184 | tf_op jit(solution)/shard_map/out_forward/pallas_call | solution.py:415
  186.2 25.4 %all-gather.5.cloned.1.call-done = bf16[12288,1024]{1,0:T(8,128)(2,1)} async-done(((bf16[384,1024]{1,0:T(8,128)(2,1)}), bf16[12288,1024]{1,0:T(8,128)(2,1)}) %all-gather.5.cloned.1.call-update) | async-done | bytes 25165840 | tf_op jit(solution)/shard_map/all_gather | solution.py:698
  211.6 26.9 %ffn_forward.1 = (bf16[2,512,4096]{2,1,0:T(8,128)(2,1)}, bf16[512,1024]{1,0:T(8,128)(2,1)}, f32[512,1024]{1,0:T(8,128)}, bf16[512,1024]{1,0:T(8,128)(2,1)}, bf16...) custom-call(f32[512,1024]{1,0:T(8,128)} %get-tuple-element.75.h_ref, bf16[512,1024]{1,0:T(8,128)(2,1)} %get-tuple-element.76.hb_ref, ...), custom_call_target="tpu_custom_call" | custom-call | flops 12884901888 | bytes 33554432 | tf_op jit(solution)/shard_map/ffn_forward/pallas_call | solution.py:510
  238.6 34.7 %ffn_backward.1 = (f32[512,1024]{1,0:T(8,128)}, bf16[512,1024]{1,0:T(8,128)(2,1)}, bf16[4,48,1024]{2,1,0:T(8,128)(2,1)}, bf16[80,1024]{1,0:T(8,128)(2,1)}) custom-call(bf16[512,1024]{1,0:T(8,128)(2,1)} %get-tuple-element.79.gb_ref, f32[512,1024]{1,0:T(8,128)} %get-tuple-element.80.g_ref, bf16[2,512,4096]{2,1,0:T(8,128)(2,1)} %get-tuple-element.81.pre_ref, ...), custom_call_target="tpu_custom_call" | custom-call | flops 12884901888 | bytes 33554432 | tf_op jit(solution)/shard_map/ffn_backward/pallas_call | solution.py:622
  273.3 16.7 %attend_back.2 = (f32[512,1024]{1,0:T(8,128)}, bf16[512,1024]{1,0:T(8,128)(2,1)}, bf16[512,1024]{1,0:T(8,128)(2,1)}) custom-call(s32[1]{0:T(128)} %bitcast.41.block_ref, bf16[512,1024]{1,0:T(8,128)(2,1)} %get-tuple-element.70.q_ref, bf16[1024,1024]{1,0:T(8,128)(2,1)} %get-tuple-element.71.k_ref, bf16[1024,1024]{1,0:T(8,128)(2,1)} %get-tuple-element.72.v_ref, ...), custom_call_target="tpu_custom_call" | custom-call | flops 10737418240 | bytes 9437184 | tf_op jit(solution)/shard_map/attend_back/pallas_call | solution.py:282
  290.0 8.6 %project_back.2 = (bf16[512,1024]{1,0:T(8,128)(2,1)}, f32[64,1024]{1,0:T(8,128)}) custom-call(s32[1]{0:T(128)} %bitcast.41.block_ref, bf16[4,3,1024,256]{3,2,1,0:T(8,128)(2,1)} %get-tuple-element.69.w_ref, bf16[48,1024]{1,0:T(8,128)(2,1)} %bitcast.100, bf16[48,1024]{1,0:T(8,128)(2,1)} %copy-done.9, bf16[1024,48]{1,0:T(8,128)(2,1)} %copy-done.6, ...), custom_call_target="tpu_custom_call" | custom-call | flops 2147483648 | bytes 12582912 | tf_op jit(solution)/shard_map/project_back/pallas_call | solution.py:368
  299.6 2.0 collective-permute-start.9
  301.6 1.3 collective-permute-start.10
  302.8 1.3 collective-permute-start.11
  304.2 18.2 %attend_back.3 = (bf16[512,1024]{1,0:T(8,128)(2,1)}, bf16[512,1024]{1,0:T(8,128)(2,1)}, bf16[512,1024]{1,0:T(8,128)(2,1)}) custom-call(s32[1]{0:T(128)} %bitcast.40.block_ref, bf16[512,1024]{1,0:T(8,128)(2,1)} %get-tuple-element.70.q_ref, bf16[1024,1024]{1,0:T(8,128)(2,1)} %get-tuple-element.71.k_ref, bf16[1024,1024]{1,0:T(8,128)(2,1)} %get-tuple-element.72.v_ref, ...), custom_call_target="tpu_custom_call" | custom-call | flops 10737418240 | bytes 9437184 | tf_op jit(solution)/shard_map/attend_back/pallas_call | solution.py:282
  322.4 10.9 %project_back.3 = (f32[512,1024]{1,0:T(8,128)}, bf16[96,1024]{1,0:T(8,128)(2,1)}) custom-call(s32[1]{0:T(128)} %bitcast.40.block_ref, bf16[4,3,1024,256]{3,2,1,0:T(8,128)(2,1)} %get-tuple-element.69.w_ref, bf16[48,1024]{1,0:T(8,128)(2,1)} %bitcast.101, bf16[48,1024]{1,0:T(8,128)(2,1)} %copy-done.9, bf16[1024,48]{1,0:T(8,128)(2,1)} %copy-done.6, ...), custom_call_target="tpu_custom_call" | custom-call | flops 3221225472 | bytes 13631488 | tf_op jit(solution)/shard_map/project_back/pallas_call | solution.py:368
  333.3 15.8 %collective-permute-done.8 = bf16[512,1024]{1,0:T(8,128)(2,1)S(1)} collective-permute-done((bf16[512,1024]{1,0:T(8,128)(2,1)}, bf16[512,1024]{1,0:T(8,128)(2,1)S(1)}, u32[]{:S(2)}, u32[]{:S(2)}) %collective-permute-start.8) | collective-permute-done | bytes 1048608 | tf_op jit(solution)/shard_map/ppermute | solution.py:972
  349.1 2.0 add_convert_fusion.refs_0_
  351.3 3.7 collective-permute-start.14
  355.0 1.1 add_convert_fusion.1
  356.1 5.1 %collective-permute-done.12 = bf16[96,1024]{1,0:T(8,128)(2,1)S(1)} collective-permute-done((bf16[96,1024]{1,0:T(8,128)(2,1)S(1)}, bf16[96,1024]{1,0:T(8,128)(2,1)S(1)}, u32[]{:S(2)}, u32[]{:S(2)}) %collective-permute-start.12) | collective-permute-done | bytes 196640 | tf_op jit(solution)/shard_map/ppermute | solution.py:822
  361.2 7.2 %collective-permute-done.13 = bf16[96,1024]{1,0:T(8,128)(2,1)S(1)} collective-permute-done((bf16[96,1024]{1,0:T(8,128)(2,1)S(1)}, bf16[96,1024]{1,0:T(8,128)(2,1)S(1)}, u32[]{:S(2)}, u32[]{:S(2)}) %collective-permute-start.13) | collective-permute-done | bytes 196640 | tf_op jit(solution)/shard_map/ppermute | solution.py:822
  370.0 5.7 %collective-permute-start.17 = (bf16[512,1024]{1,0:T(8,128)(2,1)S(1)}, bf16[512,1024]{1,0:T(8,128)(2,1)S(1)}, u32[]{:S(2)}, u32[]{:S(2)}) collective-permute-start(bf16[512,1024]{1,0:T(8,128)(2,1)S(1)} %add_convert_fusion.refs_0_), channel_id=1, source_target_pairs={{0,3},{1,0},{2,1},{3,2},{4,7},{5,4},{6,5},{7,6},{8,11},{9,8},{10,9... | collective-permute-start | bytes 3145736 | tf_op jit(solution)/shard_map/ppermute | solution.py:712
  376.9 6.6 %roll_rows.6 = bf16[2048,1024]{1,0:T(8,128)(2,1)} custom-call(s32[3]{0:T(128)} %add_add_fusion.scalar_ref, bf16[2048,1024]{1,0:T(8,128)(2,1)} %all-gather.7.cloned.1.call-done.refs_0_), custom_call_target="tpu_custom_call" | custom-call | flops 1073741824 | bytes 12582912 | tf_op jit(solution)/shard_map/roll_rows/pallas_call | solution.py:66
  383.5 24.9 %all-gather.9.cloned.1.call-done = bf16[1920,1024]{1,0:T(8,128)(2,1)} async-done(((bf16[240,1024]{1,0:T(8,128)(2,1)}), bf16[1920,1024]{1,0:T(8,128)(2,1)}) %all-gather.9.cloned.1.call-update) | async-done | bytes 3932176 | tf_op jit(solution)/shard_map/all_gather | solution.py:999
  408.4 2.4 slice.152
  411.5 2.3 fusion
  414.2 2.1 copy.63
  416.2 48.6 %collective-permute-done.16.refs_2_ = bf16[512,1024]{1,0:T(8,128)(2,1)S(1)} collective-permute-done((bf16[512,1024]{1,0:T(8,128)(2,1)S(1)}, bf16[512,1024]{1,0:T(8,128)(2,1)S(1)}, u32[]{:S(2)}, u32[]{:S(2)}) %collective-permute-start.16) | collective-permute-done | bytes 1048608 | tf_op jit(solution)/shard_map/ppermute | solution.py:712
  466.9 1.6 copy.67
  468.5 1.6 copy.68
  470.1 1.1 copy.66
  471.2 1.1 copy.69
  472.3 1.1 copy.70
  474.1 7.5 %roll_rows.7 = f32[2048,1024]{1,0:T(8,128)} custom-call(s32[3]{0:T(128)} %add_add_fusion.scalar_ref, bf16[512,1024]{1,0:T(8,128)(2,1)} %copy-done.5, bf16[512,1024]{1,0:T(8,128)(2,1)} %collective-permute-done.15.refs_1_, bf16[512,1024]{1,0:T(8,128)(2,1)} %copy-done.8, bf16[512,1024]{1,0:T(8,128)(2,1)} %copy-done.7), custom_call_target="tpu_custom_call" | custom-call | flops 1073741824 | bytes 12582912 | tf_op jit(solution)/shard_map/roll_rows/pallas_call | solution.py:66
  (136 shorter events, 25.4 us)
Async XLA Ops:
  7.2 1.8 copy-start
  7.2 204.4 %all-gather.5.cloned.1.call-start = ((), (), s32[]{:S(2)}) async-start(), calls=%async_computation | async-start | bytes 25952256 | tf_op jit(solution)/shard_map/all_gather | solution.py:698
  9.9 1.6 copy-start.12
  9.9 367.0 %all-gather.7.cloned.1.call-start = ((), (), s32[]{:S(2)}) async-start(), calls=%async_computation.1 | async-start | bytes 5242880 | tf_op jit(solution)/shard_map/all_gather | solution.py:947
  11.5 3.7 copy-start.3
  11.9 13.3 %copy-start.18 = (s32[1,2048]{1,0:T(1,128)S(1)}, s32[1,2048]{1,0:T(1,128)}, u32[]{:S(2)}) copy-start(s32[1,2048]{1,0:T(1,128)} %param.27) | copy-start | bytes 24580
  13.6 19.0 %copy-start.10 = (bf16[128,256]{1,0:T(8,128)(2,1)}, bf16[128,256]{1,0:T(8,128)(2,1)S(1)}, u32[]{:S(2)}) copy-start(bf16[128,256]{1,0:T(8,128)(2,1)S(1)} %reshape.139) | copy-start | bytes 196612
  19.1 55.7 %collective-permute-start.2 = (bf16[768,256]{1,0:T(8,128)(2,1)}, bf16[768,256]{1,0:T(8,128)(2,1)S(1)}, u32[]{:S(2)}, u32[]{:S(2)}) collective-permute-start(bf16[768,256]{1,0:T(8,128)(2,1)} %constant_dynamic-update-slice_fusion), channel_id=1, source_target_pairs={{0,3},{1,0},{2,1},{3,2},{4,7},{5,4},{6,5},{7,6},{8,11},{9,8},{10,9... | collective-permute-start | bytes 1179656 | tf_op jit(solution)/shard_map/ppermute | solution.py:712
  24.2 50.6 %collective-permute-start.1 = (bf16[768,256]{1,0:T(8,128)(2,1)}, bf16[768,256]{1,0:T(8,128)(2,1)S(1)}, u32[]{:S(2)}, u32[]{:S(2)}) collective-permute-start(bf16[768,256]{1,0:T(8,128)(2,1)} %constant_dynamic-update-slice_fusion), channel_id=1, source_target_pairs={{0,2},{1,3},{2,0},{3,1},{4,6},{5,7},{6,4},{7,5},{8,10},{9,11},{10,... | collective-permute-start | bytes 1179656 | tf_op jit(solution)/shard_map/ppermute | solution.py:712
  24.2 43.3 %collective-permute-start = (bf16[768,256]{1,0:T(8,128)(2,1)}, bf16[768,256]{1,0:T(8,128)(2,1)}, u32[]{:S(2)}, u32[]{:S(2)}) collective-permute-start(bf16[768,256]{1,0:T(8,128)(2,1)} %constant_dynamic-update-slice_fusion), channel_id=1, source_target_pairs={{0,1},{1,2},{2,3},{3,0},{4,5},{5,6},{6,7},{7,4},{8,9},{9,10},{10,1... | collective-permute-start | bytes 1179656 | tf_op jit(solution)/shard_map/ppermute | solution.py:712
  39.4 44.9 %copy-start.2 = (bf16[1024,1024]{1,0:T(8,128)(2,1)S(1)}, bf16[1024,1024]{1,0:T(8,128)(2,1)}, u32[]{:S(2)}) copy-start(bf16[1024,1024]{1,0:T(8,128)(2,1)} %roll_rows.4.x_ref) | copy-start | bytes 6291460
  74.8 0.7 copy-start.15
  75.6 0.7 copy-start.14
  76.4 36.8 %collective-permute-start.3 = (bf16[1536,256]{1,0:T(8,128)(2,1)S(1)}, bf16[1536,256]{1,0:T(8,128)(2,1)}, u32[]{:S(2)}, u32[]{:S(2)}) collective-permute-start(bf16[1536,256]{1,0:T(8,128)(2,1)S(1)} %pad_maximum_fusion.2), channel_id=1, source_target_pairs={{0,8},{8,0},{16,24},{24,16},{1,9},{9,1},{17,25},{25,17},{2,10},{10... | collective-permute-start | bytes 2359304 | tf_op jit(solution)/shard_map/ppermute | solution.py:716
  77.9 37.9 %collective-permute-start.4 = (bf16[1536,256]{1,0:T(8,128)(2,1)S(1)}, bf16[1536,256]{1,0:T(8,128)(2,1)}, u32[]{:S(2)}, u32[]{:S(2)}) collective-permute-start(bf16[1536,256]{1,0:T(8,128)(2,1)S(1)} %pad_maximum_fusion.2), channel_id=1, source_target_pairs={{0,16},{8,24},{16,0},{24,8},{1,17},{9,25},{17,1},{25,9},{2,18},{10... | collective-permute-start | bytes 2359304 | tf_op jit(solution)/shard_map/ppermute | solution.py:716
  84.3 32.6 %copy-start.9 = (bf16[48,1024]{1,0:T(8,128)(2,1)}, bf16[48,1024]{1,0:T(8,128)(2,1)S(1)}, u32[]{:S(2)}) copy-start(bf16[48,1024]{1,0:T(8,128)(2,1)S(1)} %dynamic-slice_bitcast_fusion.4.a_ref) | copy-start | bytes 294916
  84.3 34.8 %copy-start.20 = (f32[64,128]{1,0:T(8,128)S(1)}, f32[64,128]{1,0:T(8,128)}, u32[]{:S(2)}) copy-start(f32[64,128]{1,0:T(8,128)} %constant.213.clone) | copy-start | bytes 98308
  84.3 34.8 %copy-start.21 = (f32[64,128]{1,0:T(8,128)S(1)}, f32[64,128]{1,0:T(8,128)}, u32[]{:S(2)}) copy-start(f32[64,128]{1,0:T(8,128)} %constant.214.clone) | copy-start | bytes 98308
  84.3 34.7 %copy-start.23 = (f32[48,128]{1,0:T(8,128)S(1)}, f32[48,128]{1,0:T(8,128)}, u32[]{:S(2)}) copy-start(f32[48,128]{1,0:T(8,128)} %constant.211.clone) | copy-start | bytes 73732
  84.4 34.7 %copy-start.24 = (f32[48,128]{1,0:T(8,128)S(1)}, f32[48,128]{1,0:T(8,128)}, u32[]{:S(2)}) copy-start(f32[48,128]{1,0:T(8,128)} %constant.212.clone) | copy-start | bytes 73732
  85.1 33.3 %copy-start.6 = (bf16[1024,48]{1,0:T(8,128)(2,1)}, bf16[1024,48]{1,0:T(8,128)(2,1)S(1)}, u32[]{:S(2)}) copy-start(bf16[1024,48]{1,0:T(8,128)(2,1)S(1)} %convolution_convert_fusion.l_ref) | copy-start | bytes 294916
  114.2 9.3 %collective-permute-start.5 = (bf16[768,256]{1,0:T(8,128)(2,1)S(1)}, bf16[768,256]{1,0:T(8,128)(2,1)S(1)}, u32[]{:S(2)}, u32[]{:S(2)}) collective-permute-start(bf16[768,256]{1,0:T(8,128)(2,1)S(1)} %slice.145), channel_id=1, source_target_pairs={{0,16},{8,24},{16,0},{24,8},{1,17},{9,25},{17,1},{25,9},{2,18},{10... | collective-permute-start | bytes 1179656 | tf_op jit(solution)/shard_map/ppermute | solution.py:722
  116.9 9.0 %collective-permute-start.6 = (bf16[768,256]{1,0:T(8,128)(2,1)S(1)}, bf16[768,256]{1,0:T(8,128)(2,1)S(1)}, u32[]{:S(2)}, u32[]{:S(2)}) collective-permute-start(bf16[768,256]{1,0:T(8,128)(2,1)S(1)} %slice.146), channel_id=1, source_target_pairs={{0,8},{8,0},{16,24},{24,16},{1,9},{9,1},{17,25},{25,17},{2,10},{10... | collective-permute-start | bytes 1179656 | tf_op jit(solution)/shard_map/ppermute | solution.py:723
  126.0 3.7 copy-start.11
  126.0 3.6 copy-start.19
  126.0 3.6 copy-start.22
  126.0 3.6 copy-start.27
  129.0 11.8 %collective-permute-start.7 = (bf16[4,3,512,256]{3,2,1,0:T(8,128)(2,1)}, bf16[4,3,512,256]{3,2,1,0:T(8,128)(2,1)}, u32[]{:S(2)}, u32[]{:S(2)}) collective-permute-start(bf16[4,3,512,256]{3,2,1,0:T(8,128)(2,1)} %pad_maximum_fusion.near_ref), channel_id=1, source_target_pairs={{0,4},{4,0},{1,5},{5,1},{2,6},{6,2},{3,7},{7,3},{8,12},{12,8},{9,1... | collective-permute-start | bytes 9437192 | tf_op jit(solution)/shard_map/ppermute | solution.py:728
  130.6 2.1 copy-start.4
  132.7 1.5 copy-start.25
  132.7 1.5 copy-start.26
  238.5 169.9 %all-gather.9.cloned.1.call-start = ((), (), s32[]{:S(2)}) async-start(), calls=%async_computation.2 | async-start | bytes 4423680 | tf_op jit(solution)/shard_map/all_gather | solution.py:999
  290.0 8.7 %copy-start.13 = (bf16[4,48,1024]{2,1,0:T(8,128)(2,1)S(1)}, bf16[4,48,1024]{2,1,0:T(8,128)(2,1)}, u32[]{:S(2)}) copy-start(bf16[4,48,1024]{2,1,0:T(8,128)(2,1)} %get-tuple-element.103) | copy-start | bytes 1179652
  290.0 8.7 %copy-start.17 = (bf16[80,1024]{1,0:T(8,128)(2,1)S(1)}, bf16[80,1024]{1,0:T(8,128)(2,1)}, u32[]{:S(2)}) copy-start(bf16[80,1024]{1,0:T(8,128)(2,1)} %get-tuple-element.102) | copy-start | bytes 491524
  298.6 50.5 %collective-permute-start.8 = (bf16[512,1024]{1,0:T(8,128)(2,1)}, bf16[512,1024]{1,0:T(8,128)(2,1)S(1)}, u32[]{:S(2)}, u32[]{:S(2)}) collective-permute-start(bf16[512,1024]{1,0:T(8,128)(2,1)} %get-tuple-element.98), channel_id=1, source_target_pairs={{0,1},{1,0},{2,3},{3,2},{4,5},{5,4},{6,7},{7,6},{8,9},{9,8},{10,11... | collective-permute-start | bytes 3145736 | tf_op jit(solution)/shard_map/ppermute | solution.py:972
  299.6 51.7 %collective-permute-start.9 = (bf16[128,1024]{1,0:T(8,128)(2,1)}, bf16[128,1024]{1,0:T(8,128)(2,1)S(1)}, u32[]{:S(2)}, u32[]{:S(2)}) collective-permute-start(bf16[128,1024]{1,0:T(8,128)(2,1)} %get-tuple-element.155), channel_id=1, source_target_pairs={{0,1},{1,2},{2,3},{3,0},{4,5},{5,6},{6,7},{7,4},{8,9},{9,10},{10,1... | collective-permute-start | bytes 786440 | tf_op jit(solution)/shard_map/ppermute | solution.py:822
  301.6 53.5 %collective-permute-start.10 = (bf16[128,1024]{1,0:T(8,128)(2,1)S(1)}, bf16[128,1024]{1,0:T(8,128)(2,1)S(1)}, u32[]{:S(2)}, u32[]{:S(2)}) collective-permute-start(bf16[128,1024]{1,0:T(8,128)(2,1)S(1)} %get-tuple-element.156), channel_id=1, source_target_pairs={{0,2},{1,3},{2,0},{3,1},{4,6},{5,7},{6,4},{7,5},{8,10},{9,11},{10,... | collective-permute-start | bytes 786440 | tf_op jit(solution)/shard_map/ppermute | solution.py:822
  302.8 52.2 %collective-permute-start.11 = (bf16[128,1024]{1,0:T(8,128)(2,1)S(1)}, bf16[128,1024]{1,0:T(8,128)(2,1)}, u32[]{:S(2)}, u32[]{:S(2)}) collective-permute-start(bf16[128,1024]{1,0:T(8,128)(2,1)S(1)} %get-tuple-element.157), channel_id=1, source_target_pairs={{0,3},{1,0},{2,1},{3,2},{4,7},{5,4},{6,5},{7,6},{8,11},{9,8},{10,9... | collective-permute-start | bytes 786440 | tf_op jit(solution)/shard_map/ppermute | solution.py:822
  349.1 2.0 copy-start.16
  351.1 32.4 %copy-start.5 = (bf16[512,1024]{1,0:T(8,128)(2,1)}, bf16[512,1024]{1,0:T(8,128)(2,1)S(1)}, u32[]{:S(2)}) copy-start(bf16[512,1024]{1,0:T(8,128)(2,1)S(1)} %add_convert_fusion.refs_0_) | copy-start | bytes 3145732
  351.1 10.1 %collective-permute-start.12 = (bf16[96,1024]{1,0:T(8,128)(2,1)S(1)}, bf16[96,1024]{1,0:T(8,128)(2,1)S(1)}, u32[]{:S(2)}, u32[]{:S(2)}) collective-permute-start(bf16[96,1024]{1,0:T(8,128)(2,1)S(1)} %copy-done.16), channel_id=1, source_target_pairs={{0,1},{1,2},{2,3},{3,0},{4,5},{5,6},{6,7},{7,4},{8,9},{9,10},{10,1... | collective-permute-start | bytes 589832 | tf_op jit(solution)/shard_map/ppermute | solution.py:822
  351.2 17.2 %collective-permute-start.13 = (bf16[96,1024]{1,0:T(8,128)(2,1)S(1)}, bf16[96,1024]{1,0:T(8,128)(2,1)S(1)}, u32[]{:S(2)}, u32[]{:S(2)}) collective-permute-start(bf16[96,1024]{1,0:T(8,128)(2,1)S(1)} %copy-done.16), channel_id=1, source_target_pairs={{0,2},{1,3},{2,0},{3,1},{4,6},{5,7},{6,4},{7,5},{8,10},{9,11},{10,... | collective-permute-start | bytes 589832 | tf_op jit(solution)/shard_map/ppermute | solution.py:822
  351.3 17.1 %collective-permute-start.14 = (bf16[96,1024]{1,0:T(8,128)(2,1)S(1)}, bf16[96,1024]{1,0:T(8,128)(2,1)S(1)}, u32[]{:S(2)}, u32[]{:S(2)}) collective-permute-start(bf16[96,1024]{1,0:T(8,128)(2,1)S(1)} %copy-done.16), channel_id=1, source_target_pairs={{0,3},{1,0},{2,1},{3,2},{4,7},{5,4},{6,5},{7,6},{8,11},{9,8},{10,9... | collective-permute-start | bytes 589832 | tf_op jit(solution)/shard_map/ppermute | solution.py:822
  370.0 46.2 %collective-permute-start.17 = (bf16[512,1024]{1,0:T(8,128)(2,1)S(1)}, bf16[512,1024]{1,0:T(8,128)(2,1)S(1)}, u32[]{:S(2)}, u32[]{:S(2)}) collective-permute-start(bf16[512,1024]{1,0:T(8,128)(2,1)S(1)} %add_convert_fusion.refs_0_), channel_id=1, source_target_pairs={{0,3},{1,0},{2,1},{3,2},{4,7},{5,4},{6,5},{7,6},{8,11},{9,8},{10,9... | collective-permute-start | bytes 3145736 | tf_op jit(solution)/shard_map/ppermute | solution.py:712
  375.7 89.1 %collective-permute-start.16 = (bf16[512,1024]{1,0:T(8,128)(2,1)S(1)}, bf16[512,1024]{1,0:T(8,128)(2,1)S(1)}, u32[]{:S(2)}, u32[]{:S(2)}) collective-permute-start(bf16[512,1024]{1,0:T(8,128)(2,1)S(1)} %add_convert_fusion.refs_0_), channel_id=1, source_target_pairs={{0,2},{1,3},{2,0},{3,1},{4,6},{5,7},{6,4},{7,5},{8,10},{9,11},{10,... | collective-permute-start | bytes 3145736 | tf_op jit(solution)/shard_map/ppermute | solution.py:712
  376.3 89.7 %collective-permute-start.15 = (bf16[512,1024]{1,0:T(8,128)(2,1)S(1)}, bf16[512,1024]{1,0:T(8,128)(2,1)}, u32[]{:S(2)}, u32[]{:S(2)}) collective-permute-start(bf16[512,1024]{1,0:T(8,128)(2,1)S(1)} %add_convert_fusion.refs_0_), channel_id=1, source_target_pairs={{0,1},{1,2},{2,3},{3,0},{4,5},{5,6},{6,7},{7,4},{8,9},{9,10},{10,1... | collective-permute-start | bytes 3145736 | tf_op jit(solution)/shard_map/ppermute | solution.py:712
  416.2 48.7 %copy-start.7 = (bf16[512,1024]{1,0:T(8,128)(2,1)}, bf16[512,1024]{1,0:T(8,128)(2,1)S(1)}, u32[]{:S(2)}) copy-start(bf16[512,1024]{1,0:T(8,128)(2,1)S(1)} %collective-permute-done.17.refs_3_) | copy-start | bytes 3145732
  464.8 1.0 copy-start.8
  474.1 7.5 %copy-start.1 = (bf16[1024,1024]{1,0:T(8,128)(2,1)S(1)}, bf16[1024,1024]{1,0:T(8,128)(2,1)}, u32[]{:S(2)}) copy-start(bf16[1024,1024]{1,0:T(8,128)(2,1)} %param.34) | copy-start | bytes 6291460
Sparse Core Ops, SparseCore 0:
  10.9 200.7 all-gather.4
  238.6 88.8 all-gather.6
  369.5 38.8 all-gather.8

commit v3 on v2

--- a/solution.py
+++ b/solution.py
@@ -29,9 +29,11 @@
 
 
 def roll_rows(pieces, place, shift, count, dtype):
+    pieces, offsets = zip(*pieces)
     number = len(pieces)
     size, width = pieces[0].shape
-    length = number * size
+    group = lax.axis_size("tensor") if number > 1 else 1
+    length = group * size
     unit = LANES
     units = length // unit
     block = min(512, count)
@@ -48,8 +50,11 @@
             @pl.when(step == 0)
             def _():
                 for k in range(number):
-                    member = lax.rem(scalar_ref[2] + (number - k), number)
-                    rows_ref[pl.ds(pl.multiple_of(member * size, size), size)] = refs[k][...]
+                    member = scalar_ref[2] + offsets[k]
+
+                    @pl.when(jnp.logical_and(member >= 0, member < group))
+                    def _():
+                        rows_ref[pl.ds(pl.multiple_of(member * size, size), size)] = refs[k][...]
         else:
             rows_ref = refs[0]
         offset = scalar_ref[1]
@@ -310,8 +315,8 @@
     def kernel(block_ref, w_ref, f_ref, a_ref, l_ref, x_ref, *rest):
         g_refs = rest[:number]
         base_ref = rest[number] if based else None
-        before_ref = rest[number + based] if added else None
-        out_ref, part_ref, acc_ref, lat_ref, b_ref = rest[-5:]
+        before_refs = rest[number + based : number + based + 2] if added else None
+        out_ref, part_ref, b_ref, acc_ref, lat_ref = rest[-5:]
         step = pl.program_id(0)
 
         @pl.when(step == 0)
@@ -330,20 +335,22 @@
             parts.append(tn(l_ref[:, p * rank : (p + 1) * rank], g))
         acc_ref[...] = total
         lat_ref[...] += jnp.concatenate(lats, axis=1)
-        b_ref[step] = jnp.concatenate(parts, axis=0)
+        if added:
+            parts = parts[:1] + [
+                part + before_refs[1][step, j * rank : (j + 1) * rank]
+                for j, part in enumerate(parts[1:])
+            ]
+        b_ref[step] = jnp.concatenate(parts, axis=0).astype(b_ref.dtype)
 
         @pl.when(step == shards - 1)
         def _():
             lat = lat_ref[...].astype(BF16)
             final = acc_ref[...] + nn(lat, a_ref[first * rank :])
             out_ref[...] = final.astype(out_ref.dtype)
-            part = jnp.concatenate([b_ref[t] for t in range(shards)], axis=1)
-            part = jnp.concatenate([part, tn(lat, x_ref[...])], axis=0)
+            part = tn(lat, x_ref[...])
             if added:
-                other = before_ref[...]
                 none = jnp.zeros((rank, width), F32)
-                size = depth - rank
-                part = part + jnp.concatenate([none, other[:size], none, other[size:]], axis=0)
+                part = part + jnp.concatenate([none, before_refs[0][...]], axis=0)
             part_ref[...] = part.astype(part_ref.dtype)
 
     whole = lambda array: pl.BlockSpec(array.shape, lambda i, s: (0,) * array.ndim)
@@ -363,24 +370,28 @@
         operands.append(base)
         specs.append(fixed(count))
     if added:
-        operands.append(before)
-        specs.append(whole(before))
+        operands += list(before)
+        specs += [whole(array) for array in before]
     return pl.pallas_call(
         kernel,
         grid_spec=pltpu.PrefetchScalarGridSpec(
             num_scalar_prefetch=1,
             grid=(shards,),
             in_specs=specs,
-            out_specs=[fixed(count), fixed(2 * depth)],
+            out_specs=[
+                fixed(count),
+                fixed(depth),
+                pl.BlockSpec((shards, depth, local), lambda i, s: (0, 0, 0)),
+            ],
             scratch_shapes=[
                 pltpu.VMEM((count, width), F32),
                 pltpu.VMEM((count, depth), F32),
-                pltpu.VMEM((shards, depth, local), F32),
             ],
         ),
         out_shape=[
             jax.ShapeDtypeStruct((count, width), F32 if based else BF16),
-            jax.ShapeDtypeStruct((2 * depth, width), BF16 if based else F32),
+            jax.ShapeDtypeStruct((depth, width), BF16 if based else F32),
+            jax.ShapeDtypeStruct((shards, depth, local), BF16 if based else F32),
         ],
         cost_estimate=pl.CostEstimate(
             flops=2 * number * count * width * width,
@@ -467,7 +478,7 @@
     count, width = hidden.shape
     shards, _, units = fb.shape
     rank = db.shape[0]
-    sub = min(512, units)
+    sub = min(1024, units)
     arrays, views, upper, lower = ffn_views(weights, width, sub)
     inner = units // sub
     steps = shards * inner
@@ -555,7 +566,7 @@
     count, width = grad.shape
     shards, _, units = fb.shape
     rank = ob.shape[0]
-    sub = min(512, units)
+    sub = min(1024, units)
     inner = units // sub
     steps = shards * inner
     arrays, views, upper, lower = ffn_views(weights, width, sub)
@@ -828,6 +839,67 @@
     for block in blocks[1:]:
         total = total + block.astype(F32)
     return total
+
+
+def line_gather(block):
+    shards = lax.axis_size("tensor")
+    blocks = [(block, 0)]
+    up = down = block
+    for step in range(1, shards):
+        links = [(i, i + 1) for i in range(step - 1, shards - 1)]
+        up = lax.ppermute(up, "tensor", links)
+        down = lax.ppermute(down, "tensor", [(shards - 1 - i, shards - 1 - j) for i, j in links])
+        blocks += [(up, -step), (down, step)]
+    return blocks
+
+
+def after(array, *marks):
+    return lax.optimization_barrier((array, *marks))[0]
+
+
+def place_sums(every, plan, adapters, place):
+    count, rows, width = every.shape
+    rows -= 16
+    owners = jnp.sum(
+        every[:, rows, :adapters].astype(jnp.int32) * jnp.arange(adapters, dtype=jnp.int32), axis=1
+    )
+    scalars = jnp.concatenate([jnp.reshape(place, (1,)), owners]).astype(jnp.int32)
+
+    def kernel(scalar_ref, every_ref, *refs):
+        outs, total_ref = refs[:-1], refs[-1]
+        adapter = pl.program_id(0)
+        total_ref[...] = jnp.zeros_like(total_ref)
+        for s in range(count):
+
+            @pl.when(scalar_ref[1 + s] == adapter)
+            def _():
+                total_ref[...] += every_ref[s, :rows].astype(F32)
+
+        for (first, size, columns), out in zip(plan, outs):
+            if columns is None:
+                out[0] = total_ref[first : first + size]
+            else:
+                start = pl.multiple_of(scalar_ref[0] * columns, LANES)
+                out[0] = total_ref[first : first + size, pl.ds(start, columns)]
+
+    shapes = [(adapters, size, width if columns is None else columns) for _, size, columns in plan]
+    return pl.pallas_call(
+        kernel,
+        grid_spec=pltpu.PrefetchScalarGridSpec(
+            num_scalar_prefetch=1,
+            grid=(adapters,),
+            in_specs=[pl.BlockSpec(every.shape, lambda i, s: (0, 0, 0))],
+            out_specs=[pl.BlockSpec((1,) + shape[1:], lambda i, s: (i, 0, 0)) for shape in shapes],
+            scratch_shapes=[pltpu.VMEM((rows, width), F32)],
+        ),
+        out_shape=[jax.ShapeDtypeStruct(shape, F32) for shape in shapes],
+        cost_estimate=pl.CostEstimate(
+            flops=count * rows * width,
+            bytes_accessed=(2 * count + 4 * adapters) * rows * width,
+            transcendentals=0,
+        ),
+        name="place_sums",
+    )(scalars, every)
 
 
 def after(array, *marks):
@@ -887,9 +959,9 @@
     start = jnp.sum(jnp.where(long, jnp.arange(length - half + 1, dtype=jnp.int32), 0))
     group_start = start + group * half
     own_start = start + place * count
-    x_group = roll_rows([layer_input], place, group_start, half, BF16)
+    x_group = roll_rows([(layer_input, 0)], place, group_start, half, BF16)
     x_own_b = window(x_group, member * count, count)
-    cotangent = roll_rows([output_grad], place, own_start, count, F32)
+    cotangent = roll_rows([(output_grad, 0)], place, own_start, count, F32)
     labels_twice = jnp.concatenate([labels, labels[:half]])
     labels_group = window(labels_twice, group_start, half)
     labels_own = window(labels_group, member * count, count)
@@ -960,10 +1032,10 @@
             query, keys, values, mixed, grad_mixed, logs, labels_own, labels_group, tables,
             tables_own, target, dq, False,
         )
-        sent, part_of = project_back(
+        sent, *part_of = project_back(
             [dk, dv], 1, qkv_all, qb, qa, latent_qkv, x_group, target, None, None
         )
-        before = part_of if before is None else before + part_of
+        before = part_of if before is None else [a + b for a, b in zip(before, part_of)]
         links = [
             (g * members + i, g * members + (i + d) % members)
             for g in range(2)
@@ -975,47 +1047,60 @@
         mine = lax.dynamic_index_in_dim(split, target, 0, keepdims=False)
         return jnp.concatenate([common, mine.reshape(-1, width)], axis=0)
 
+    def late_share(target):
+        mine = lax.dynamic_index_in_dim(qkv_b_part, target, 0, keepdims=False)
+        return jnp.concatenate([qkv_a_part, mine.reshape(-1, width)], axis=0)
+
     common = after(common, sent)
     early = send_grads(early_share)
     dq, dk, dv = attend_back(
         query, keys, values, mixed, grad_mixed, logs, labels_own, labels_group, tables, tables_own,
         member, dq, True,
     )
-    back, qkv_part = project_back(
+    back, qkv_a_part, qkv_b_part = project_back(
         [dq, dk, dv], 0, qkv_all, qb, qa, latent_qkv, x_group, member, grad_first, before
     )
-    for piece in received:
-        back = back + after(piece, back).astype(F32)
-    back = back.astype(BF16)
-    blocks = [back] + send_round(back)
-    qkv_part = after(qkv_part, back)
-    late = send_grads(lambda target: qkv_part)
+    late = send_grads(late_share)
 
     adapters = qkv_a.shape[0]
     hot = (adapter == jnp.arange(adapters, dtype=jnp.int32)).astype(BF16)
     flag = jnp.zeros((16, width), BF16).at[0, :adapters].set(hot)
-    early = [after(piece, back) for piece in early]
-    sums = jnp.concatenate([add_all(early).astype(BF16), add_all(late).astype(BF16), flag], axis=0)
-    every = lax.all_gather(sums, DP, axis=0)
-    placed = jnp.einsum(
-        "sj,srn->jrn", every[:, -16, :adapters], every[:, :-16], preferred_element_type=F32
-    )
-    own_columns = lambda rows: lax.dynamic_slice_in_dim(rows, place * local, local, 2)
-    mark = 5 * rank
-    down_b_grad = placed[:, :rank]
-    ffn_a_grad = placed[:, rank : 3 * rank]
-    out_b_grad = placed[:, 3 * rank : 4 * rank]
-    out_a_grad = own_columns(placed[:, 4 * rank : mark])
-    extent = 3 * rank * units // width
-    own_split = placed[:, mark : mark + extent].reshape(adapters, 3 * rank, units)
-    down_a_grad = own_split[:, :rank]
-    ffn_b_grad = own_split[:, rank:]
-    mark += extent
-    qkv_b_grad = own_columns(placed[:, mark : mark + 3 * rank])
-    qkv_a_grad = placed[:, mark + 3 * rank : mark + 6 * rank]
-
-    output = roll_rows([after(rolled, back)], place, -start, length, BF16)
-    blocks = [after(block, output, qkv_a_grad) for block in blocks]
+    early_sum = add_all([early[0]] + [after(piece, qkv_a_part) for piece in early[1:]]).astype(BF16)
+    early_every = lax.all_gather(jnp.concatenate([early_sum, flag], axis=0), DP, axis=0)
+    for piece in received:
+        back = back + after(piece, back, early_sum).astype(F32)
+    back = back.astype(BF16)
+    blocks = line_gather(back)
+    late_sum = add_all([late[0]] + [after(piece, back) for piece in late[1:]]).astype(BF16)
+    late_every = lax.all_gather(jnp.concatenate([late_sum, flag], axis=0), DP, axis=0)
+    plan = [
+        (0, rank, None),
+        (rank, 2 * rank, None),
+        (3 * rank, rank, None),
+        (4 * rank, rank, local),
+    ]
+    straight = units == width
+    if straight:
+        plan += [(5 * rank, rank, None), (6 * rank, 2 * rank, None)]
+    else:
+        plan += [(5 * rank, 3 * rank * units // width, None)]
+    early_grads = place_sums(early_every, plan, adapters, place)
+    down_b_grad, ffn_a_grad, out_b_grad, out_a_grad = early_grads[:4]
+    if straight:
+        down_a_grad, ffn_b_grad = early_grads[4:]
+    else:
+        own_split = early_grads[4].reshape(adapters, 3 * rank, units)
+        down_a_grad, ffn_b_grad = own_split[:, :rank], own_split[:, rank:]
+    qkv_a_grad, qkv_b_grad = place_sums(
+        late_every,
+        [(0, 3 * rank, None), (3 * rank, 3 * rank * local // width, None)],
+        adapters,
+        place,
+    )
+    qkv_b_grad = qkv_b_grad.reshape(adapters, 3 * rank, local)
+
+    output = roll_rows([(after(rolled, back), 0)], place, -start, length, BF16)
+    blocks = [(after(block, output, qkv_a_grad, out_b_grad), i) for block, i in blocks]
     grad_whole = roll_rows(blocks, place, -start, length, F32)
     return (
         output,

time: 498 us -> 524 us (1.052); the launches traced: 488 us -> 522 us
  waiting for transfers between devices: 195 us -> 217 us
  Pallas kernels: 185 us -> 194 us
  local copies, waits for them, and re-layouts: 45.1 us -> 38.8 us
  other arithmetic: 15.8 us -> 21.6 us
  starting transfers between devices: 27.2 us -> 32.8 us
    all_gather x1, waiting for transfers between devices: 0.01 us -> 75.7 us  [layer(): rolled = lax.all_gather(result, 'tensor', axis=0, tiled=True)]
    ppermute x6 -> x3, waiting for transfers between devices: 83 us -> 32.9 us  [send_round(): lax.ppermute(piece, 'tensor', cyclic(shards, k))]
    ppermute x0 -> x6, waiting for transfers between devices: none -> 44.6 us  [the longest x3 44.5 us: line_gather(): lax.ppermute(down, 'tensor', [(shards - 1 - i, shards - 1 - j) for i, j i...]
    all_gather x1 -> x2, waiting for transfers between devices: 24.9 us -> 0.02 us  [the longest x1 0.02 us: layer(): lax.all_gather(jnp.concatenate([late_sum, flag], axis=0), DP, axis=0)]
    ppermute x1, waiting for transfers between devices: 15.8 us -> 0.01 us  [layer(): received.append(lax.ppermute(sent, 'tensor', links))]
    ppermute x0 -> x6, starting transfers between devices: none -> 11.6 us  [the longest x3 7.71 us: line_gather(): up = lax.ppermute(up, 'tensor', links)]
    pallas_call x0 -> x2, Pallas kernels: none -> 11.5 us  [place_sums(): pl.pallas_call(kernel, grid_spec=pltpu.PrefetchScalarGridSpec(num_scalar_...]
    unnamed x67 -> x63, local copies, waits for them, and re-layouts: 16.3 us -> 6.05 us
  transfers between devices with their start and end apart: 21 -> 25, of which waited for: 11 -> 11; matrix products, arithmetic and copies ran while one was open for 10% -> 10% of each run, Pallas kernels for 31% -> 19%
where the time goes in v3:
time: 524 us; the launch traced here: 522 us
  waiting for transfers between devices  217 us (41%)
  Pallas kernels  194 us (37%)
  local copies, waits for them, and re-layouts  38.8 us (7%)
  starting transfers between devices  32.8 us (6%)
  other arithmetic  21.6 us (4%)
  between operations  16.9 us (3%)
    all_gather x1, waiting for transfers between devices, layer(): rolled = lax.all_gather(result, 'tensor', axis=0, tiled=True)  75.7 us
    ppermute x3, waiting for transfers between devices, line_gather(): lax.ppermute(down, 'tensor', [(shards - 1 - i, shards - 1 - j) for i, j i...  44.5 us
    pallas_call x2, Pallas kernels, attend_back(): pl.pallas_call(kernel, grid_spec=pltpu.PrefetchScalarGridSpec(num_scalar_...  34.9 us
    ppermute x3, waiting for transfers between devices, send_round(): lax.ppermute(piece, 'tensor', cyclic(shards, k))  32.9 us
    pallas_call x1, Pallas kernels, ffn_backward(): pl.pallas_call(kernel, grid=(shards, inner), in_specs=specs, out_specs=[f...  32.7 us
    ppermute x1, waiting for transfers between devices, spread_first(): lax.ppermute(stack, 'yx', flip(1))  27.3 us
    pallas_call x1, Pallas kernels, ffn_forward(): pl.pallas_call(kernel, grid=(shards, inner), in_specs=[full(hidden), full...  26.6 us
    all_gather x1, waiting for transfers between devices, gather_ffn(): whole = lax.all_gather(piece, ALL, axis=0, tiled=True)  24.4 us
  transfers between devices with their start and end apart: 25, of which 11 were waited for; matrix products, arithmetic and copies ran while one was open for 10% of the time, Pallas kernels for 19%

profile of v3, /device:TPU:0, one launch (start us, length us, event | category | flops | bytes accessed | tf_op | source)
XLA Modules:
  0.0 521.8 jit_solution(6637145561005238531)
XLA Ops:
  7.2 1.2 constant_dynamic-slice_fusion.5
  10.0 1.6 copy.49
  15.2 1.4 constant_dynamic-update-slice_fusion.3
  16.6 1.3 constant_dynamic-update-slice_fusion.2
  19.1 5.1 collective-permute-start.2
  24.2 1.0 collective-permute-start
  28.6 4.6 roll_rows.5.c_ref
  33.2 4.9 roll_rows.4.x_ref
  38.1 1.4 dynamic-slice_bitcast_fusion.7.b_ref.ob_ref
  39.4 1.5 dynamic-slice_bitcast_fusion.6.db_ref
  41.0 26.5 %collective-permute-done = bf16[768,256]{1,0:T(8,128)(2,1)} collective-permute-done((bf16[768,256]{1,0:T(8,128)(2,1)}, bf16[768,256]{1,0:T(8,128)(2,1)}, u32[]{:S(2)}, u32[]{:S(2)}) %collective-permute-start) | collective-permute-done | bytes 393248 | tf_op jit(solution)/shard_map/ppermute | solution.py:723
  68.5 6.3 %collective-permute-done.1 = bf16[768,256]{1,0:T(8,128)(2,1)S(1)} collective-permute-done((bf16[768,256]{1,0:T(8,128)(2,1)}, bf16[768,256]{1,0:T(8,128)(2,1)S(1)}, u32[]{:S(2)}, u32[]{:S(2)}) %collective-permute-start.1) | collective-permute-done | bytes 393248 | tf_op jit(solution)/shard_map/ppermute | solution.py:723
  76.4 1.6 collective-permute-start.3
  77.9 1.5 collective-permute-start.4
  80.1 1.0 copy.53.all_ref
  81.2 1.5 dynamic-slice_bitcast_fusion.5.f_ref.fa_ref
  85.9 27.3 %collective-permute-done.3 = bf16[1536,256]{1,0:T(8,128)(2,1)} collective-permute-done((bf16[1536,256]{1,0:T(8,128)(2,1)S(1)}, bf16[1536,256]{1,0:T(8,128)(2,1)}, u32[]{:S(2)}, u32[]{:S(2)}) %collective-permute-start.3) | collective-permute-done | bytes 786464 | tf_op jit(solution)/shard_map/ppermute | solution.py:727
  113.2 1.0 slice.110
  114.2 1.6 collective-permute-start.5
  115.8 1.1 slice.111
  116.9 1.5 collective-permute-start.6
  119.5 4.0 collective-permute-done.5
  123.6 2.3 collective-permute-done.6
  126.0 3.0 pad_maximum_fusion.near_ref
  132.3 1.0 constant_dynamic-slice_fusion.17.o_ref.x_ref
  133.3 1.5 pad_maximum_fusion.1.own_ref
  136.0 1.0 slice_bitcast_fusion
  137.0 1.0 slice_bitcast_fusion.1
  137.9 1.0 slice_bitcast_fusion.2
  142.0 8.4 %shard_map.294 = (bf16[4,3,1024,256]{3,2,1,0:T(8,128)(2,1)}, bf16[1024,1024]{1,0:T(8,128)(2,1)}) custom-call(s32[3]{0:T(128)} %pad_add_fusion.scalar_ref, bf16[8,512,256]{2,1,0:T(8,128)(2,1)} %pad_maximum_fusion.1.own_ref, bf16[4,3,512,256]{3,2,1,0:T(8,128)(2,1)} %pad_maximum_fusion.near_ref, bf16[4,3,512,256]{3,2,1,0:T(8,128)(2,1)} %collective-permute-done.7.far_ref), custom_call_target="tpu_custom_call" | custom-call | bytes 16777216 | tf_op jit(solution)/shard_map/pallas_call | solution.py:773
  150.5 12.0 %project_qkv.1 = (bf16[512,1024]{1,0:T(8,128)(2,1)}, bf16[1024,1024]{1,0:T(8,128)(2,1)}, bf16[1024,1024]{1,0:T(8,128)(2,1)}) custom-call(bf16[1024,1024]{1,0:T(8,128)(2,1)} %roll_rows.4.x_ref, bf16[512,1024]{1,0:T(8,128)(2,1)} %constant_dynamic-slice_fusion.17.o_ref.x_ref, bf16[4,3,1024,256]{3,2,1,0:T(8,128)(2,1)} %get-tuple-element.83.w_ref, ...), custom_call_target="tpu_custom_call" | custom-call | flops 5368709120 | bytes 20971520 | tf_op jit(solution)/shard_map/project_qkv/pallas_call | solution.py:127
  162.5 17.9 %attend.1 = (bf16[512,1024]{1,0:T(8,128)(2,1)}, f32[8,8,512]{2,1,0:T(8,128)}) custom-call(bf16[512,1024]{1,0:T(8,128)(2,1)} %get-tuple-element.84.q_ref, bf16[1024,1024]{1,0:T(8,128)(2,1)} %get-tuple-element.85.k_ref, bf16[1024,1024]{1,0:T(8,128)(2,1)} %get-tuple-element.86.v_ref, s32[1,512]{1,0:T(1,128)} %bitcast.114, s32[1024,1]{1,0:T(8,128)} %copy.53.all_ref), custom_call_target="tpu_custom_call" | custom-call | flops 8589934592 | bytes 6291456 | tf_op jit(solution)/shard_map/attend/pallas_call | solution.py:191
  180.4 6.8 %out_forward.1 = (f32[512,1024]{1,0:T(8,128)}, bf16[512,1024]{1,0:T(8,128)(2,1)}, f32[512,1024]{1,0:T(8,128)}, f32[512,1]{1,0:T(8,128)}, bf16[512,16]{1,0:T(8,128)(2,1)}, /*index=5*/bf16[512,32]{1,0:T(8,128)(2,1)}) custom-call(bf16[512,1024]{1,0:T(8,128)(2,1)} %get-tuple-element.87.m_ref, bf16[1024,1024]{1,0:T(8,128)(2,1)} %get-tuple-element.88.w_ref.wo_ref, ...), custom_call_target="tpu_custom_call" | custom-call | flops 1073741824 | bytes 9437184 | tf_op jit(solution)/shard_map/out_forward/pallas_call | solution.py:426
  187.2 24.4 %all-gather.8.cloned.1.call-done = bf16[12288,1024]{1,0:T(8,128)(2,1)} async-done(((bf16[384,1024]{1,0:T(8,128)(2,1)}), bf16[12288,1024]{1,0:T(8,128)(2,1)}) %all-gather.8.cloned.1.call-update) | async-done | bytes 25165840 | tf_op jit(solution)/shard_map/all_gather | solution.py:709
  211.6 26.6 %ffn_forward.1 = (bf16[2,512,4096]{2,1,0:T(8,128)(2,1)}, bf16[512,1024]{1,0:T(8,128)(2,1)}, f32[512,1024]{1,0:T(8,128)}, bf16[512,1024]{1,0:T(8,128)(2,1)}, bf16...) custom-call(f32[512,1024]{1,0:T(8,128)} %get-tuple-element.89.h_ref, bf16[512,1024]{1,0:T(8,128)(2,1)} %get-tuple-element.90.hb_ref, ...), custom_call_target="tpu_custom_call" | custom-call | flops 12884901888 | bytes 33554432 | tf_op jit(solution)/shard_map/ffn_forward/pallas_call | solution.py:521
  238.2 32.7 %ffn_backward.1 = (f32[512,1024]{1,0:T(8,128)}, bf16[512,1024]{1,0:T(8,128)(2,1)}, bf16[4,48,1024]{2,1,0:T(8,128)(2,1)}, bf16[80,1024]{1,0:T(8,128)(2,1)}) custom-call(bf16[512,1024]{1,0:T(8,128)(2,1)} %get-tuple-element.93.gb_ref, f32[512,1024]{1,0:T(8,128)} %get-tuple-element.94.g_ref, bf16[2,512,4096]{2,1,0:T(8,128)(2,1)} %get-tuple-element.95.pre_ref, ...), custom_call_target="tpu_custom_call" | custom-call | flops 12884901888 | bytes 33554432 | tf_op jit(solution)/shard_map/ffn_backward/pallas_call | solution.py:633
  270.9 16.6 %attend_back.2 = (f32[512,1024]{1,0:T(8,128)}, bf16[512,1024]{1,0:T(8,128)(2,1)}, bf16[512,1024]{1,0:T(8,128)(2,1)}) custom-call(s32[1]{0:T(128)} %bitcast.41.block_ref, bf16[512,1024]{1,0:T(8,128)(2,1)} %get-tuple-element.84.q_ref, bf16[1024,1024]{1,0:T(8,128)(2,1)} %get-tuple-element.85.k_ref, bf16[1024,1024]{1,0:T(8,128)(2,1)} %get-tuple-element.86.v_ref, ...), custom_call_target="tpu_custom_call" | custom-call | flops 10737418240 | bytes 9437184 | tf_op jit(solution)/shard_map/attend_back/pallas_call | solution.py:287
  287.6 8.6 %project_back.2 = (bf16[512,1024]{1,0:T(8,128)(2,1)}, f32[32,1024]{1,0:T(8,128)}, f32[4,32,256]{2,1,0:T(8,128)}) custom-call(s32[1]{0:T(128)} %bitcast.41.block_ref, bf16[4,3,1024,256]{3,2,1,0:T(8,128)(2,1)} %get-tuple-element.83.w_ref, bf16[48,1024]{1,0:T(8,128)(2,1)} %bitcast.103, bf16[48,1024]{1,0:T(8,128)(2,1)} %copy-done.12, ...), custom_call_target="tpu_custom_call" | custom-call | flops 2147483648 | bytes 12582912 | tf_op jit(solution)/shard_map/project_back/pallas_call | solution.py:375
  297.2 2.0 collective-permute-start.9
  299.2 1.5 collective-permute-start.10
  300.7 1.4 collective-permute-start.11
  302.0 18.2 %attend_back.3 = (bf16[512,1024]{1,0:T(8,128)(2,1)}, bf16[512,1024]{1,0:T(8,128)(2,1)}, bf16[512,1024]{1,0:T(8,128)(2,1)}) custom-call(s32[1]{0:T(128)} %bitcast.40.block_ref, bf16[512,1024]{1,0:T(8,128)(2,1)} %get-tuple-element.84.q_ref, bf16[1024,1024]{1,0:T(8,128)(2,1)} %get-tuple-element.85.k_ref, bf16[1024,1024]{1,0:T(8,128)(2,1)} %get-tuple-element.86.v_ref, ...), custom_call_target="tpu_custom_call" | custom-call | flops 10737418240 | bytes 9437184 | tf_op jit(solution)/shard_map/attend_back/pallas_call | solution.py:287
  320.3 10.7 %project_back.3 = (f32[512,1024]{1,0:T(8,128)}, bf16[48,1024]{1,0:T(8,128)(2,1)}, bf16[4,48,256]{2,1,0:T(8,128)(2,1)}) custom-call(s32[1]{0:T(128)} %bitcast.40.block_ref, bf16[4,3,1024,256]{3,2,1,0:T(8,128)(2,1)} %get-tuple-element.83.w_ref, bf16[48,1024]{1,0:T(8,128)(2,1)} %bitcast.104, bf16[48,1024]{1,0:T(8,128)(2,1)} %copy-done.12, ...), custom_call_target="tpu_custom_call" | custom-call | flops 3221225472 | bytes 13631488 | tf_op jit(solution)/shard_map/project_back/pallas_call | solution.py:375
  331.0 1.6 constant_dynamic-slice_fusion.3
  333.4 1.7 pad_maximum_fusion.14
  336.5 1.5 collective-permute-start.13
  338.0 1.8 collective-permute-start.14
  340.5 1.1 add_convert_fusion.1
  341.7 1.6 add_convert_fusion.refs_0_
  343.6 4.4 collective-permute-done.13
  348.1 1.0 add_convert_fusion.2
  351.1 1.3 collective-permute-start.16
  352.4 5.3 %collective-permute-start.15 = (bf16[512,1024]{1,0:T(8,128)(2,1)S(1)}, bf16[512,1024]{1,0:T(8,128)(2,1)S(1)}, u32[]{:S(2)}, u32[]{:S(2)}) collective-permute-start(bf16[512,1024]{1,0:T(8,128)(2,1)S(1)} %add_convert_fusion.refs_0_), channel_id=1, source_target_pairs={{0,1},{1,2},{2,3},{4,5},{5,6},{6,7},{8,9},{9,10},{10,11},{12,13},{... | collective-permute-start | bytes 3145736 | tf_op jit(solution)/shard_map/ppermute | solution.py:850
  357.8 20.8 %collective-permute-done.16.refs_2_ = bf16[512,1024]{1,0:T(8,128)(2,1)S(1)} collective-permute-done((bf16[512,1024]{1,0:T(8,128)(2,1)S(1)}, bf16[512,1024]{1,0:T(8,128)(2,1)S(1)}, u32[]{:S(2)}, u32[]{:S(2)}) %collective-permute-start.16) | collective-permute-done | bytes 1048608 | tf_op jit(solution)/shard_map/ppermute | solution.py:851
  378.5 1.3 collective-permute-start.18
  380.6 23.8 %collective-permute-done.18.refs_4_ = bf16[512,1024]{1,0:T(8,128)(2,1)S(1)} collective-permute-done((bf16[512,1024]{1,0:T(8,128)(2,1)S(1)}, bf16[512,1024]{1,0:T(8,128)(2,1)S(1)}, u32[]{:S(2)}, u32[]{:S(2)}) %collective-permute-start.18) | collective-permute-done | bytes 1048608 | tf_op jit(solution)/shard_map/ppermute | solution.py:851
  404.4 1.3 collective-permute-start.20
  405.7 1.7 collective-permute-start.19
  410.8 5.3 %place_sums.2 = (f32[8,48,1024]{2,1,0:T(8,128)}, f32[8,12,1024]{2,1,0:T(8,128)}) custom-call(s32[9]{0:T(128)} %pad_add_fusion.1.scalar_ref, bf16[8,76,1024]{2,1,0:T(8,128)(2,1)} %all-gather.14.cloned.1.call-done.every_ref), custom_call_target="tpu_custom_call" | custom-call | flops 491520 | bytes 2949120 | tf_op jit(solution)/shard_map/place_sums/pallas_call | solution.py:886
  416.1 1.9 reshape.178
  418.6 6.1 %place_sums.3 = (f32[8,16,1024]{2,1,0:T(8,128)}, f32[8,32,1024]{2,1,0:T(8,128)}, f32[8,16,1024]{2,1,0:T(8,128)}, f32[8,16,256]{2,1,0:T(8,128)}, f32[8,16,1024]{2,1,0:T(8,128)}, /*index=5*/f32[8,32,1024]{2,1,0:T(8,128)}) custom-call(s32[9]{0:T(128)} %pad_add_fusion.2.scalar_ref, bf16[8,144,1024]{2,1,0:T(8,128)(2,1)} %bitcast.100), custom_call_target="tpu_custom_call" | custom-call | flops 1048576 | bytes 6291456 | tf_op jit(solution)/shard_map/place_sums/pallas_call | solution.py:886
  424.8 75.7 %all-gather.10.cloned.1.call-done.refs_0_ = bf16[2048,1024]{1,0:T(8,128)(2,1)} async-done(((bf16[512,1024]{1,0:T(8,128)(2,1)}), bf16[2048,1024]{1,0:T(8,128)(2,1)}) %all-gather.10.cloned.1.call-update) | async-done | bytes 4194320 | tf_op jit(solution)/shard_map/all_gather | solution.py:1019
  500.5 6.2 %roll_rows.6 = bf16[2048,1024]{1,0:T(8,128)(2,1)} custom-call(s32[3]{0:T(128)} %add_add_fusion.scalar_ref, bf16[2048,1024]{1,0:T(8,128)(2,1)} %all-gather.10.cloned.1.call-done.refs_0_), custom_call_target="tpu_custom_call" | custom-call | flops 1073741824 | bytes 12582912 | tf_op jit(solution)/shard_map/roll_rows/pallas_call | solution.py:71
  506.7 8.5 %roll_rows.7 = f32[2048,1024]{1,0:T(8,128)} custom-call(s32[3]{0:T(128)} %add_add_fusion.scalar_ref, bf16[512,1024]{1,0:T(8,128)(2,1)} %copy-done.5, bf16[512,1024]{1,0:T(8,128)(2,1)} %copy-done.9, bf16[512,1024]{1,0:T(8,128)(2,1)} %copy-done.8, bf16[512,1024]{1,0:T(8,128)(2,1)} %copy-done.11, bf16[512,1024]{1,0:T(8,128)(2,1)} %copy-done.10, ...), custom_call_target="tpu_custom_call" | custom-call | flops 1073741824 | bytes 12582912 | tf_op jit(solution)/shard_map/roll_rows/pallas_call | solution.py:71
  (151 shorter events, 33.5 us)
Async XLA Ops:
  7.2 1.8 copy-start
  7.2 204.4 %all-gather.8.cloned.1.call-start = ((), (), s32[]{:S(2)}) async-start(), calls=%async_computation | async-start | bytes 25952256 | tf_op jit(solution)/shard_map/all_gather | solution.py:709
  9.9 1.6 copy-start.15
  9.9 398.0 %all-gather.14.cloned.1.call-start = ((), (), s32[]{:S(2)}) async-start(), calls=%async_computation.3 | async-start | bytes 1474560 | tf_op jit(solution)/shard_map/all_gather | solution.py:1075
  11.5 3.7 copy-start.3
  11.9 13.3 %copy-start.22 = (s32[1,2048]{1,0:T(1,128)S(1)}, s32[1,2048]{1,0:T(1,128)}, u32[]{:S(2)}) copy-start(s32[1,2048]{1,0:T(1,128)} %param.27) | copy-start | bytes 24580
  13.6 19.6 %copy-start.14 = (bf16[128,256]{1,0:T(8,128)(2,1)}, bf16[128,256]{1,0:T(8,128)(2,1)S(1)}, u32[]{:S(2)}) copy-start(bf16[128,256]{1,0:T(8,128)(2,1)S(1)} %reshape.164) | copy-start | bytes 196612
  14.5 18.7 %copy-start.20 = (bf16[64,256]{1,0:T(8,128)(2,1)}, bf16[64,256]{1,0:T(8,128)(2,1)S(1)}, u32[]{:S(2)}) copy-start(bf16[64,256]{1,0:T(8,128)(2,1)S(1)} %reshape.165) | copy-start | bytes 98308
  19.1 55.7 %collective-permute-start.2 = (bf16[768,256]{1,0:T(8,128)(2,1)}, bf16[768,256]{1,0:T(8,128)(2,1)S(1)}, u32[]{:S(2)}, u32[]{:S(2)}) collective-permute-start(bf16[768,256]{1,0:T(8,128)(2,1)} %constant_dynamic-update-slice_fusion), channel_id=1, source_target_pairs={{0,3},{1,0},{2,1},{3,2},{4,7},{5,4},{6,5},{7,6},{8,11},{9,8},{10,9... | collective-permute-start | bytes 1179656 | tf_op jit(solution)/shard_map/ppermute | solution.py:723
  24.2 50.6 %collective-permute-start.1 = (bf16[768,256]{1,0:T(8,128)(2,1)}, bf16[768,256]{1,0:T(8,128)(2,1)S(1)}, u32[]{:S(2)}, u32[]{:S(2)}) collective-permute-start(bf16[768,256]{1,0:T(8,128)(2,1)} %constant_dynamic-update-slice_fusion), channel_id=1, source_target_pairs={{0,2},{1,3},{2,0},{3,1},{4,6},{5,7},{6,4},{7,5},{8,10},{9,11},{10,... | collective-permute-start | bytes 1179656 | tf_op jit(solution)/shard_map/ppermute | solution.py:723
  24.2 43.3 %collective-permute-start = (bf16[768,256]{1,0:T(8,128)(2,1)}, bf16[768,256]{1,0:T(8,128)(2,1)}, u32[]{:S(2)}, u32[]{:S(2)}) collective-permute-start(bf16[768,256]{1,0:T(8,128)(2,1)} %constant_dynamic-update-slice_fusion), channel_id=1, source_target_pairs={{0,1},{1,2},{2,3},{3,0},{4,5},{5,6},{6,7},{7,4},{8,9},{9,10},{10,1... | collective-permute-start | bytes 1179656 | tf_op jit(solution)/shard_map/ppermute | solution.py:723
  39.4 44.1 %copy-start.2 = (bf16[1024,1024]{1,0:T(8,128)(2,1)S(1)}, bf16[1024,1024]{1,0:T(8,128)(2,1)}, u32[]{:S(2)}) copy-start(bf16[1024,1024]{1,0:T(8,128)(2,1)} %roll_rows.4.x_ref) | copy-start | bytes 6291460
  74.8 0.7 copy-start.19
  75.6 0.7 copy-start.18
  76.4 36.8 %collective-permute-start.3 = (bf16[1536,256]{1,0:T(8,128)(2,1)S(1)}, bf16[1536,256]{1,0:T(8,128)(2,1)}, u32[]{:S(2)}, u32[]{:S(2)}) collective-permute-start(bf16[1536,256]{1,0:T(8,128)(2,1)S(1)} %pad_maximum_fusion.2), channel_id=1, source_target_pairs={{0,8},{8,0},{16,24},{24,16},{1,9},{9,1},{17,25},{25,17},{2,10},{10... | collective-permute-start | bytes 2359304 | tf_op jit(solution)/shard_map/ppermute | solution.py:727
  77.9 37.9 %collective-permute-start.4 = (bf16[1536,256]{1,0:T(8,128)(2,1)S(1)}, bf16[1536,256]{1,0:T(8,128)(2,1)}, u32[]{:S(2)}, u32[]{:S(2)}) collective-permute-start(bf16[1536,256]{1,0:T(8,128)(2,1)S(1)} %pad_maximum_fusion.2), channel_id=1, source_target_pairs={{0,16},{8,24},{16,0},{24,8},{1,17},{9,25},{17,1},{25,9},{2,18},{10... | collective-permute-start | bytes 2359304 | tf_op jit(solution)/shard_map/ppermute | solution.py:727
  83.5 33.3 %copy-start.12 = (bf16[48,1024]{1,0:T(8,128)(2,1)}, bf16[48,1024]{1,0:T(8,128)(2,1)S(1)}, u32[]{:S(2)}) copy-start(bf16[48,1024]{1,0:T(8,128)(2,1)S(1)} %dynamic-slice_bitcast_fusion.4.a_ref) | copy-start | bytes 294916
  83.5 35.5 %copy-start.23 = (f32[64,128]{1,0:T(8,128)S(1)}, f32[64,128]{1,0:T(8,128)}, u32[]{:S(2)}) copy-start(f32[64,128]{1,0:T(8,128)} %constant.223.clone) | copy-start | bytes 98308
  83.6 35.5 %copy-start.24 = (f32[64,128]{1,0:T(8,128)S(1)}, f32[64,128]{1,0:T(8,128)}, u32[]{:S(2)}) copy-start(f32[64,128]{1,0:T(8,128)} %constant.224.clone) | copy-start | bytes 98308
  83.6 35.5 %copy-start.25 = (f32[48,128]{1,0:T(8,128)S(1)}, f32[48,128]{1,0:T(8,128)}, u32[]{:S(2)}) copy-start(f32[48,128]{1,0:T(8,128)} %constant.221.clone) | copy-start | bytes 73732
  83.6 35.5 %copy-start.26 = (f32[48,128]{1,0:T(8,128)S(1)}, f32[48,128]{1,0:T(8,128)}, u32[]{:S(2)}) copy-start(f32[48,128]{1,0:T(8,128)} %constant.222.clone) | copy-start | bytes 73732
  84.3 34.1 %copy-start.7 = (bf16[1024,48]{1,0:T(8,128)(2,1)}, bf16[1024,48]{1,0:T(8,128)(2,1)S(1)}, u32[]{:S(2)}) copy-start(bf16[1024,48]{1,0:T(8,128)(2,1)S(1)} %convolution_convert_fusion.l_ref) | copy-start | bytes 294916
  114.2 9.3 %collective-permute-start.5 = (bf16[768,256]{1,0:T(8,128)(2,1)S(1)}, bf16[768,256]{1,0:T(8,128)(2,1)S(1)}, u32[]{:S(2)}, u32[]{:S(2)}) collective-permute-start(bf16[768,256]{1,0:T(8,128)(2,1)S(1)} %slice.110), channel_id=1, source_target_pairs={{0,16},{8,24},{16,0},{24,8},{1,17},{9,25},{17,1},{25,9},{2,18},{10... | collective-permute-start | bytes 1179656 | tf_op jit(solution)/shard_map/ppermute | solution.py:733
  116.9 9.0 %collective-permute-start.6 = (bf16[768,256]{1,0:T(8,128)(2,1)S(1)}, bf16[768,256]{1,0:T(8,128)(2,1)S(1)}, u32[]{:S(2)}, u32[]{:S(2)}) collective-permute-start(bf16[768,256]{1,0:T(8,128)(2,1)S(1)} %slice.111), channel_id=1, source_target_pairs={{0,8},{8,0},{16,24},{24,16},{1,9},{9,1},{17,25},{25,17},{2,10},{10... | collective-permute-start | bytes 1179656 | tf_op jit(solution)/shard_map/ppermute | solution.py:734
  126.0 3.0 copy-start.29
  129.0 13.1 %collective-permute-start.7 = (bf16[4,3,512,256]{3,2,1,0:T(8,128)(2,1)}, bf16[4,3,512,256]{3,2,1,0:T(8,128)(2,1)}, u32[]{:S(2)}, u32[]{:S(2)}) collective-permute-start(bf16[4,3,512,256]{3,2,1,0:T(8,128)(2,1)} %pad_maximum_fusion.near_ref), channel_id=1, source_target_pairs={{0,4},{4,0},{1,5},{5,1},{2,6},{6,2},{3,7},{7,3},{8,12},{12,8},{9,1... | collective-permute-start | bytes 9437192 | tf_op jit(solution)/shard_map/ppermute | solution.py:739
  130.6 2.7 copy-start.4
  133.3 1.5 copy-start.27
  133.3 2.1 copy-start.28
  287.6 8.7 %copy-start.17 = (bf16[4,48,1024]{2,1,0:T(8,128)(2,1)S(1)}, bf16[4,48,1024]{2,1,0:T(8,128)(2,1)}, u32[]{:S(2)}) copy-start(bf16[4,48,1024]{2,1,0:T(8,128)(2,1)} %get-tuple-element.116) | copy-start | bytes 1179652
  287.6 8.7 %copy-start.13 = (bf16[80,1024]{1,0:T(8,128)(2,1)S(1)}, bf16[80,1024]{1,0:T(8,128)(2,1)}, u32[]{:S(2)}) copy-start(bf16[80,1024]{1,0:T(8,128)(2,1)} %get-tuple-element.115) | copy-start | bytes 491524
  296.2 45.4 %collective-permute-start.8 = (bf16[512,1024]{1,0:T(8,128)(2,1)}, bf16[512,1024]{1,0:T(8,128)(2,1)}, u32[]{:S(2)}, u32[]{:S(2)}) collective-permute-start(bf16[512,1024]{1,0:T(8,128)(2,1)} %get-tuple-element.113), channel_id=1, source_target_pairs={{0,1},{1,0},{2,3},{3,2},{4,5},{5,4},{6,7},{7,6},{8,9},{9,8},{10,11... | collective-permute-start | bytes 3145736 | tf_op jit(solution)/shard_map/ppermute | solution.py:1044
  297.2 39.3 %collective-permute-start.9 = (bf16[128,1024]{1,0:T(8,128)(2,1)}, bf16[128,1024]{1,0:T(8,128)(2,1)S(1)}, u32[]{:S(2)}, u32[]{:S(2)}) collective-permute-start(bf16[128,1024]{1,0:T(8,128)(2,1)} %get-tuple-element.154), channel_id=1, source_target_pairs={{0,1},{1,2},{2,3},{3,0},{4,5},{5,6},{6,7},{7,4},{8,9},{9,10},{10,1... | collective-permute-start | bytes 786440 | tf_op jit(solution)/shard_map/ppermute | solution.py:833
  299.2 38.8 %collective-permute-start.10 = (bf16[128,1024]{1,0:T(8,128)(2,1)}, bf16[128,1024]{1,0:T(8,128)(2,1)S(1)}, u32[]{:S(2)}, u32[]{:S(2)}) collective-permute-start(bf16[128,1024]{1,0:T(8,128)(2,1)} %get-tuple-element.155), channel_id=1, source_target_pairs={{0,2},{1,3},{2,0},{3,1},{4,6},{5,7},{6,4},{7,5},{8,10},{9,11},{10,... | collective-permute-start | bytes 786440 | tf_op jit(solution)/shard_map/ppermute | solution.py:833
  300.7 39.1 %collective-permute-start.11 = (bf16[128,1024]{1,0:T(8,128)(2,1)S(1)}, bf16[128,1024]{1,0:T(8,128)(2,1)S(1)}, u32[]{:S(2)}, u32[]{:S(2)}) collective-permute-start(bf16[128,1024]{1,0:T(8,128)(2,1)S(1)} %get-tuple-element.156), channel_id=1, source_target_pairs={{0,3},{1,0},{2,1},{3,2},{4,7},{5,4},{6,5},{7,6},{8,11},{9,8},{10,9... | collective-permute-start | bytes 786440 | tf_op jit(solution)/shard_map/ppermute | solution.py:833
  331.0 10.7 %copy-start.6 = (f32[512,1024]{1,0:T(8,128)S(1)}, f32[512,1024]{1,0:T(8,128)}, u32[]{:S(2)}) copy-start(f32[512,1024]{1,0:T(8,128)} %get-tuple-element.112) | copy-start | bytes 6291460
  335.1 8.6 %collective-permute-start.12 = (bf16[60,1024]{1,0:T(8,128)(2,1)}, bf16[60,1024]{1,0:T(8,128)(2,1)}, u32[]{:S(2)}, u32[]{:S(2)}) collective-permute-start(bf16[60,1024]{1,0:T(8,128)(2,1)} %get-tuple-element.163), channel_id=1, source_target_pairs={{0,1},{1,2},{2,3},{3,0},{4,5},{5,6},{6,7},{7,4},{8,9},{9,10},{10,1... | collective-permute-start | bytes 368648 | tf_op jit(solution)/shard_map/ppermute | solution.py:833
  336.5 11.6 %collective-permute-start.13 = (bf16[60,1024]{1,0:T(8,128)(2,1)}, bf16[60,1024]{1,0:T(8,128)(2,1)S(1)}, u32[]{:S(2)}, u32[]{:S(2)}) collective-permute-start(bf16[60,1024]{1,0:T(8,128)(2,1)} %get-tuple-element.164), channel_id=1, source_target_pairs={{0,2},{1,3},{2,0},{3,1},{4,6},{5,7},{6,4},{7,5},{8,10},{9,11},{10,... | collective-permute-start | bytes 368648 | tf_op jit(solution)/shard_map/ppermute | solution.py:833
  338.0 10.1 %collective-permute-start.14 = (bf16[60,1024]{1,0:T(8,128)(2,1)}, bf16[60,1024]{1,0:T(8,128)(2,1)S(1)}, u32[]{:S(2)}, u32[]{:S(2)}) collective-permute-start(bf16[60,1024]{1,0:T(8,128)(2,1)} %get-tuple-element.165), channel_id=1, source_target_pairs={{0,3},{1,0},{2,1},{3,2},{4,7},{5,4},{6,5},{7,6},{8,11},{9,8},{10,9... | collective-permute-start | bytes 368648 | tf_op jit(solution)/shard_map/ppermute | solution.py:833
  339.8 0.7 copy-start.21
  341.7 6.4 %copy-start.16 = (bf16[48,1024]{1,0:T(8,128)(2,1)S(1)}, bf16[48,1024]{1,0:T(8,128)(2,1)}, u32[]{:S(2)}) copy-start(bf16[48,1024]{1,0:T(8,128)(2,1)} %get-tuple-element.117) | copy-start | bytes 294916
  343.3 72.8 %copy-start.5 = (bf16[512,1024]{1,0:T(8,128)(2,1)}, bf16[512,1024]{1,0:T(8,128)(2,1)S(1)}, u32[]{:S(2)}) copy-start(bf16[512,1024]{1,0:T(8,128)(2,1)S(1)} %add_convert_fusion.refs_0_) | copy-start | bytes 3145732
  349.8 58.9 %all-gather.12.cloned.1.call-start = ((), (), s32[]{:S(2)}) async-start(), calls=%async_computation.2 | async-start | bytes 2654208 | tf_op jit(solution)/shard_map/all_gather | solution.py:1069
  350.6 150.0 %all-gather.10.cloned.1.call-start = ((), (), s32[]{:S(2)}) async-start(), calls=%async_computation.1 | async-start | bytes 5242880 | tf_op jit(solution)/shard_map/all_gather | solution.py:1019
  351.1 27.4 %collective-permute-start.16 = (bf16[512,1024]{1,0:T(8,128)(2,1)S(1)}, bf16[512,1024]{1,0:T(8,128)(2,1)S(1)}, u32[]{:S(2)}, u32[]{:S(2)}) collective-permute-start(bf16[512,1024]{1,0:T(8,128)(2,1)S(1)} %add_convert_fusion.refs_0_), channel_id=1, source_target_pairs={{3,2},{2,1},{1,0},{7,6},{6,5},{5,4},{11,10},{10,9},{9,8},{15,14},{... | collective-permute-start | bytes 3145736 | tf_op jit(solution)/shard_map/ppermute | solution.py:851
  352.4 27.4 %collective-permute-start.15 = (bf16[512,1024]{1,0:T(8,128)(2,1)S(1)}, bf16[512,1024]{1,0:T(8,128)(2,1)S(1)}, u32[]{:S(2)}, u32[]{:S(2)}) collective-permute-start(bf16[512,1024]{1,0:T(8,128)(2,1)S(1)} %add_convert_fusion.refs_0_), channel_id=1, source_target_pairs={{0,1},{1,2},{2,3},{4,5},{5,6},{6,7},{8,9},{9,10},{10,11},{12,13},{... | collective-permute-start | bytes 3145736 | tf_op jit(solution)/shard_map/ppermute | solution.py:850
  378.5 1.3 copy-start.8
  378.5 25.8 %collective-permute-start.18 = (bf16[512,1024]{1,0:T(8,128)(2,1)S(1)}, bf16[512,1024]{1,0:T(8,128)(2,1)S(1)}, u32[]{:S(2)}, u32[]{:S(2)}) collective-permute-start(bf16[512,1024]{1,0:T(8,128)(2,1)S(1)} %collective-permute-done.16.refs_2_), channel_id=1, source_target_pairs={{2,1},{1,0},{6,5},{5,4},{10,9},{9,8},{14,13},{13,12},{18,17},{17,1... | collective-permute-start | bytes 3145736 | tf_op jit(solution)/shard_map/ppermute | solution.py:851
  379.8 24.5 %copy-start.9 = (bf16[512,1024]{1,0:T(8,128)(2,1)}, bf16[512,1024]{1,0:T(8,128)(2,1)S(1)}, u32[]{:S(2)}) copy-start(bf16[512,1024]{1,0:T(8,128)(2,1)S(1)} %collective-permute-done.15.refs_1_) | copy-start | bytes 3145732
  379.9 25.8 %collective-permute-start.17 = (bf16[512,1024]{1,0:T(8,128)(2,1)S(1)}, bf16[512,1024]{1,0:T(8,128)(2,1)S(1)}, u32[]{:S(2)}, u32[]{:S(2)}) collective-permute-start(bf16[512,1024]{1,0:T(8,128)(2,1)S(1)} %collective-permute-done.15.refs_1_), channel_id=1, source_target_pairs={{1,2},{2,3},{5,6},{6,7},{9,10},{10,11},{13,14},{14,15},{17,18},{18... | collective-permute-start | bytes 3145736 | tf_op jit(solution)/shard_map/ppermute | solution.py:850
  404.4 20.4 %copy-start.10 = (bf16[512,1024]{1,0:T(8,128)(2,1)}, bf16[512,1024]{1,0:T(8,128)(2,1)S(1)}, u32[]{:S(2)}) copy-start(bf16[512,1024]{1,0:T(8,128)(2,1)S(1)} %collective-permute-done.18.refs_4_) | copy-start | bytes 3145732
  404.4 102.4 %collective-permute-start.20 = (bf16[512,1024]{1,0:T(8,128)(2,1)S(1)}, bf16[512,1024]{1,0:T(8,128)(2,1)}, u32[]{:S(2)}, u32[]{:S(2)}) collective-permute-start(bf16[512,1024]{1,0:T(8,128)(2,1)S(1)} %collective-permute-done.18.refs_4_), channel_id=1, source_target_pairs={{1,0},{5,4},{9,8},{13,12},{17,16},{21,20},{25,24},{29,28}} | collective-permute-start | bytes 3145736 | tf_op jit(solution)/shard_map/ppermute | solution.py:851
  405.7 19.1 %copy-start.11 = (bf16[512,1024]{1,0:T(8,128)(2,1)}, bf16[512,1024]{1,0:T(8,128)(2,1)S(1)}, u32[]{:S(2)}) copy-start(bf16[512,1024]{1,0:T(8,128)(2,1)S(1)} %collective-permute-done.17.refs_3_) | copy-start | bytes 3145732
  405.7 101.1 %collective-permute-start.19 = (bf16[512,1024]{1,0:T(8,128)(2,1)S(1)}, bf16[512,1024]{1,0:T(8,128)(2,1)}, u32[]{:S(2)}, u32[]{:S(2)}) collective-permute-start(bf16[512,1024]{1,0:T(8,128)(2,1)S(1)} %collective-permute-done.17.refs_3_), channel_id=1, source_target_pairs={{2,3},{6,7},{10,11},{14,15},{18,19},{22,23},{26,27},{30,31}} | collective-permute-start | bytes 3145736 | tf_op jit(solution)/shard_map/ppermute | solution.py:850
  506.7 8.5 %copy-start.1 = (bf16[1024,1024]{1,0:T(8,128)(2,1)S(1)}, bf16[1024,1024]{1,0:T(8,128)(2,1)}, u32[]{:S(2)}) copy-start(bf16[1024,1024]{1,0:T(8,128)(2,1)} %param.34) | copy-start | bytes 6291460
Sparse Core Ops, SparseCore 0:
  10.9 200.7 all-gather.7
  349.9 24.9 all-gather.13
  377.4 28.8 all-gather.11
  407.7 92.7 all-gather.9

commit v4 on v3

--- a/solution.py
+++ b/solution.py
@@ -36,7 +36,7 @@
     length = group * size
     unit = LANES
     units = length // unit
-    block = min(512, count)
+    block = min(1024, count)
     shift = lax.rem(shift + length, length)
     first = shift // unit
     scalars = jnp.stack([first, shift - first * unit, place]).astype(jnp.int32)
@@ -454,136 +454,191 @@
     )(*operands)
 
 
-def ffn_views(weights, width, sub):
-    if len(weights) == 1:
-        (packed,) = weights
-        _, parts, rows, units = packed.shape
-        low = units // parts
+class Whole:
+    def __init__(self, upper, lower):
+        self.operands = [upper, lower]
+        self.shards, _, self.width, self.units = upper.shape
+        self.sub = min(512, self.units)
+        self.inner = self.units // self.sub
+        self.pick = lambda t, s: t
+        width, sub = self.width, self.sub
+        self.specs = [
+            pl.BlockSpec((1, 2, width, sub), lambda t, b, s: (t, 0, 0, b)),
+            pl.BlockSpec((1, sub, width), lambda t, b, s: (t, b, 0)),
+        ]
+
+    def up(self, refs, rows, i):
+        return nn(rows, refs[0][0, i])
+
+    def up_back(self, refs, grads, i):
+        return nt(grads, refs[0][0, i])
+
+    def down(self, refs):
+        return refs[1][0]
+
+
+class Gathered:
+    def __init__(self, packed, skip):
+        self.operands = [packed, packed]
+        shards, self.parts, rows, self.units = packed.shape
+        self.shards = shards - skip
+        self.width = self.units
+        self.sub = self.units // 2
+        self.inner = 2
+        width, sub = self.width, self.sub
+        low = self.units // self.parts
         high = rows - low
-        specs = [
-            pl.BlockSpec((1, parts, high, sub), lambda t, b: (t, 0, 0, b)),
-            pl.BlockSpec((1, sub // low, low, width), lambda t, b: (t, b, high // low, 0)),
+        self.pick = lambda t, s: lax.rem(s[0] + skip + t, shards)
+        self.specs = [
+            pl.BlockSpec((1, self.parts, high, sub), lambda t, b, s: (self.pick(t, s), 0, 0, b)),
+            pl.BlockSpec((1, sub // low, low, width), lambda t, b, s: (self.pick(t, s), b, high // low, 0)),
         ]
-        upper = lambda ref, i: ref[0, i * parts // 2 : (i + 1) * parts // 2].reshape(width, sub)
-        lower = lambda ref: ref[0].reshape(sub, width)
-        return [packed, packed], specs, upper, lower
-    specs = [
-        pl.BlockSpec((1, 2, width, sub), lambda t, b: (t, 0, 0, b)),
-        pl.BlockSpec((1, sub, width), lambda t, b: (t, b, 0)),
-    ]
-    return list(weights), specs, lambda ref, i: ref[0, i], lambda ref: ref[0]
-
-
-def ffn_forward(hidden, hidden_b, latent, weights, fb, da, db, gain, shift, cotangent):
-    count, width = hidden.shape
-    shards, _, units = fb.shape
-    rank = db.shape[0]
-    sub = min(1024, units)
-    arrays, views, upper, lower = ffn_views(weights, width, sub)
-    inner = units // sub
+
+    def gate_up(self, refs, i):
+        half = self.parts // 2
+        return refs[0][0, i * half : (i + 1) * half].reshape(self.width, self.sub)
+
+    def up(self, refs, rows, i):
+        return nn(rows, self.gate_up(refs, i))
+
+    def up_back(self, refs, grads, i):
+        return nt(grads, self.gate_up(refs, i))
+
+    def down(self, refs):
+        return refs[1][0].reshape(self.sub, self.width)
+
+
+def ffn_forward(weights, hidden_b, latent, fb, da, total, down, end, pre, first, number):
+    count, width = total.shape
+    shards, units = weights.shards, weights.units
+    rank = da.shape[1]
+    sub, inner = weights.sub, weights.inner
     steps = shards * inner
-
-    def kernel(h_ref, hb_ref, l_ref, w_ref, wd_ref, fb_ref, da_ref, db_ref, g_ref, s_ref, c_ref,
-               pre_ref, res_ref, mid_ref, midb_ref, ld_ref, ldg_ref, acc_ref, lat_ref):
+    scalars = jnp.reshape(lax.axis_index("tensor"), (1,)).astype(jnp.int32)
+
+    def kernel(place_ref, w0_ref, w1_ref, hb_ref, l_ref, fb_ref, da_ref, t_ref, d_ref, *rest):
+        refs = (w0_ref, w1_ref)
         step = pl.program_id(0) * inner + pl.program_id(1)
+        if pre is not None:
+            rest = rest[1:]
+        if end:
+            db_ref, g_ref, s_ref, c_ref = rest[:4]
+            pre_ref, res_ref, mid_ref, midb_ref, ld_ref, ldg_ref, acc_ref, lat_ref = rest[4:]
+        else:
+            pre_ref, acc_ref, lat_ref = rest
 
         @pl.when(step == 0)
         def _():
-            acc_ref[...] = h_ref[...]
-            lat_ref[...] = jnp.zeros_like(lat_ref)
+            acc_ref[...] = t_ref[...]
+            lat_ref[...] = d_ref[...]
 
         h = hb_ref[...]
         lat = l_ref[...]
-        gate = nn(h, upper(w_ref, 0)) + nn(lat[:, :rank], fb_ref[0, :rank])
-        up = nn(h, upper(w_ref, 1)) + nn(lat[:, rank:], fb_ref[0, rank:])
+        factor = fb_ref[0]
+        gate = weights.up(refs, h, 0) + nn(lat[:, :rank], factor[:rank])
+        up = weights.up(refs, h, 1) + nn(lat[:, rank:], factor[rank:])
         pre_ref[0] = gate.astype(BF16)
         pre_ref[1] = up.astype(BF16)
         active = (gate * jax.nn.sigmoid(gate) * up).astype(BF16)
-        acc_ref[...] += nn(active, lower(wd_ref))
+        acc_ref[...] += nn(active, weights.down(refs))
         lat_ref[...] += nt(active, da_ref[0])
 
-        @pl.when(step == steps - 1)
-        def _():
-            latent_down = lat_ref[...].astype(BF16)
-            total = acc_ref[...] + nn(latent_down, db_ref[...])
-            result, normed, inverse = norm_forward(total, g_ref[...], s_ref[...])
-            res_ref[...] = result.astype(BF16)
-            grad = norm_backward(c_ref[...], normed, inverse, g_ref[...])
-            mid_ref[...] = grad
-            grad_b = grad.astype(BF16)
-            midb_ref[...] = grad_b
-            ld_ref[...] = latent_down
-            ldg_ref[...] = nt(grad_b, db_ref[...]).astype(BF16)
-
-    full = lambda array: pl.BlockSpec(array.shape, lambda t, b: (0,) * array.ndim)
-    fixed = lambda rows, size: pl.BlockSpec((rows, size), lambda t, b: (0, 0))
-    operands = [hidden, hidden_b, latent, *arrays, fb, da, db, gain, shift, cotangent]
-    return pl.pallas_call(
-        kernel,
-        grid=(shards, inner),
-        in_specs=[
-            full(hidden),
-            full(hidden_b),
-            full(latent),
-            *views,
-            pl.BlockSpec((1, 2 * rank, sub), lambda t, b: (t, 0, b)),
-            pl.BlockSpec((1, rank, sub), lambda t, b: (t, 0, b)),
-            full(db),
-            full(gain),
-            full(shift),
-            full(cotangent),
-        ],
-        out_specs=[
-            pl.BlockSpec((2, count, sub), lambda t, b: (0, 0, t * inner + b)),
-            fixed(count, width),
-            fixed(count, width),
-            fixed(count, width),
-            fixed(count, rank),
-            fixed(count, rank),
-        ],
-        out_shape=[
-            jax.ShapeDtypeStruct((2, count, shards * units), BF16),
+        if end:
+
+            @pl.when(step == steps - 1)
+            def _():
+                latent_down = lat_ref[...].astype(BF16)
+                sums = acc_ref[...] + nn(latent_down, db_ref[...])
+                result, normed, inverse = norm_forward(sums, g_ref[...], s_ref[...])
+                res_ref[...] = result.astype(BF16)
+                grad = norm_backward(c_ref[...], normed, inverse, g_ref[...])
+                mid_ref[...] = grad
+                grad_b = grad.astype(BF16)
+                midb_ref[...] = grad_b
+                ld_ref[...] = latent_down
+                ldg_ref[...] = nt(grad_b, db_ref[...]).astype(BF16)
+
+    full = lambda array: pl.BlockSpec(array.shape, lambda t, b, s: (0,) * array.ndim)
+    fixed = lambda size: pl.BlockSpec((count, size), lambda t, b, s: (0, 0))
+    operands = [*weights.operands, hidden_b, latent, fb, da, total, down]
+    specs = [
+        *weights.specs,
+        full(hidden_b),
+        full(latent),
+        pl.BlockSpec((1, 2 * rank, sub), lambda t, b, s: (weights.pick(t, s), 0, b)),
+        pl.BlockSpec((1, rank, sub), lambda t, b, s: (weights.pick(t, s), 0, b)),
+        full(total),
+        full(down),
+    ]
+    out_specs = [pl.BlockSpec((2, count, sub), lambda t, b, s: (0, 0, (first + t) * inner + b))]
+    out_shape = [jax.ShapeDtypeStruct((2, count, number * units), BF16)]
+    scratch = []
+    aliases = {}
+    if pre is not None:
+        aliases = {len(operands) + 1: 0}
+        operands.append(pre)
+        specs.append(pl.BlockSpec(memory_space=pl.ANY))
+    if end:
+        operands += list(end)
+        specs += [full(array) for array in end]
+        out_specs += [fixed(width)] * 3 + [fixed(rank)] * 2
+        out_shape += [
             jax.ShapeDtypeStruct((count, width), BF16),
             jax.ShapeDtypeStruct((count, width), F32),
             jax.ShapeDtypeStruct((count, width), BF16),
             jax.ShapeDtypeStruct((count, rank), BF16),
             jax.ShapeDtypeStruct((count, rank), BF16),
-        ],
-        scratch_shapes=[pltpu.VMEM((count, width), F32), pltpu.VMEM((count, rank), F32)],
+        ]
+        scratch = [pltpu.VMEM((count, width), F32), pltpu.VMEM((count, rank), F32)]
+    else:
+        out_specs += [fixed(width), fixed(rank)]
+        out_shape += [
+            jax.ShapeDtypeStruct((count, width), F32),
+            jax.ShapeDtypeStruct((count, rank), F32),
+        ]
+    return pl.pallas_call(
+        kernel,
+        grid_spec=pltpu.PrefetchScalarGridSpec(
+            num_scalar_prefetch=1,
+            grid=(shards, inner),
+            in_specs=specs,
+            out_specs=out_specs,
+            scratch_shapes=scratch,
+        ),
+        out_shape=out_shape,
+        input_output_aliases=aliases,
         cost_estimate=pl.CostEstimate(
             flops=6 * count * width * shards * units,
             bytes_accessed=6 * width * shards * units + 4 * count * shards * units,
             transcendentals=count * shards * units,
         ),
         name="ffn_forward",
-    )(*operands)
-
-
-def ffn_backward(
-    grad_b, grad, pre, latent_down, latent_down_grad, latent_ffn, weights, fb, da, fa, hidden_b,
-    normed, inverse, gain, latent_out, ob, oa, mixed, out_all,
-):
-    count, width = grad.shape
-    shards, _, units = fb.shape
-    rank = ob.shape[0]
-    sub = min(1024, units)
-    inner = units // sub
+    )(scalars, *operands)
+
+
+def ffn_backward(weights, grad_b, pre, latent_down_grad, latent_ffn, fb, da, total, end):
+    count, width = total.shape
+    shards, units = weights.shards, weights.units
+    rank = da.shape[1]
+    sub, inner = weights.sub, weights.inner
     steps = shards * inner
-    arrays, views, upper, lower = ffn_views(weights, width, sub)
-
-    def kernel(gb_ref, g_ref, pre_ref, ld_ref, ldg_ref, lf_ref, w_ref, wd_ref, fb_ref, da_ref, fa_ref,
-               hb_ref, n_ref, i_ref, gain_ref, lo_ref, ob_ref, oa_ref, m_ref, wo_ref,
-               first_ref, mixed_ref, split_ref, common_ref, acc_ref, lat_ref):
+    scalars = jnp.reshape(lax.axis_index("tensor"), (1,)).astype(jnp.int32)
+
+    def kernel(place_ref, w0_ref, w1_ref, gb_ref, pre_ref, ldg_ref, lf_ref, fb_ref, da_ref, t_ref, *rest):
+        refs = (w0_ref, w1_ref)
         step = pl.program_id(0) * inner + pl.program_id(1)
+        ld_ref, fa_ref, hb_ref, n_ref, i_ref, gain_ref, lo_ref, ob_ref, oa_ref, m_ref, wo_ref = rest[:11]
+        split_ref, first_ref, mixed_ref, common_ref, acc_ref, lat_ref = rest[11:]
 
         @pl.when(step == 0)
         def _():
-            acc_ref[...] = g_ref[...]
+            acc_ref[...] = t_ref[...]
             lat_ref[...] = jnp.zeros_like(lat_ref)
 
         ldg = ldg_ref[...]
         lf = lf_ref[...]
-        grad_active = nt(gb_ref[...], lower(wd_ref)) + nn(ldg, da_ref[0])
+        factor = fb_ref[0]
+        grad_active = nt(gb_ref[...], weights.down(refs)) + nn(ldg, da_ref[0])
         gate = pre_ref[0].astype(F32)
         up = pre_ref[1].astype(F32)
         sigma = jax.nn.sigmoid(gate)
@@ -591,19 +646,20 @@
         active = (swish * up).astype(BF16)
         grad_gate = (grad_active * up * (sigma + swish * (1.0 - sigma))).astype(BF16)
         grad_up = (grad_active * swish).astype(BF16)
-        split_ref[0] = jnp.concatenate(
+        split = jnp.concatenate(
             [tn(ldg, active), tn(lf[:, :rank], grad_gate), tn(lf[:, rank:], grad_up)], axis=0
-        ).astype(BF16)
-        acc_ref[...] += nt(grad_gate, upper(w_ref, 0)) + nt(grad_up, upper(w_ref, 1))
+        )
+        split_ref[0] = split.astype(BF16)
+        acc_ref[...] += weights.up_back(refs, grad_gate, 0) + weights.up_back(refs, grad_up, 1)
         lat_ref[...] += jnp.concatenate(
-            [nt(grad_gate, fb_ref[0, :rank]), nt(grad_up, fb_ref[0, rank:])], axis=1
+            [nt(grad_gate, factor[:rank]), nt(grad_up, factor[rank:])], axis=1
         )
 
         @pl.when(step == steps - 1)
         def _():
             lat = lat_ref[...].astype(BF16)
-            total = acc_ref[...] + nn(lat, fa_ref[...])
-            first = norm_backward(total, n_ref[...], i_ref[...], gain_ref[...])
+            sums = acc_ref[...] + nn(lat, fa_ref[...])
+            first = norm_backward(sums, n_ref[...], i_ref[...], gain_ref[...])
             first_ref[...] = first
             branch = first.astype(BF16)
             log = nt(branch, ob_ref[...]).astype(BF16)
@@ -618,42 +674,46 @@
             ).astype(BF16)
             mixed_ref[...] = (nt(branch, wo_ref[...]) + nn(log, oa_ref[...])).astype(BF16)
 
-    full = lambda array: pl.BlockSpec(array.shape, lambda t, b: (0,) * array.ndim)
-    fixed = lambda rows, size: pl.BlockSpec((rows, size), lambda t, b: (0, 0))
-    head = [grad_b, grad, pre, latent_down, latent_down_grad, latent_ffn]
-    rest = [fa, hidden_b, normed, inverse, gain, latent_out, ob, oa, mixed, out_all]
-    specs = [full(array) for array in head]
-    specs[2] = pl.BlockSpec((2, count, sub), lambda t, b: (0, 0, t * inner + b))
-    specs += views
-    specs += [
-        pl.BlockSpec((1, 2 * rank, sub), lambda t, b: (t, 0, b)),
-        pl.BlockSpec((1, rank, sub), lambda t, b: (t, 0, b)),
+    full = lambda array: pl.BlockSpec(array.shape, lambda t, b, s: (0,) * array.ndim)
+    fixed = lambda rows, size: pl.BlockSpec((rows, size), lambda t, b, s: (0, 0))
+    operands = [*weights.operands, grad_b, pre, latent_down_grad, latent_ffn, fb, da, total, *end]
+    specs = [
+        *weights.specs,
+        full(grad_b),
+        pl.BlockSpec((2, count, sub), lambda t, b, s: (0, 0, t * inner + b)),
+        full(latent_down_grad),
+        full(latent_ffn),
+        pl.BlockSpec((1, 2 * rank, sub), lambda t, b, s: (weights.pick(t, s), 0, b)),
+        pl.BlockSpec((1, rank, sub), lambda t, b, s: (weights.pick(t, s), 0, b)),
+        full(total),
+        *[full(array) for array in end],
     ]
-    specs += [full(array) for array in rest]
+    out_specs = [pl.BlockSpec((1, 3 * rank, sub), lambda t, b, s: (t, 0, b))]
+    out_shape = [jax.ShapeDtypeStruct((shards, 3 * rank, units), BF16)]
+    out_specs += [fixed(count, width), fixed(count, width), fixed(5 * rank, width)]
+    out_shape += [
+        jax.ShapeDtypeStruct((count, width), F32),
+        jax.ShapeDtypeStruct((count, width), BF16),
+        jax.ShapeDtypeStruct((5 * rank, width), BF16),
+    ]
+    scratch = [pltpu.VMEM((count, width), F32), pltpu.VMEM((count, 2 * rank), F32)]
     return pl.pallas_call(
         kernel,
-        grid=(shards, inner),
-        in_specs=specs,
-        out_specs=[
-            fixed(count, width),
-            fixed(count, width),
-            pl.BlockSpec((1, 3 * rank, sub), lambda t, b: (t, 0, b)),
-            fixed(5 * rank, width),
-        ],
-        out_shape=[
-            jax.ShapeDtypeStruct((count, width), F32),
-            jax.ShapeDtypeStruct((count, width), BF16),
-            jax.ShapeDtypeStruct((shards, 3 * rank, units), BF16),
-            jax.ShapeDtypeStruct((5 * rank, width), BF16),
-        ],
-        scratch_shapes=[pltpu.VMEM((count, width), F32), pltpu.VMEM((count, 2 * rank), F32)],
+        grid_spec=pltpu.PrefetchScalarGridSpec(
+            num_scalar_prefetch=1,
+            grid=(shards, inner),
+            in_specs=specs,
+            out_specs=out_specs,
+            scratch_shapes=scratch,
+        ),
+        out_shape=out_shape,
         cost_estimate=pl.CostEstimate(
             flops=6 * count * width * shards * units,
             bytes_accessed=6 * width * shards * units + 4 * count * shards * units,
             transcendentals=count * shards * units,
         ),
         name="ffn_backward",
-    )(*head, *arrays, fb, da, *rest)
+    )(scalars, *operands)
 
 
 def norm_forward(rows, gain, shift):
@@ -1013,14 +1073,29 @@
         mixed, out_all, oa, ob, x_own_b, ln_gain[:1], ln_bias[:1], fa
     )
 
+    zero = jnp.zeros((count, rank), F32)
+    end = (db, ln_gain[1:], ln_bias[1:], cotangent)
+    packed = len(ffn_all) == 1
+    if packed:
+        mine = lambda stack: lax.dynamic_slice_in_dim(stack, place, 1, 0)
+        own = Whole(w_gate_up[None], w_down[None])
+        pre, total, down = ffn_forward(
+            own, hidden_b, latent_ffn, mine(fb), mine(da), hidden, zero, None, None, 0, shards
+        )
+        others, every = Gathered(ffn_all[0], 1), Gathered(ffn_all[0], 0)
+    else:
+        pre, total, down = None, hidden, zero
+        others = every = Whole(*ffn_all)
     pre, result, grad_mid, grad_ffn, latent_down, latent_down_grad = ffn_forward(
-        hidden, hidden_b, latent_ffn, ffn_all, fb, da, db, ln_gain[1:], ln_bias[1:], cotangent
+        others, hidden_b, latent_ffn, fb, da, total, down, end, pre, shards - others.shards, shards
     )
     rolled = lax.all_gather(result, "tensor", axis=0, tiled=True)
 
-    grad_first, grad_mixed, split, common = ffn_backward(
-        grad_ffn, grad_mid, pre, latent_down, latent_down_grad, latent_ffn, ffn_all, fb, da, fa,
-        hidden_b, normed, inverse, ln_gain[:1], latent_out, ob, oa, mixed, out_all,
+    end = (
+        latent_down, fa, hidden_b, normed, inverse, ln_gain[:1], latent_out, ob, oa, mixed, out_all,
+    )
+    split, grad_first, grad_mixed, common = ffn_backward(
+        every, grad_ffn, pre, latent_down_grad, latent_ffn, fb, da, grad_mid, end
     )
 
     dq = None
@@ -1044,7 +1119,8 @@
         received.append(lax.ppermute(sent, "tensor", links))
 
     def early_share(target):
-        mine = lax.dynamic_index_in_dim(split, target, 0, keepdims=False)
+        entry = lax.rem(target - place + shards, shards) if packed else target
+        mine = lax.dynamic_index_in_dim(split, entry, 0, keepdims=False)
         return jnp.concatenate([common, mine.reshape(-1, width)], axis=0)
 
     def late_share(target):
@@ -1065,14 +1141,14 @@
     adapters = qkv_a.shape[0]
     hot = (adapter == jnp.arange(adapters, dtype=jnp.int32)).astype(BF16)
     flag = jnp.zeros((16, width), BF16).at[0, :adapters].set(hot)
-    early_sum = add_all([early[0]] + [after(piece, qkv_a_part) for piece in early[1:]]).astype(BF16)
-    early_every = lax.all_gather(jnp.concatenate([early_sum, flag], axis=0), DP, axis=0)
     for piece in received:
-        back = back + after(piece, back, early_sum).astype(F32)
+        back = back + after(piece, back).astype(F32)
     back = back.astype(BF16)
     blocks = line_gather(back)
-    late_sum = add_all([late[0]] + [after(piece, back) for piece in late[1:]]).astype(BF16)
-    late_every = lax.all_gather(jnp.concatenate([late_sum, flag], axis=0), DP, axis=0)
+    output = roll_rows([(after(rolled, back), 0)], place, -start, length, BF16)
+    early_sum = add_all([early[0]] + [after(piece, output) for piece in early[1:]]).astype(BF16)
+    late_sum = add_all([late[0]] + [after(piece, output) for piece in late[1:]]).astype(BF16)
+    every_sum = lax.all_gather(jnp.concatenate([early_sum, late_sum, flag], axis=0), DP, axis=0)
     plan = [
         (0, rank, None),
         (rank, 2 * rank, None),
@@ -1084,22 +1160,21 @@
         plan += [(5 * rank, rank, None), (6 * rank, 2 * rank, None)]
     else:
         plan += [(5 * rank, 3 * rank * units // width, None)]
-    early_grads = place_sums(early_every, plan, adapters, place)
-    down_b_grad, ffn_a_grad, out_b_grad, out_a_grad = early_grads[:4]
+    mark = early_sum.shape[0]
+    plan += [
+        (mark, 3 * rank, None),
+        (mark + 3 * rank, 3 * rank * local // width, None),
+    ]
+    grads = place_sums(every_sum, plan, adapters, place)
+    down_b_grad, ffn_a_grad, out_b_grad, out_a_grad = grads[:4]
     if straight:
-        down_a_grad, ffn_b_grad = early_grads[4:]
+        down_a_grad, ffn_b_grad = grads[4:6]
     else:
-        own_split = early_grads[4].reshape(adapters, 3 * rank, units)
+        own_split = grads[4].reshape(adapters, 3 * rank, units)
         down_a_grad, ffn_b_grad = own_split[:, :rank], own_split[:, rank:]
-    qkv_a_grad, qkv_b_grad = place_sums(
-        late_every,
-        [(0, 3 * rank, None), (3 * rank, 3 * rank * local // width, None)],
-        adapters,
-        place,
-    )
+    qkv_a_grad, qkv_b_grad = grads[-2:]
     qkv_b_grad = qkv_b_grad.reshape(adapters, 3 * rank, local)
 
-    output = roll_rows([(after(rolled, back), 0)], place, -start, length, BF16)
     blocks = [(after(block, output, qkv_a_grad, out_b_grad), i) for block, i in blocks]
     grad_whole = roll_rows(blocks, place, -start, length, F32)
     return (

time: 524 us -> 459 us (0.88)
  waiting for transfers between devices: 217 us -> 157 us
    all_gather x1, waiting for transfers between devices: 75.7 us -> 0.02 us  [layer(): rolled = lax.all_gather(result, 'tensor', axis=0, tiled=True)]
    ppermute x3, waiting for transfers between devices: 44.5 us -> 59.9 us  [line_gather(): lax.ppermute(down, 'tensor', [(shards - 1 - i, shards - 1 - j) for i, j i...]
    all_gather x1, waiting for transfers between devices: 24.4 us -> 13.4 us  [gather_ffn(): whole = lax.all_gather(piece, ALL, axis=0, tiled=True)]
    ppermute x1, waiting for transfers between devices: 0.01 us -> 9.82 us  [layer(): received.append(lax.ppermute(sent, 'tensor', links))]
    pallas_call x2 -> x3, Pallas kernels: 59.3 us -> 67.2 us  [the longest x1 35.5 us: ffn_backward(): pl.pallas_call(kernel, grid_spec=pltpu.PrefetchScalarGridSpec(num_scalar_...]
    pallas_call x2 -> x1, Pallas kernels: 11.5 us -> 6.98 us  [place_sums(): pl.pallas_call(kernel, grid_spec=pltpu.PrefetchScalarGridSpec(num_scalar_...]
  transfers between devices with their start and end apart: 25 -> 24, of which waited for: 11 -> 12; matrix products, arithmetic and copies ran while one was open for 10% -> 11% of each run, Pallas kernels for 19% -> 36%
where the time goes in v4:
time: 459 us; the launch traced here: 457 us
  Pallas kernels  197 us (43%)
  waiting for transfers between devices  157 us (34%)
  local copies, waits for them, and re-layouts  34.5 us (8%)
  starting transfers between devices  29.9 us (7%)
  other arithmetic  20.8 us (5%)
  between operations  16.9 us (4%)
    ppermute x3, waiting for transfers between devices, line_gather(): lax.ppermute(down, 'tensor', [(shards - 1 - i, shards - 1 - j) for i, j i...  59.9 us
    pallas_call x1, Pallas kernels, ffn_backward(): pl.pallas_call(kernel, grid_spec=pltpu.PrefetchScalarGridSpec(num_scalar_...  35.5 us
    pallas_call x2, Pallas kernels, attend_back(): pl.pallas_call(kernel, grid_spec=pltpu.PrefetchScalarGridSpec(num_scalar_...  35 us
    ppermute x3, waiting for transfers between devices, send_round(): lax.ppermute(piece, 'tensor', cyclic(shards, k))  33.1 us
    pallas_call x2, Pallas kernels, ffn_forward(): pl.pallas_call(kernel, grid_spec=pltpu.PrefetchScalarGridSpec(num_scalar_...  31.6 us
    ppermute x1, waiting for transfers between devices, spread_first(): lax.ppermute(stack, 'yx', flip(1))  28.9 us
    pallas_call x4, Pallas kernels, roll_rows(): pl.pallas_call(kernel, grid_spec=pltpu.PrefetchScalarGridSpec(num_scalar_...  23.8 us
    pallas_call x2, Pallas kernels, project_back(): pl.pallas_call(kernel, grid_spec=pltpu.PrefetchScalarGridSpec(num_scalar_...  19.4 us
  transfers between devices with their start and end apart: 24, of which 12 were waited for; matrix products, arithmetic and copies ran while one was open for 11% of the time, Pallas kernels for 36%

profile of v4, /device:TPU:0, one launch (start us, length us, event | category | flops | bytes accessed | tf_op | source)
XLA Modules:
  0.0 457.0 jit_solution(6311772212361771317)
XLA Ops:
  7.2 1.1 constant_dynamic-slice_fusion.19
  8.4 1.0 constant_dynamic-slice_fusion.18
  10.4 1.6 copy.50
  15.6 1.3 constant_dynamic-update-slice_fusion.3
  17.0 1.3 constant_dynamic-update-slice_fusion.2
  19.5 5.1 %collective-permute-start.2 = (bf16[768,256]{1,0:T(8,128)(2,1)}, bf16[768,256]{1,0:T(8,128)(2,1)}, u32[]{:S(2)}, u32[]{:S(2)}) collective-permute-start(bf16[768,256]{1,0:T(8,128)(2,1)} %constant_dynamic-update-slice_fusion), channel_id=1, source_target_pairs={{0,3},{1,0},{2,1},{3,2},{4,7},{5,4},{6,5},{7,6},{8,11},{9,8},{10,9... | collective-permute-start | bytes 1179656 | tf_op jit(solution)/shard_map/ppermute | solution.py:783
  24.6 1.0 collective-permute-start
  28.7 4.7 %roll_rows.5.rest_4_ = f32[512,1024]{1,0:T(8,128)} custom-call(s32[3]{0:T(128)} %add_add_fusion.2.scalar_ref, bf16[2048,1024]{1,0:T(8,128)(2,1)} %refs_0_.3), custom_call_target="tpu_custom_call" | custom-call | flops 268435456 | bytes 6291456 | tf_op jit(solution)/shard_map/roll_rows/pallas_call | solution.py:71
  33.4 4.9 %roll_rows.4.x_ref = bf16[1024,1024]{1,0:T(8,128)(2,1)} custom-call(s32[3]{0:T(128)} %add_add_fusion.1.scalar_ref, bf16[2048,1024]{1,0:T(8,128)(2,1)} %refs_0_.2), custom_call_target="tpu_custom_call" | custom-call | flops 536870912 | bytes 8388608 | tf_op jit(solution)/shard_map/roll_rows/pallas_call | solution.py:71
  38.4 1.4 dynamic-slice_bitcast_fusion.6.b_ref.rest_7_
  39.8 1.5 dynamic-slice_bitcast_fusion.5.rest_1_
  41.3 26.6 %collective-permute-done = bf16[768,256]{1,0:T(8,128)(2,1)} collective-permute-done((bf16[768,256]{1,0:T(8,128)(2,1)}, bf16[768,256]{1,0:T(8,128)(2,1)}, u32[]{:S(2)}, u32[]{:S(2)}) %collective-permute-start) | collective-permute-done | bytes 393248 | tf_op jit(solution)/shard_map/ppermute | solution.py:783
  68.9 6.4 %collective-permute-done.1 = bf16[768,256]{1,0:T(8,128)(2,1)} collective-permute-done((bf16[768,256]{1,0:T(8,128)(2,1)}, bf16[768,256]{1,0:T(8,128)(2,1)}, u32[]{:S(2)}, u32[]{:S(2)}) %collective-permute-start.1) | collective-permute-done | bytes 393248 | tf_op jit(solution)/shard_map/ppermute | solution.py:783
  78.2 1.5 collective-permute-start.3
  79.7 1.5 collective-permute-start.4
  81.9 1.0 copy.54.all_ref
  82.9 1.5 dynamic-slice_bitcast_fusion.4.f_ref.rest_1_
  85.9 28.9 %collective-permute-done.3 = bf16[1536,256]{1,0:T(8,128)(2,1)} collective-permute-done((bf16[1536,256]{1,0:T(8,128)(2,1)}, bf16[1536,256]{1,0:T(8,128)(2,1)}, u32[]{:S(2)}, u32[]{:S(2)}) %collective-permute-start.3) | collective-permute-done | bytes 786464 | tf_op jit(solution)/shard_map/ppermute | solution.py:787
  114.7 1.0 slice.107
  115.8 1.5 collective-permute-start.5
  117.3 1.0 slice.108
  120.1 5.4 %collective-permute-done.5 = bf16[768,256]{1,0:T(8,128)(2,1)S(1)} collective-permute-done((bf16[768,256]{1,0:T(8,128)(2,1)S(1)}, bf16[768,256]{1,0:T(8,128)(2,1)S(1)}, u32[]{:S(2)}, u32[]{:S(2)}) %collective-permute-start.5) | collective-permute-done | bytes 393248 | tf_op jit(solution)/shard_map/ppermute | solution.py:793
  125.5 2.4 collective-permute-done.6
  128.0 3.3 pad_maximum_fusion.near_ref
  132.2 1.1 constant_dynamic-slice_fusion.8
  133.3 1.0 constant_dynamic-slice_fusion.17.o_ref.x_ref
  134.3 1.5 pad_maximum_fusion.1.own_ref
  136.5 1.0 slice_bitcast_fusion
  137.5 1.0 slice_bitcast_fusion.1
  142.5 8.5 %shard_map.294 = (bf16[4,3,1024,256]{3,2,1,0:T(8,128)(2,1)}, bf16[1024,1024]{1,0:T(8,128)(2,1)}) custom-call(s32[3]{0:T(128)} %pad_add_fusion.scalar_ref, bf16[8,512,256]{2,1,0:T(8,128)(2,1)} %pad_maximum_fusion.1.own_ref, bf16[4,3,512,256]{3,2,1,0:T(8,128)(2,1)} %pad_maximum_fusion.near_ref, bf16[4,3,512,256]{3,2,1,0:T(8,128)(2,1)} %collective-permute-done.7.far_ref), custom_call_target="tpu_custom_call" | custom-call | bytes 16777216 | tf_op jit(solution)/shard_map/pallas_call | solution.py:833
  151.0 12.0 %project_qkv.1 = (bf16[512,1024]{1,0:T(8,128)(2,1)}, bf16[1024,1024]{1,0:T(8,128)(2,1)}, bf16[1024,1024]{1,0:T(8,128)(2,1)}) custom-call(bf16[1024,1024]{1,0:T(8,128)(2,1)} %roll_rows.4.x_ref, bf16[512,1024]{1,0:T(8,128)(2,1)} %constant_dynamic-slice_fusion.17.o_ref.x_ref, bf16[4,3,1024,256]{3,2,1,0:T(8,128)(2,1)} %get-tuple-element.86.w_ref, ...), custom_call_target="tpu_custom_call" | custom-call | flops 5368709120 | bytes 20971520 | tf_op jit(solution)/shard_map/project_qkv/pallas_call | solution.py:127
  162.9 17.9 %attend.1 = (bf16[512,1024]{1,0:T(8,128)(2,1)}, f32[8,8,512]{2,1,0:T(8,128)}) custom-call(bf16[512,1024]{1,0:T(8,128)(2,1)} %get-tuple-element.87.q_ref, bf16[1024,1024]{1,0:T(8,128)(2,1)} %get-tuple-element.88.k_ref, bf16[1024,1024]{1,0:T(8,128)(2,1)} %get-tuple-element.89.v_ref, s32[1,512]{1,0:T(1,128)} %bitcast.112, s32[1024,1]{1,0:T(8,128)} %copy.54.all_ref), custom_call_target="tpu_custom_call" | custom-call | flops 8589934592 | bytes 6291456 | tf_op jit(solution)/shard_map/attend/pallas_call | solution.py:191
  180.8 6.8 %out_forward.1 = (f32[512,1024]{1,0:T(8,128)}, bf16[512,1024]{1,0:T(8,128)(2,1)}, f32[512,1024]{1,0:T(8,128)}, f32[512,1]{1,0:T(8,128)}, bf16[512,16]{1,0:T(8,128)(2,1)}, /*index=5*/bf16[512,32]{1,0:T(8,128)(2,1)}) custom-call(bf16[512,1024]{1,0:T(8,128)(2,1)} %get-tuple-element.90.m_ref.rest_9_, bf16[1024,1024]{1,0:T(8,128)(2,1)} %get-tuple-element.91.w_ref.rest_10_, ...), custom_call_target="tpu_custom_call" | custom-call | flops 1073741824 | bytes 9437184 | tf_op jit(solution)/shard_map/out_forward/pallas_call | solution.py:426
  188.4 9.2 %ffn_forward.2 = (bf16[2,512,4096]{2,1,0:T(8,128)(2,1)}, f32[512,1024]{1,0:T(8,128)}, f32[512,16]{1,0:T(8,128)}) custom-call(s32[1]{0:T(128)} %bitcast.2.place_ref, bf16[1,2,1024,1024]{3,2,1,0:T(8,128)(2,1)} %bitcast.107, bf16[1,1024,1024]{2,1,0:T(8,128)(2,1)} %bitcast.110, bf16[512,1024]{1,0:T(8,128)(2,1)} %get-tuple-element.92.hb_ref.rest_2_, ...), custom_call_target="tpu_custom_call" | custom-call | flops 3221225472 | bytes 8388608 | tf_op jit(solution)/shard_map/ffn_forward/pallas_call | solution.py:599
  197.6 13.4 %all-gather.6.cloned.1.call-done = bf16[12288,1024]{1,0:T(8,128)(2,1)} async-done(((bf16[384,1024]{1,0:T(8,128)(2,1)}), bf16[12288,1024]{1,0:T(8,128)(2,1)}) %all-gather.6.cloned.1.call-update) | async-done | bytes 25165840 | tf_op jit(solution)/shard_map/all_gather | solution.py:769
  211.0 22.4 %ffn_forward.3 = (bf16[2,512,4096]{2,1,0:T(8,128)(2,1)}, bf16[512,1024]{1,0:T(8,128)(2,1)}, f32[512,1024]{1,0:T(8,128)}, bf16[512,1024]{1,0:T(8,128)(2,1)}, bf16...) custom-call(s32[1]{0:T(128)} %bitcast.2.place_ref, ...), custom_call_target="tpu_custom_call", output_to_operand_aliasing={{0}: (9, {})} | custom-call | flops 9663676416 | bytes 25165824 | tf_op jit(solution)/shard_map/ffn_forward/pallas_call | solution.py:599
  235.4 35.5 %ffn_backward.1 = (bf16[4,48,1024]{2,1,0:T(8,128)(2,1)}, f32[512,1024]{1,0:T(8,128)}, bf16[512,1024]{1,0:T(8,128)(2,1)}, bf16[80,1024]{1,0:T(8,128)(2,1)}) custom-call(s32[1]{0:T(128)} %bitcast.2.place_ref, bf16[4,8,384,1024]{3,2,1,0:T(8,128)(2,1)} %bitcast.89, bf16[4,8,384,1024]{3,2,1,0:T(8,128)(2,1)} %bitcast.90, ...), custom_call_target="tpu_custom_call" | custom-call | flops 12884901888 | bytes 33554432 | tf_op jit(solution)/shard_map/ffn_backward/pallas_call | solution.py:700
  270.9 16.6 %attend_back.2 = (f32[512,1024]{1,0:T(8,128)}, bf16[512,1024]{1,0:T(8,128)(2,1)}, bf16[512,1024]{1,0:T(8,128)(2,1)}) custom-call(s32[1]{0:T(128)} %bitcast.43.block_ref, bf16[512,1024]{1,0:T(8,128)(2,1)} %get-tuple-element.87.q_ref, bf16[1024,1024]{1,0:T(8,128)(2,1)} %get-tuple-element.88.k_ref, bf16[1024,1024]{1,0:T(8,128)(2,1)} %get-tuple-element.89.v_ref, ...), custom_call_target="tpu_custom_call" | custom-call | flops 10737418240 | bytes 9437184 | tf_op jit(solution)/shard_map/attend_back/pallas_call | solution.py:287
  287.6 8.6 %project_back.2 = (bf16[512,1024]{1,0:T(8,128)(2,1)}, f32[32,1024]{1,0:T(8,128)}, f32[4,32,256]{2,1,0:T(8,128)}) custom-call(s32[1]{0:T(128)} %bitcast.43.block_ref, bf16[4,3,1024,256]{3,2,1,0:T(8,128)(2,1)} %get-tuple-element.86.w_ref, bf16[48,1024]{1,0:T(8,128)(2,1)} %bitcast.100, bf16[48,1024]{1,0:T(8,128)(2,1)} %copy-done.12, ...), custom_call_target="tpu_custom_call" | custom-call | flops 2147483648 | bytes 12582912 | tf_op jit(solution)/shard_map/project_back/pallas_call | solution.py:375
  297.2 2.0 collective-permute-start.9
  299.2 1.2 collective-permute-start.10
  300.4 1.2 collective-permute-start.11
  301.6 18.3 %attend_back.3 = (bf16[512,1024]{1,0:T(8,128)(2,1)}, bf16[512,1024]{1,0:T(8,128)(2,1)}, bf16[512,1024]{1,0:T(8,128)(2,1)}) custom-call(s32[1]{0:T(128)} %bitcast.42.block_ref, bf16[512,1024]{1,0:T(8,128)(2,1)} %get-tuple-element.87.q_ref, bf16[1024,1024]{1,0:T(8,128)(2,1)} %get-tuple-element.88.k_ref, bf16[1024,1024]{1,0:T(8,128)(2,1)} %get-tuple-element.89.v_ref, ...), custom_call_target="tpu_custom_call" | custom-call | flops 10737418240 | bytes 9437184 | tf_op jit(solution)/shard_map/attend_back/pallas_call | solution.py:287
  319.9 10.7 %project_back.3 = (f32[512,1024]{1,0:T(8,128)}, bf16[48,1024]{1,0:T(8,128)(2,1)}, bf16[4,48,256]{2,1,0:T(8,128)(2,1)}) custom-call(s32[1]{0:T(128)} %bitcast.42.block_ref, bf16[4,3,1024,256]{3,2,1,0:T(8,128)(2,1)} %get-tuple-element.86.w_ref, bf16[48,1024]{1,0:T(8,128)(2,1)} %bitcast.101, bf16[48,1024]{1,0:T(8,128)(2,1)} %copy-done.12, ...), custom_call_target="tpu_custom_call" | custom-call | flops 3221225472 | bytes 13631488 | tf_op jit(solution)/shard_map/project_back/pallas_call | solution.py:375
  331.5 1.7 pad_maximum_fusion.13
  334.0 9.8 %collective-permute-done.8 = bf16[512,1024]{1,0:T(8,128)(2,1)S(1)} collective-permute-done((bf16[512,1024]{1,0:T(8,128)(2,1)}, bf16[512,1024]{1,0:T(8,128)(2,1)S(1)}, u32[]{:S(2)}, u32[]{:S(2)}) %collective-permute-start.8) | collective-permute-done | bytes 1048608 | tf_op jit(solution)/shard_map/ppermute | solution.py:1119
  343.9 2.4 collective-permute-start.14
  346.2 1.9 add_convert_fusion.refs_0_
  348.2 5.8 %roll_rows.6 = bf16[2048,1024]{1,0:T(8,128)(2,1)} custom-call(s32[3]{0:T(128)} %add_add_fusion.scalar_ref, bf16[2048,1024]{1,0:T(8,128)(2,1)} %all-gather.8.cloned.1.call-done.refs_0_), custom_call_target="tpu_custom_call" | custom-call | flops 1073741824 | bytes 12582912 | tf_op jit(solution)/shard_map/roll_rows/pallas_call | solution.py:71
  354.0 1.1 collective-permute-done.11
  355.1 2.9 collective-permute-done.14
  358.0 1.1 add_convert_fusion.1
  359.1 1.0 add_convert_fusion.2
  360.9 1.3 collective-permute-start.16
  362.3 4.6 %collective-permute-start.15 = (bf16[512,1024]{1,0:T(8,128)(2,1)S(1)}, bf16[512,1024]{1,0:T(8,128)(2,1)S(1)}, u32[]{:S(2)}, u32[]{:S(2)}) collective-permute-start(bf16[512,1024]{1,0:T(8,128)(2,1)S(1)} %add_convert_fusion.refs_0_), channel_id=1, source_target_pairs={{0,1},{1,2},{2,3},{4,5},{5,6},{6,7},{8,9},{9,10},{10,11},{12,13},{... | collective-permute-start | bytes 3145736 | tf_op jit(solution)/shard_map/ppermute | solution.py:910
  366.9 21.1 %collective-permute-done.16.refs_2_ = bf16[512,1024]{1,0:T(8,128)(2,1)S(1)} collective-permute-done((bf16[512,1024]{1,0:T(8,128)(2,1)S(1)}, bf16[512,1024]{1,0:T(8,128)(2,1)S(1)}, u32[]{:S(2)}, u32[]{:S(2)}) %collective-permute-start.16) | collective-permute-done | bytes 1048608 | tf_op jit(solution)/shard_map/ppermute | solution.py:911
  388.0 1.3 collective-permute-start.18
  390.1 24.4 %collective-permute-done.18.refs_4_ = bf16[512,1024]{1,0:T(8,128)(2,1)} collective-permute-done((bf16[512,1024]{1,0:T(8,128)(2,1)S(1)}, bf16[512,1024]{1,0:T(8,128)(2,1)}, u32[]{:S(2)}, u32[]{:S(2)}) %collective-permute-start.18) | collective-permute-done | bytes 1048608 | tf_op jit(solution)/shard_map/ppermute | solution.py:911
  414.4 1.3 collective-permute-start.20
  415.7 1.7 collective-permute-start.19
  418.9 7.0 %place_sums.1 = (f32[8,16,1024]{2,1,0:T(8,128)}, f32[8,32,1024]{2,1,0:T(8,128)}, f32[8,16,1024]{2,1,0:T(8,128)}, f32[8,16,256]{2,1,0:T(8,128)}, f32[8,16,1024]{2...) custom-call(s32[9]{0:T(128)} %pad_add_fusion.1.scalar_ref, ...), custom_call_target="tpu_custom_call" | custom-call | flops 1540096 | bytes 9240576 | tf_op jit(solution)/shard_map/place_sums/pallas_call | solution.py:946
  425.8 14.4 %collective-permute-done.20.refs_6_ = bf16[512,1024]{1,0:T(8,128)(2,1)} collective-permute-done((bf16[512,1024]{1,0:T(8,128)(2,1)}, bf16[512,1024]{1,0:T(8,128)(2,1)}, u32[]{:S(2)}, u32[]{:S(2)}) %collective-permute-start.20) | collective-permute-done | bytes 1048608 | tf_op jit(solution)/shard_map/ppermute | solution.py:911
  440.2 1.9 reshape.178
  442.1 8.4 %roll_rows.7 = f32[2048,1024]{1,0:T(8,128)} custom-call(s32[3]{0:T(128)} %add_add_fusion.scalar_ref, bf16[512,1024]{1,0:T(8,128)(2,1)} %copy-done.5, bf16[512,1024]{1,0:T(8,128)(2,1)} %copy-done.10, bf16[512,1024]{1,0:T(8,128)(2,1)} %copy-done.9, bf16[512,1024]{1,0:T(8,128)(2,1)} %copy-done.11, bf16[512,1024]{1,0:T(8,128)(2,1)} %collective-permute-done.18.refs_4_, ...), custom_call_target="tpu_custom_call" | custom-call | flops 1073741824 | bytes 12582912 | tf_op jit(solution)/shard_map/roll_rows/pallas_call | solution.py:71
  (139 shorter events, 28.2 us)
Async XLA Ops:
  7.2 77.2 %copy-start = (bf16[8,48,1024]{2,1,0:T(8,128)(2,1)S(1)}, bf16[8,48,1024]{2,1,0:T(8,128)(2,1)}, u32[]{:S(2)}) copy-start(bf16[8,48,1024]{2,1,0:T(8,128)(2,1)} %param.35) | copy-start | bytes 2359300
  7.2 203.8 %all-gather.6.cloned.1.call-start = ((), (), s32[]{:S(2)}) async-start(), calls=%async_computation | async-start | bytes 25952256 | tf_op jit(solution)/shard_map/all_gather | solution.py:769
  10.3 1.6 copy-start.14
  10.4 337.9 %all-gather.8.cloned.1.call-start = ((), (), s32[]{:S(2)}) async-start(), calls=%async_computation.1 | async-start | bytes 5242880 | tf_op jit(solution)/shard_map/all_gather | solution.py:1092
  12.0 3.6 copy-start.3
  12.4 13.2 %copy-start.19 = (s32[1,2048]{1,0:T(1,128)S(1)}, s32[1,2048]{1,0:T(1,128)}, u32[]{:S(2)}) copy-start(s32[1,2048]{1,0:T(1,128)} %param.27) | copy-start | bytes 24580
  19.5 56.8 %collective-permute-start.2 = (bf16[768,256]{1,0:T(8,128)(2,1)}, bf16[768,256]{1,0:T(8,128)(2,1)}, u32[]{:S(2)}, u32[]{:S(2)}) collective-permute-start(bf16[768,256]{1,0:T(8,128)(2,1)} %constant_dynamic-update-slice_fusion), channel_id=1, source_target_pairs={{0,3},{1,0},{2,1},{3,2},{4,7},{5,4},{6,5},{7,6},{8,11},{9,8},{10,9... | collective-permute-start | bytes 1179656 | tf_op jit(solution)/shard_map/ppermute | solution.py:783
  24.6 50.7 %collective-permute-start.1 = (bf16[768,256]{1,0:T(8,128)(2,1)}, bf16[768,256]{1,0:T(8,128)(2,1)}, u32[]{:S(2)}, u32[]{:S(2)}) collective-permute-start(bf16[768,256]{1,0:T(8,128)(2,1)} %constant_dynamic-update-slice_fusion), channel_id=1, source_target_pairs={{0,2},{1,3},{2,0},{3,1},{4,6},{5,7},{6,4},{7,5},{8,10},{9,11},{10,... | collective-permute-start | bytes 1179656 | tf_op jit(solution)/shard_map/ppermute | solution.py:783
  24.6 43.3 %collective-permute-start = (bf16[768,256]{1,0:T(8,128)(2,1)}, bf16[768,256]{1,0:T(8,128)(2,1)}, u32[]{:S(2)}, u32[]{:S(2)}) collective-permute-start(bf16[768,256]{1,0:T(8,128)(2,1)} %constant_dynamic-update-slice_fusion), channel_id=1, source_target_pairs={{0,1},{1,2},{2,3},{3,0},{4,5},{5,6},{6,7},{7,4},{8,9},{9,10},{10,1... | collective-permute-start | bytes 1179656 | tf_op jit(solution)/shard_map/ppermute | solution.py:783
  39.8 44.6 %copy-start.2 = (bf16[1024,1024]{1,0:T(8,128)(2,1)S(1)}, bf16[1024,1024]{1,0:T(8,128)(2,1)}, u32[]{:S(2)}) copy-start(bf16[1024,1024]{1,0:T(8,128)(2,1)} %roll_rows.4.x_ref) | copy-start | bytes 6291460
  78.2 36.5 %collective-permute-start.3 = (bf16[1536,256]{1,0:T(8,128)(2,1)}, bf16[1536,256]{1,0:T(8,128)(2,1)}, u32[]{:S(2)}, u32[]{:S(2)}) collective-permute-start(bf16[1536,256]{1,0:T(8,128)(2,1)} %pad_maximum_fusion.3), channel_id=1, source_target_pairs={{0,8},{8,0},{16,24},{24,16},{1,9},{9,1},{17,25},{25,17},{2,10},{10... | collective-permute-start | bytes 2359304 | tf_op jit(solution)/shard_map/ppermute | solution.py:787
  79.7 37.6 %collective-permute-start.4 = (bf16[1536,256]{1,0:T(8,128)(2,1)}, bf16[1536,256]{1,0:T(8,128)(2,1)}, u32[]{:S(2)}, u32[]{:S(2)}) collective-permute-start(bf16[1536,256]{1,0:T(8,128)(2,1)} %pad_maximum_fusion.3), channel_id=1, source_target_pairs={{0,16},{8,24},{16,0},{24,8},{1,17},{9,25},{17,1},{25,9},{2,18},{10... | collective-permute-start | bytes 2359304 | tf_op jit(solution)/shard_map/ppermute | solution.py:787
  84.4 34.0 %copy-start.12 = (bf16[48,1024]{1,0:T(8,128)(2,1)}, bf16[48,1024]{1,0:T(8,128)(2,1)S(1)}, u32[]{:S(2)}) copy-start(bf16[48,1024]{1,0:T(8,128)(2,1)S(1)} %dynamic-slice_bitcast_fusion.3.a_ref) | copy-start | bytes 294916
  84.4 35.2 %copy-start.20 = (f32[64,128]{1,0:T(8,128)S(1)}, f32[64,128]{1,0:T(8,128)}, u32[]{:S(2)}) copy-start(f32[64,128]{1,0:T(8,128)} %constant.239.clone) | copy-start | bytes 98308
  84.4 35.2 %copy-start.21 = (f32[64,128]{1,0:T(8,128)S(1)}, f32[64,128]{1,0:T(8,128)}, u32[]{:S(2)}) copy-start(f32[64,128]{1,0:T(8,128)} %constant.240.clone) | copy-start | bytes 98308
  84.4 35.2 %copy-start.22 = (f32[48,128]{1,0:T(8,128)S(1)}, f32[48,128]{1,0:T(8,128)}, u32[]{:S(2)}) copy-start(f32[48,128]{1,0:T(8,128)} %constant.237.clone) | copy-start | bytes 73732
  84.4 35.2 %copy-start.23 = (f32[48,128]{1,0:T(8,128)S(1)}, f32[48,128]{1,0:T(8,128)}, u32[]{:S(2)}) copy-start(f32[48,128]{1,0:T(8,128)} %constant.238.clone) | copy-start | bytes 73732
  85.1 35.0 %copy-start.7 = (bf16[1024,48]{1,0:T(8,128)(2,1)}, bf16[1024,48]{1,0:T(8,128)(2,1)S(1)}, u32[]{:S(2)}) copy-start(bf16[1024,48]{1,0:T(8,128)(2,1)S(1)} %convolution_convert_fusion.l_ref) | copy-start | bytes 294916
  115.8 9.8 %collective-permute-start.5 = (bf16[768,256]{1,0:T(8,128)(2,1)S(1)}, bf16[768,256]{1,0:T(8,128)(2,1)S(1)}, u32[]{:S(2)}, u32[]{:S(2)}) collective-permute-start(bf16[768,256]{1,0:T(8,128)(2,1)S(1)} %slice.107), channel_id=1, source_target_pairs={{0,16},{8,24},{16,0},{24,8},{1,17},{9,25},{17,1},{25,9},{2,18},{10... | collective-permute-start | bytes 1179656 | tf_op jit(solution)/shard_map/ppermute | solution.py:793
  118.4 9.5 %collective-permute-start.6 = (bf16[768,256]{1,0:T(8,128)(2,1)S(1)}, bf16[768,256]{1,0:T(8,128)(2,1)S(1)}, u32[]{:S(2)}, u32[]{:S(2)}) collective-permute-start(bf16[768,256]{1,0:T(8,128)(2,1)S(1)} %slice.108), channel_id=1, source_target_pairs={{0,8},{8,0},{16,24},{24,16},{1,9},{9,1},{17,25},{25,17},{2,10},{10... | collective-permute-start | bytes 1179656 | tf_op jit(solution)/shard_map/ppermute | solution.py:794
  128.0 3.3 copy-start.26
  131.3 11.2 %collective-permute-start.7 = (bf16[4,3,512,256]{3,2,1,0:T(8,128)(2,1)}, bf16[4,3,512,256]{3,2,1,0:T(8,128)(2,1)}, u32[]{:S(2)}, u32[]{:S(2)}) collective-permute-start(bf16[4,3,512,256]{3,2,1,0:T(8,128)(2,1)} %pad_maximum_fusion.near_ref), channel_id=1, source_target_pairs={{0,4},{4,0},{1,5},{5,1},{2,6},{6,2},{3,7},{7,3},{8,12},{12,8},{9,1... | collective-permute-start | bytes 9437192 | tf_op jit(solution)/shard_map/ppermute | solution.py:799
  132.2 2.1 copy-start.4
  134.3 1.5 copy-start.24
  134.3 1.5 copy-start.25
  139.6 11.3 %copy-start.8 = (bf16[4,16,1024]{2,1,0:T(8,128)(2,1)}, bf16[4,16,1024]{2,1,0:T(8,128)(2,1)S(1)}, u32[]{:S(2)}) copy-start(bf16[4,16,1024]{2,1,0:T(8,128)(2,1)S(1)} %reshape.171.da_ref) | copy-start | bytes 393220
  139.9 11.0 %copy-start.6 = (bf16[4,32,1024]{2,1,0:T(8,128)(2,1)}, bf16[4,32,1024]{2,1,0:T(8,128)(2,1)S(1)}, u32[]{:S(2)}) copy-start(bf16[4,32,1024]{2,1,0:T(8,128)(2,1)S(1)} %reshape.170.fb_ref) | copy-start | bytes 786436
  233.4 184.0 %all-gather.10.cloned.1.call-start = ((), (), s32[]{:S(2)}) async-start(), calls=%async_computation.2 | async-start | bytes 3833856 | tf_op jit(solution)/shard_map/all_gather | solution.py:1151
  287.6 8.7 %copy-start.16 = (bf16[4,48,1024]{2,1,0:T(8,128)(2,1)S(1)}, bf16[4,48,1024]{2,1,0:T(8,128)(2,1)}, u32[]{:S(2)}) copy-start(bf16[4,48,1024]{2,1,0:T(8,128)(2,1)} %get-tuple-element.124) | copy-start | bytes 1179652
  287.6 8.7 %copy-start.13 = (bf16[80,1024]{1,0:T(8,128)(2,1)S(1)}, bf16[80,1024]{1,0:T(8,128)(2,1)}, u32[]{:S(2)}) copy-start(bf16[80,1024]{1,0:T(8,128)(2,1)} %get-tuple-element.123) | copy-start | bytes 491524
  296.2 47.6 %collective-permute-start.8 = (bf16[512,1024]{1,0:T(8,128)(2,1)}, bf16[512,1024]{1,0:T(8,128)(2,1)S(1)}, u32[]{:S(2)}, u32[]{:S(2)}) collective-permute-start(bf16[512,1024]{1,0:T(8,128)(2,1)} %get-tuple-element.119), channel_id=1, source_target_pairs={{0,1},{1,0},{2,3},{3,2},{4,5},{5,4},{6,7},{7,6},{8,9},{9,8},{10,11... | collective-permute-start | bytes 3145736 | tf_op jit(solution)/shard_map/ppermute | solution.py:1119
  297.2 46.7 %collective-permute-start.9 = (bf16[128,1024]{1,0:T(8,128)(2,1)S(1)}, bf16[128,1024]{1,0:T(8,128)(2,1)S(1)}, u32[]{:S(2)}, u32[]{:S(2)}) collective-permute-start(bf16[128,1024]{1,0:T(8,128)(2,1)S(1)} %get-tuple-element.160), channel_id=1, source_target_pairs={{0,1},{1,2},{2,3},{3,0},{4,5},{5,6},{6,7},{7,4},{8,9},{9,10},{10,1... | collective-permute-start | bytes 786440 | tf_op jit(solution)/shard_map/ppermute | solution.py:893
  299.2 54.8 %collective-permute-start.10 = (bf16[128,1024]{1,0:T(8,128)(2,1)}, bf16[128,1024]{1,0:T(8,128)(2,1)S(1)}, u32[]{:S(2)}, u32[]{:S(2)}) collective-permute-start(bf16[128,1024]{1,0:T(8,128)(2,1)} %get-tuple-element.161), channel_id=1, source_target_pairs={{0,2},{1,3},{2,0},{3,1},{4,6},{5,7},{6,4},{7,5},{8,10},{9,11},{10,... | collective-permute-start | bytes 786440 | tf_op jit(solution)/shard_map/ppermute | solution.py:893
  300.4 54.7 %collective-permute-start.11 = (bf16[128,1024]{1,0:T(8,128)(2,1)}, bf16[128,1024]{1,0:T(8,128)(2,1)S(1)}, u32[]{:S(2)}, u32[]{:S(2)}) collective-permute-start(bf16[128,1024]{1,0:T(8,128)(2,1)} %get-tuple-element.162), channel_id=1, source_target_pairs={{0,3},{1,0},{2,1},{3,2},{4,7},{5,4},{6,5},{7,6},{8,11},{9,8},{10,9... | collective-permute-start | bytes 786440 | tf_op jit(solution)/shard_map/ppermute | solution.py:893
  333.2 21.9 %collective-permute-start.12 = (bf16[60,1024]{1,0:T(8,128)(2,1)}, bf16[60,1024]{1,0:T(8,128)(2,1)S(1)}, u32[]{:S(2)}, u32[]{:S(2)}) collective-permute-start(bf16[60,1024]{1,0:T(8,128)(2,1)} %get-tuple-element.169), channel_id=1, source_target_pairs={{0,1},{1,2},{2,3},{3,0},{4,5},{5,6},{6,7},{7,4},{8,9},{9,10},{10,1... | collective-permute-start | bytes 368648 | tf_op jit(solution)/shard_map/ppermute | solution.py:893
  343.8 11.2 %collective-permute-start.13 = (bf16[60,1024]{1,0:T(8,128)(2,1)}, bf16[60,1024]{1,0:T(8,128)(2,1)S(1)}, u32[]{:S(2)}, u32[]{:S(2)}) collective-permute-start(bf16[60,1024]{1,0:T(8,128)(2,1)} %get-tuple-element.170), channel_id=1, source_target_pairs={{0,2},{1,3},{2,0},{3,1},{4,6},{5,7},{6,4},{7,5},{8,10},{9,11},{10,... | collective-permute-start | bytes 368648 | tf_op jit(solution)/shard_map/ppermute | solution.py:893
  343.9 14.1 %collective-permute-start.14 = (bf16[60,1024]{1,0:T(8,128)(2,1)}, bf16[60,1024]{1,0:T(8,128)(2,1)}, u32[]{:S(2)}, u32[]{:S(2)}) collective-permute-start(bf16[60,1024]{1,0:T(8,128)(2,1)} %get-tuple-element.171), channel_id=1, source_target_pairs={{0,3},{1,0},{2,1},{3,2},{4,7},{5,4},{6,5},{7,6},{8,11},{9,8},{10,9... | collective-permute-start | bytes 368648 | tf_op jit(solution)/shard_map/ppermute | solution.py:893
  348.2 14.1 %copy-start.5 = (bf16[512,1024]{1,0:T(8,128)(2,1)}, bf16[512,1024]{1,0:T(8,128)(2,1)S(1)}, u32[]{:S(2)}) copy-start(bf16[512,1024]{1,0:T(8,128)(2,1)S(1)} %add_convert_fusion.refs_0_) | copy-start | bytes 3145732
  348.2 10.9 %copy-start.15 = (bf16[48,1024]{1,0:T(8,128)(2,1)S(1)}, bf16[48,1024]{1,0:T(8,128)(2,1)}, u32[]{:S(2)}) copy-start(bf16[48,1024]{1,0:T(8,128)(2,1)} %get-tuple-element.128) | copy-start | bytes 294916
  348.2 11.9 %copy-start.18 = (bf16[16,1024]{1,0:T(8,128)(2,1)S(1)}, bf16[16,1024]{1,0:T(8,128)(2,1)}, u32[]{:S(2)}) copy-start(bf16[16,1024]{1,0:T(8,128)(2,1)} %pad_convert_fusion) | copy-start | bytes 98308
  355.1 2.9 copy-start.17
  360.9 27.1 %collective-permute-start.16 = (bf16[512,1024]{1,0:T(8,128)(2,1)S(1)}, bf16[512,1024]{1,0:T(8,128)(2,1)S(1)}, u32[]{:S(2)}, u32[]{:S(2)}) collective-permute-start(bf16[512,1024]{1,0:T(8,128)(2,1)S(1)} %add_convert_fusion.refs_0_), channel_id=1, source_target_pairs={{3,2},{2,1},{1,0},{7,6},{6,5},{5,4},{11,10},{10,9},{9,8},{15,14},{... | collective-permute-start | bytes 3145736 | tf_op jit(solution)/shard_map/ppermute | solution.py:911
  362.3 27.1 %collective-permute-start.15 = (bf16[512,1024]{1,0:T(8,128)(2,1)S(1)}, bf16[512,1024]{1,0:T(8,128)(2,1)S(1)}, u32[]{:S(2)}, u32[]{:S(2)}) collective-permute-start(bf16[512,1024]{1,0:T(8,128)(2,1)S(1)} %add_convert_fusion.refs_0_), channel_id=1, source_target_pairs={{0,1},{1,2},{2,3},{4,5},{5,6},{6,7},{8,9},{9,10},{10,11},{12,13},{... | collective-permute-start | bytes 3145736 | tf_op jit(solution)/shard_map/ppermute | solution.py:910
  388.0 54.1 %copy-start.9 = (bf16[512,1024]{1,0:T(8,128)(2,1)}, bf16[512,1024]{1,0:T(8,128)(2,1)S(1)}, u32[]{:S(2)}) copy-start(bf16[512,1024]{1,0:T(8,128)(2,1)S(1)} %collective-permute-done.16.refs_2_) | copy-start | bytes 3145732
  388.0 26.4 %collective-permute-start.18 = (bf16[512,1024]{1,0:T(8,128)(2,1)S(1)}, bf16[512,1024]{1,0:T(8,128)(2,1)}, u32[]{:S(2)}, u32[]{:S(2)}) collective-permute-start(bf16[512,1024]{1,0:T(8,128)(2,1)S(1)} %collective-permute-done.16.refs_2_), channel_id=1, source_target_pairs={{2,1},{1,0},{6,5},{5,4},{10,9},{9,8},{14,13},{13,12},{18,17},{17,1... | collective-permute-start | bytes 3145736 | tf_op jit(solution)/shard_map/ppermute | solution.py:911
  389.3 25.1 %copy-start.10 = (bf16[512,1024]{1,0:T(8,128)(2,1)}, bf16[512,1024]{1,0:T(8,128)(2,1)S(1)}, u32[]{:S(2)}) copy-start(bf16[512,1024]{1,0:T(8,128)(2,1)S(1)} %collective-permute-done.15.refs_1_) | copy-start | bytes 3145732
  389.3 26.4 %collective-permute-start.17 = (bf16[512,1024]{1,0:T(8,128)(2,1)S(1)}, bf16[512,1024]{1,0:T(8,128)(2,1)S(1)}, u32[]{:S(2)}, u32[]{:S(2)}) collective-permute-start(bf16[512,1024]{1,0:T(8,128)(2,1)S(1)} %collective-permute-done.15.refs_1_), channel_id=1, source_target_pairs={{1,2},{2,3},{5,6},{6,7},{9,10},{10,11},{13,14},{14,15},{17,18},{18... | collective-permute-start | bytes 3145736 | tf_op jit(solution)/shard_map/ppermute | solution.py:910
  414.4 25.8 %collective-permute-start.20 = (bf16[512,1024]{1,0:T(8,128)(2,1)}, bf16[512,1024]{1,0:T(8,128)(2,1)}, u32[]{:S(2)}, u32[]{:S(2)}) collective-permute-start(bf16[512,1024]{1,0:T(8,128)(2,1)} %collective-permute-done.18.refs_4_), channel_id=1, source_target_pairs={{1,0},{5,4},{9,8},{13,12},{17,16},{21,20},{25,24},{29,28}} | collective-permute-start | bytes 3145736 | tf_op jit(solution)/shard_map/ppermute | solution.py:911
  415.7 26.4 %copy-start.11 = (bf16[512,1024]{1,0:T(8,128)(2,1)}, bf16[512,1024]{1,0:T(8,128)(2,1)S(1)}, u32[]{:S(2)}) copy-start(bf16[512,1024]{1,0:T(8,128)(2,1)S(1)} %collective-permute-done.17.refs_3_) | copy-start | bytes 3145732
  415.7 24.5 %collective-permute-start.19 = (bf16[512,1024]{1,0:T(8,128)(2,1)S(1)}, bf16[512,1024]{1,0:T(8,128)(2,1)}, u32[]{:S(2)}, u32[]{:S(2)}) collective-permute-start(bf16[512,1024]{1,0:T(8,128)(2,1)S(1)} %collective-permute-done.17.refs_3_), channel_id=1, source_target_pairs={{2,3},{6,7},{10,11},{14,15},{18,19},{22,23},{26,27},{30,31}} | collective-permute-start | bytes 3145736 | tf_op jit(solution)/shard_map/ppermute | solution.py:910
  442.1 8.4 %copy-start.1 = (bf16[8,48,1024]{2,1,0:T(8,128)(2,1)S(1)}, bf16[8,48,1024]{2,1,0:T(8,128)(2,1)}, u32[]{:S(2)}) copy-start(bf16[8,48,1024]{2,1,0:T(8,128)(2,1)} %param.35) | copy-start | bytes 2359300
Sparse Core Ops, SparseCore 0:
  10.9 200.0 all-gather.5
  233.6 86.2 all-gather.7
  361.1 33.7 all-gather.9

commit v5 on v4

--- a/solution.py
+++ b/solution.py
@@ -522,8 +522,8 @@
         if pre is not None:
             rest = rest[1:]
         if end:
-            db_ref, g_ref, s_ref, c_ref = rest[:4]
-            pre_ref, res_ref, mid_ref, midb_ref, ld_ref, ldg_ref, acc_ref, lat_ref = rest[4:]
+            db_ref, g_ref, s_ref = rest[:3]
+            pre_ref, res_ref, sums_ref, ld_ref, acc_ref, lat_ref = rest[3:]
         else:
             pre_ref, acc_ref, lat_ref = rest
 
@@ -549,14 +549,10 @@
             def _():
                 latent_down = lat_ref[...].astype(BF16)
                 sums = acc_ref[...] + nn(latent_down, db_ref[...])
-                result, normed, inverse = norm_forward(sums, g_ref[...], s_ref[...])
+                result, _, _ = norm_forward(sums, g_ref[...], s_ref[...])
                 res_ref[...] = result.astype(BF16)
-                grad = norm_backward(c_ref[...], normed, inverse, g_ref[...])
-                mid_ref[...] = grad
-                grad_b = grad.astype(BF16)
-                midb_ref[...] = grad_b
+                sums_ref[...] = sums
                 ld_ref[...] = latent_down
-                ldg_ref[...] = nt(grad_b, db_ref[...]).astype(BF16)
 
     full = lambda array: pl.BlockSpec(array.shape, lambda t, b, s: (0,) * array.ndim)
     fixed = lambda size: pl.BlockSpec((count, size), lambda t, b, s: (0, 0))
@@ -581,12 +577,10 @@
     if end:
         operands += list(end)
         specs += [full(array) for array in end]
-        out_specs += [fixed(width)] * 3 + [fixed(rank)] * 2
+        out_specs += [fixed(width)] * 2 + [fixed(rank)]
         out_shape += [
             jax.ShapeDtypeStruct((count, width), BF16),
             jax.ShapeDtypeStruct((count, width), F32),
-            jax.ShapeDtypeStruct((count, width), BF16),
-            jax.ShapeDtypeStruct((count, rank), BF16),
             jax.ShapeDtypeStruct((count, rank), BF16),
         ]
         scratch = [pltpu.VMEM((count, width), F32), pltpu.VMEM((count, rank), F32)]
@@ -616,23 +610,28 @@
     )(scalars, *operands)
 
 
-def ffn_backward(weights, grad_b, pre, latent_down_grad, latent_ffn, fb, da, total, end):
-    count, width = total.shape
+def ffn_backward(weights, sums, cotangent, gain_two, db, pre, latent_ffn, fb, da, end):
+    count, width = sums.shape
     shards, units = weights.shards, weights.units
     rank = da.shape[1]
     sub, inner = weights.sub, weights.inner
     steps = shards * inner
     scalars = jnp.reshape(lax.axis_index("tensor"), (1,)).astype(jnp.int32)
 
-    def kernel(place_ref, w0_ref, w1_ref, gb_ref, pre_ref, ldg_ref, lf_ref, fb_ref, da_ref, t_ref, *rest):
+    def kernel(place_ref, w0_ref, w1_ref, sums_ref, c_ref, g2_ref, db_ref, pre_ref, lf_ref, fb_ref, da_ref, *rest):
         refs = (w0_ref, w1_ref)
         step = pl.program_id(0) * inner + pl.program_id(1)
         ld_ref, fa_ref, hb_ref, n_ref, i_ref, gain_ref, lo_ref, ob_ref, oa_ref, m_ref, wo_ref = rest[:11]
-        split_ref, first_ref, mixed_ref, common_ref, acc_ref, lat_ref = rest[11:]
+        split_ref, first_ref, mixed_ref, common_ref, acc_ref, lat_ref, gb_ref, ldg_ref = rest[11:]
 
         @pl.when(step == 0)
         def _():
-            acc_ref[...] = t_ref[...]
+            _, normed, inverse = norm_forward(sums_ref[...], g2_ref[...], 0.0)
+            grad = norm_backward(c_ref[...], normed, inverse, g2_ref[...])
+            acc_ref[...] = grad
+            grad_b = grad.astype(BF16)
+            gb_ref[...] = grad_b
+            ldg_ref[...] = nt(grad_b, db_ref[...]).astype(BF16)
             lat_ref[...] = jnp.zeros_like(lat_ref)
 
         ldg = ldg_ref[...]
@@ -676,16 +675,17 @@
 
     full = lambda array: pl.BlockSpec(array.shape, lambda t, b, s: (0,) * array.ndim)
     fixed = lambda rows, size: pl.BlockSpec((rows, size), lambda t, b, s: (0, 0))
-    operands = [*weights.operands, grad_b, pre, latent_down_grad, latent_ffn, fb, da, total, *end]
+    operands = [*weights.operands, sums, cotangent, gain_two, db, pre, latent_ffn, fb, da, *end]
     specs = [
         *weights.specs,
-        full(grad_b),
+        full(sums),
+        full(cotangent),
+        full(gain_two),
+        full(db),
         pl.BlockSpec((2, count, sub), lambda t, b, s: (0, 0, t * inner + b)),
-        full(latent_down_grad),
         full(latent_ffn),
         pl.BlockSpec((1, 2 * rank, sub), lambda t, b, s: (weights.pick(t, s), 0, b)),
         pl.BlockSpec((1, rank, sub), lambda t, b, s: (weights.pick(t, s), 0, b)),
-        full(total),
         *[full(array) for array in end],
     ]
     out_specs = [pl.BlockSpec((1, 3 * rank, sub), lambda t, b, s: (t, 0, b))]
@@ -696,7 +696,12 @@
         jax.ShapeDtypeStruct((count, width), BF16),
         jax.ShapeDtypeStruct((5 * rank, width), BF16),
     ]
-    scratch = [pltpu.VMEM((count, width), F32), pltpu.VMEM((count, 2 * rank), F32)]
+    scratch = [
+        pltpu.VMEM((count, width), F32),
+        pltpu.VMEM((count, 2 * rank), F32),
+        pltpu.VMEM((count, width), BF16),
+        pltpu.VMEM((count, rank), BF16),
+    ]
     return pl.pallas_call(
         kernel,
         grid_spec=pltpu.PrefetchScalarGridSpec(
@@ -1074,7 +1079,7 @@
     )
 
     zero = jnp.zeros((count, rank), F32)
-    end = (db, ln_gain[1:], ln_bias[1:], cotangent)
+    end = (db, ln_gain[1:], ln_bias[1:])
     packed = len(ffn_all) == 1
     if packed:
         mine = lambda stack: lax.dynamic_slice_in_dim(stack, place, 1, 0)
@@ -1086,7 +1091,7 @@
     else:
         pre, total, down = None, hidden, zero
         others = every = Whole(*ffn_all)
-    pre, result, grad_mid, grad_ffn, latent_down, latent_down_grad = ffn_forward(
+    pre, result, sums, latent_down = ffn_forward(
         others, hidden_b, latent_ffn, fb, da, total, down, end, pre, shards - others.shards, shards
     )
     rolled = lax.all_gather(result, "tensor", axis=0, tiled=True)
@@ -1095,7 +1100,7 @@
         latent_down, fa, hidden_b, normed, inverse, ln_gain[:1], latent_out, ob, oa, mixed, out_all,
     )
     split, grad_first, grad_mixed, common = ffn_backward(
-        every, grad_ffn, pre, latent_down_grad, latent_ffn, fb, da, grad_mid, end
+        every, sums, cotangent, ln_gain[1:], db, pre, latent_ffn, fb, da, end
     )
 
     dq = None

time: 459 us -> 456 us (level)
  transfers between devices with their start and end apart: 24 -> 24, of which waited for: 12 -> 12; matrix products, arithmetic and copies ran while one was open for 11% -> 11% of each run, Pallas kernels for 36% -> 37%
where the time goes in v5:
time: 456 us; the launch traced here: 454 us
  Pallas kernels  197 us (43%)
  waiting for transfers between devices  154 us (34%)
  local copies, waits for them, and re-layouts  34.5 us (8%)
  starting transfers between devices  30 us (7%)
  other arithmetic  20.9 us (5%)
  between operations  17 us (4%)
    ppermute x3, waiting for transfers between devices, line_gather(): lax.ppermute(down, 'tensor', [(shards - 1 - i, shards - 1 - j) for i, j i...  59.5 us
    pallas_call x1, Pallas kernels, ffn_backward(): pl.pallas_call(kernel, grid_spec=pltpu.PrefetchScalarGridSpec(num_scalar_...  37.5 us
    pallas_call x2, Pallas kernels, attend_back(): pl.pallas_call(kernel, grid_spec=pltpu.PrefetchScalarGridSpec(num_scalar_...  35 us
    ppermute x3, waiting for transfers between devices, send_round(): lax.ppermute(piece, 'tensor', cyclic(shards, k))  32.9 us
    pallas_call x2, Pallas kernels, ffn_forward(): pl.pallas_call(kernel, grid_spec=pltpu.PrefetchScalarGridSpec(num_scalar_...  29.1 us
    ppermute x1, waiting for transfers between devices, spread_first(): lax.ppermute(stack, 'yx', flip(1))  28.9 us
    pallas_call x4, Pallas kernels, roll_rows(): pl.pallas_call(kernel, grid_spec=pltpu.PrefetchScalarGridSpec(num_scalar_...  23.8 us
    pallas_call x2, Pallas kernels, project_back(): pl.pallas_call(kernel, grid_spec=pltpu.PrefetchScalarGridSpec(num_scalar_...  19.3 us
  transfers between devices with their start and end apart: 24, of which 12 were waited for; matrix products, arithmetic and copies ran while one was open for 11% of the time, Pallas kernels for 37%

profile of v5, /device:TPU:0, one launch (start us, length us, event | category | flops | bytes accessed | tf_op | source)
XLA Modules:
  0.0 454.1 jit_solution(17475611506832710513)
XLA Ops:
  7.2 1.1 constant_dynamic-slice_fusion.19
  8.4 1.0 constant_dynamic-slice_fusion.18
  10.4 1.6 copy.50
  15.6 1.3 constant_dynamic-update-slice_fusion.3
  16.9 1.3 constant_dynamic-update-slice_fusion.2
  19.5 5.1 %collective-permute-start.2 = (bf16[768,256]{1,0:T(8,128)(2,1)}, bf16[768,256]{1,0:T(8,128)(2,1)}, u32[]{:S(2)}, u32[]{:S(2)}) collective-permute-start(bf16[768,256]{1,0:T(8,128)(2,1)} %constant_dynamic-update-slice_fusion), channel_id=1, source_target_pairs={{0,3},{1,0},{2,1},{3,2},{4,7},{5,4},{6,5},{7,6},{8,11},{9,8},{10,9... | collective-permute-start | bytes 1179656 | tf_op jit(solution)/shard_map/ppermute | solution.py:788
  24.6 1.0 collective-permute-start
  28.9 4.7 %roll_rows.5.c_ref = f32[512,1024]{1,0:T(8,128)} custom-call(s32[3]{0:T(128)} %add_add_fusion.2.scalar_ref, bf16[2048,1024]{1,0:T(8,128)(2,1)} %refs_0_.3), custom_call_target="tpu_custom_call" | custom-call | flops 268435456 | bytes 6291456 | tf_op jit(solution)/shard_map/roll_rows/pallas_call | solution.py:71
  33.5 4.9 %roll_rows.4.x_ref = bf16[1024,1024]{1,0:T(8,128)(2,1)} custom-call(s32[3]{0:T(128)} %add_add_fusion.1.scalar_ref, bf16[2048,1024]{1,0:T(8,128)(2,1)} %refs_0_.2), custom_call_target="tpu_custom_call" | custom-call | flops 536870912 | bytes 8388608 | tf_op jit(solution)/shard_map/roll_rows/pallas_call | solution.py:71
  38.6 1.4 dynamic-slice_bitcast_fusion.6.b_ref.rest_7_
  39.9 1.5 dynamic-slice_bitcast_fusion.5.rest_1_.db_ref
  41.4 26.4 %collective-permute-done = bf16[768,256]{1,0:T(8,128)(2,1)} collective-permute-done((bf16[768,256]{1,0:T(8,128)(2,1)}, bf16[768,256]{1,0:T(8,128)(2,1)}, u32[]{:S(2)}, u32[]{:S(2)}) %collective-permute-start) | collective-permute-done | bytes 393248 | tf_op jit(solution)/shard_map/ppermute | solution.py:788
  68.8 6.4 %collective-permute-done.1 = bf16[768,256]{1,0:T(8,128)(2,1)} collective-permute-done((bf16[768,256]{1,0:T(8,128)(2,1)}, bf16[768,256]{1,0:T(8,128)(2,1)}, u32[]{:S(2)}, u32[]{:S(2)}) %collective-permute-start.1) | collective-permute-done | bytes 393248 | tf_op jit(solution)/shard_map/ppermute | solution.py:788
  78.2 1.5 collective-permute-start.3
  79.7 1.5 collective-permute-start.4
  81.8 1.0 copy.54.all_ref
  82.8 1.5 dynamic-slice_bitcast_fusion.4.f_ref.rest_1_
  85.8 28.9 %collective-permute-done.3 = bf16[1536,256]{1,0:T(8,128)(2,1)} collective-permute-done((bf16[1536,256]{1,0:T(8,128)(2,1)}, bf16[1536,256]{1,0:T(8,128)(2,1)}, u32[]{:S(2)}, u32[]{:S(2)}) %collective-permute-start.3) | collective-permute-done | bytes 786464 | tf_op jit(solution)/shard_map/ppermute | solution.py:792
  114.8 1.0 slice.108
  115.8 1.5 collective-permute-start.5
  117.3 1.0 slice.109
  120.1 5.4 %collective-permute-done.5 = bf16[768,256]{1,0:T(8,128)(2,1)S(1)} collective-permute-done((bf16[768,256]{1,0:T(8,128)(2,1)S(1)}, bf16[768,256]{1,0:T(8,128)(2,1)S(1)}, u32[]{:S(2)}, u32[]{:S(2)}) %collective-permute-start.5) | collective-permute-done | bytes 393248 | tf_op jit(solution)/shard_map/ppermute | solution.py:798
  125.5 2.4 collective-permute-done.6
  127.9 3.3 pad_maximum_fusion.near_ref
  132.2 1.1 constant_dynamic-slice_fusion.8
  133.3 1.0 constant_dynamic-slice_fusion.17.o_ref.x_ref
  134.3 1.5 pad_maximum_fusion.1.own_ref
  136.5 1.0 slice_bitcast_fusion
  137.5 1.0 slice_bitcast_fusion.1
  142.5 8.5 %shard_map.294 = (bf16[4,3,1024,256]{3,2,1,0:T(8,128)(2,1)}, bf16[1024,1024]{1,0:T(8,128)(2,1)}) custom-call(s32[3]{0:T(128)} %pad_add_fusion.scalar_ref, bf16[8,512,256]{2,1,0:T(8,128)(2,1)} %pad_maximum_fusion.1.own_ref, bf16[4,3,512,256]{3,2,1,0:T(8,128)(2,1)} %pad_maximum_fusion.near_ref, bf16[4,3,512,256]{3,2,1,0:T(8,128)(2,1)} %collective-permute-done.7.far_ref), custom_call_target="tpu_custom_call" | custom-call | bytes 16777216 | tf_op jit(solution)/shard_map/pallas_call | solution.py:838
  150.9 12.0 %project_qkv.1 = (bf16[512,1024]{1,0:T(8,128)(2,1)}, bf16[1024,1024]{1,0:T(8,128)(2,1)}, bf16[1024,1024]{1,0:T(8,128)(2,1)}) custom-call(bf16[1024,1024]{1,0:T(8,128)(2,1)} %roll_rows.4.x_ref, bf16[512,1024]{1,0:T(8,128)(2,1)} %constant_dynamic-slice_fusion.17.o_ref.x_ref, bf16[4,3,1024,256]{3,2,1,0:T(8,128)(2,1)} %get-tuple-element.84.w_ref, ...), custom_call_target="tpu_custom_call" | custom-call | flops 5368709120 | bytes 20971520 | tf_op jit(solution)/shard_map/project_qkv/pallas_call | solution.py:127
  162.9 17.9 %attend.1 = (bf16[512,1024]{1,0:T(8,128)(2,1)}, f32[8,8,512]{2,1,0:T(8,128)}) custom-call(bf16[512,1024]{1,0:T(8,128)(2,1)} %get-tuple-element.85.q_ref, bf16[1024,1024]{1,0:T(8,128)(2,1)} %get-tuple-element.86.k_ref, bf16[1024,1024]{1,0:T(8,128)(2,1)} %get-tuple-element.87.v_ref, s32[1,512]{1,0:T(1,128)} %bitcast.112, s32[1024,1]{1,0:T(8,128)} %copy.54.all_ref), custom_call_target="tpu_custom_call" | custom-call | flops 8589934592 | bytes 6291456 | tf_op jit(solution)/shard_map/attend/pallas_call | solution.py:191
  180.8 6.8 %out_forward.1 = (f32[512,1024]{1,0:T(8,128)}, bf16[512,1024]{1,0:T(8,128)(2,1)}, f32[512,1024]{1,0:T(8,128)}, f32[512,1]{1,0:T(8,128)}, bf16[512,16]{1,0:T(8,128)(2,1)}, /*index=5*/bf16[512,32]{1,0:T(8,128)(2,1)}) custom-call(bf16[512,1024]{1,0:T(8,128)(2,1)} %get-tuple-element.88.m_ref.rest_9_, bf16[1024,1024]{1,0:T(8,128)(2,1)} %get-tuple-element.89.w_ref.rest_10_, ...), custom_call_target="tpu_custom_call" | custom-call | flops 1073741824 | bytes 9437184 | tf_op jit(solution)/shard_map/out_forward/pallas_call | solution.py:426
  188.4 9.2 %ffn_forward.2 = (bf16[2,512,4096]{2,1,0:T(8,128)(2,1)}, f32[512,1024]{1,0:T(8,128)}, f32[512,16]{1,0:T(8,128)}) custom-call(s32[1]{0:T(128)} %bitcast.2.place_ref, bf16[1,2,1024,1024]{3,2,1,0:T(8,128)(2,1)} %bitcast.107, bf16[1,1024,1024]{2,1,0:T(8,128)(2,1)} %bitcast.110, bf16[512,1024]{1,0:T(8,128)(2,1)} %get-tuple-element.90.hb_ref.rest_2_, ...), custom_call_target="tpu_custom_call" | custom-call | flops 3221225472 | bytes 8388608 | tf_op jit(solution)/shard_map/ffn_forward/pallas_call | solution.py:593
  197.6 13.4 %all-gather.6.cloned.1.call-done = bf16[12288,1024]{1,0:T(8,128)(2,1)} async-done(((bf16[384,1024]{1,0:T(8,128)(2,1)}), bf16[12288,1024]{1,0:T(8,128)(2,1)}) %all-gather.6.cloned.1.call-update) | async-done | bytes 25165840 | tf_op jit(solution)/shard_map/all_gather | solution.py:774
  211.0 19.9 %ffn_forward.3 = (bf16[2,512,4096]{2,1,0:T(8,128)(2,1)}, bf16[512,1024]{1,0:T(8,128)(2,1)}, f32[512,1024]{1,0:T(8,128)}, bf16[512,16]{1,0:T(8,128)(2,1)}) custom-call(s32[1]{0:T(128)} %bitcast.2.place_ref, bf16[4,8,384,1024]{3,2,1,0:T(8,128)(2,1)} %bitcast.87, bf16[4,8,384,1024]{3,2,1,0:T(8,128)(2,1)} %bitcast.88, ...), custom_call_target="tpu_custom_call", output_to_operand_aliasing={{0}: (9, {})} | custom-call | flops 9663676416 | bytes 25165824 | tf_op jit(solution)/shard_map/ffn_forward/pallas_call | solution.py:593
  233.0 37.5 %ffn_backward.1 = (bf16[4,48,1024]{2,1,0:T(8,128)(2,1)}, f32[512,1024]{1,0:T(8,128)}, bf16[512,1024]{1,0:T(8,128)(2,1)}, bf16[80,1024]{1,0:T(8,128)(2,1)}) custom-call(s32[1]{0:T(128)} %bitcast.2.place_ref, bf16[4,8,384,1024]{3,2,1,0:T(8,128)(2,1)} %bitcast.89, bf16[4,8,384,1024]{3,2,1,0:T(8,128)(2,1)} %bitcast.90, f32[512,1024]{1,0:T(8,128)} %get-tuple-element.97.sums_ref, ...), custom_call_target="tpu_custom_call" | custom-call | flops 12884901888 | bytes 33554432 | tf_op jit(solution)/shard_map/ffn_backward/pallas_call | solution.py:705
  270.4 16.6 %attend_back.2 = (f32[512,1024]{1,0:T(8,128)}, bf16[512,1024]{1,0:T(8,128)(2,1)}, bf16[512,1024]{1,0:T(8,128)(2,1)}) custom-call(s32[1]{0:T(128)} %bitcast.43.block_ref, bf16[512,1024]{1,0:T(8,128)(2,1)} %get-tuple-element.85.q_ref, bf16[1024,1024]{1,0:T(8,128)(2,1)} %get-tuple-element.86.k_ref, bf16[1024,1024]{1,0:T(8,128)(2,1)} %get-tuple-element.87.v_ref, ...), custom_call_target="tpu_custom_call" | custom-call | flops 10737418240 | bytes 9437184 | tf_op jit(solution)/shard_map/attend_back/pallas_call | solution.py:287
  287.1 8.6 %project_back.2 = (bf16[512,1024]{1,0:T(8,128)(2,1)}, f32[32,1024]{1,0:T(8,128)}, f32[4,32,256]{2,1,0:T(8,128)}) custom-call(s32[1]{0:T(128)} %bitcast.43.block_ref, bf16[4,3,1024,256]{3,2,1,0:T(8,128)(2,1)} %get-tuple-element.84.w_ref, bf16[48,1024]{1,0:T(8,128)(2,1)} %bitcast.100, bf16[48,1024]{1,0:T(8,128)(2,1)} %copy-done.12, ...), custom_call_target="tpu_custom_call" | custom-call | flops 2147483648 | bytes 12582912 | tf_op jit(solution)/shard_map/project_back/pallas_call | solution.py:375
  296.7 2.0 collective-permute-start.9
  298.7 1.3 collective-permute-start.10
  300.0 1.1 collective-permute-start.11
  301.1 18.3 %attend_back.3 = (bf16[512,1024]{1,0:T(8,128)(2,1)}, bf16[512,1024]{1,0:T(8,128)(2,1)}, bf16[512,1024]{1,0:T(8,128)(2,1)}) custom-call(s32[1]{0:T(128)} %bitcast.42.block_ref, bf16[512,1024]{1,0:T(8,128)(2,1)} %get-tuple-element.85.q_ref, bf16[1024,1024]{1,0:T(8,128)(2,1)} %get-tuple-element.86.k_ref, bf16[1024,1024]{1,0:T(8,128)(2,1)} %get-tuple-element.87.v_ref, ...), custom_call_target="tpu_custom_call" | custom-call | flops 10737418240 | bytes 9437184 | tf_op jit(solution)/shard_map/attend_back/pallas_call | solution.py:287
  319.4 10.7 %project_back.3 = (f32[512,1024]{1,0:T(8,128)}, bf16[48,1024]{1,0:T(8,128)(2,1)}, bf16[4,48,256]{2,1,0:T(8,128)(2,1)}) custom-call(s32[1]{0:T(128)} %bitcast.42.block_ref, bf16[4,3,1024,256]{3,2,1,0:T(8,128)(2,1)} %get-tuple-element.84.w_ref, bf16[48,1024]{1,0:T(8,128)(2,1)} %bitcast.101, bf16[48,1024]{1,0:T(8,128)(2,1)} %copy-done.12, ...), custom_call_target="tpu_custom_call" | custom-call | flops 3221225472 | bytes 13631488 | tf_op jit(solution)/shard_map/project_back/pallas_call | solution.py:375
  331.0 1.7 pad_maximum_fusion.13
  333.6 7.8 %collective-permute-done.8 = bf16[512,1024]{1,0:T(8,128)(2,1)S(1)} collective-permute-done((bf16[512,1024]{1,0:T(8,128)(2,1)}, bf16[512,1024]{1,0:T(8,128)(2,1)S(1)}, u32[]{:S(2)}, u32[]{:S(2)}) %collective-permute-start.8) | collective-permute-done | bytes 1048608 | tf_op jit(solution)/shard_map/ppermute | solution.py:1124
  341.5 2.4 collective-permute-start.14
  343.8 1.9 add_convert_fusion.refs_0_
  345.8 5.8 %roll_rows.6 = bf16[2048,1024]{1,0:T(8,128)(2,1)} custom-call(s32[3]{0:T(128)} %add_add_fusion.scalar_ref, bf16[2048,1024]{1,0:T(8,128)(2,1)} %all-gather.8.cloned.1.call-done.refs_0_), custom_call_target="tpu_custom_call" | custom-call | flops 1073741824 | bytes 12582912 | tf_op jit(solution)/shard_map/roll_rows/pallas_call | solution.py:71
  351.6 1.0 collective-permute-done.11
  352.7 2.8 collective-permute-done.14
  355.5 1.1 add_convert_fusion.1
  356.6 1.0 add_convert_fusion.2
  358.4 1.3 collective-permute-start.16
  359.7 4.6 %collective-permute-start.15 = (bf16[512,1024]{1,0:T(8,128)(2,1)S(1)}, bf16[512,1024]{1,0:T(8,128)(2,1)S(1)}, u32[]{:S(2)}, u32[]{:S(2)}) collective-permute-start(bf16[512,1024]{1,0:T(8,128)(2,1)S(1)} %add_convert_fusion.refs_0_), channel_id=1, source_target_pairs={{0,1},{1,2},{2,3},{4,5},{5,6},{6,7},{8,9},{9,10},{10,11},{12,13},{... | collective-permute-start | bytes 3145736 | tf_op jit(solution)/shard_map/ppermute | solution.py:915
  364.4 21.0 %collective-permute-done.16.refs_2_ = bf16[512,1024]{1,0:T(8,128)(2,1)S(1)} collective-permute-done((bf16[512,1024]{1,0:T(8,128)(2,1)S(1)}, bf16[512,1024]{1,0:T(8,128)(2,1)S(1)}, u32[]{:S(2)}, u32[]{:S(2)}) %collective-permute-start.16) | collective-permute-done | bytes 1048608 | tf_op jit(solution)/shard_map/ppermute | solution.py:916
  385.4 1.3 collective-permute-start.18
  387.4 24.2 %collective-permute-done.18.refs_4_ = bf16[512,1024]{1,0:T(8,128)(2,1)} collective-permute-done((bf16[512,1024]{1,0:T(8,128)(2,1)S(1)}, bf16[512,1024]{1,0:T(8,128)(2,1)}, u32[]{:S(2)}, u32[]{:S(2)}) %collective-permute-start.18) | collective-permute-done | bytes 1048608 | tf_op jit(solution)/shard_map/ppermute | solution.py:916
  411.7 1.3 collective-permute-start.20
  413.0 1.7 collective-permute-start.19
  416.1 7.0 %place_sums.1 = (f32[8,16,1024]{2,1,0:T(8,128)}, f32[8,32,1024]{2,1,0:T(8,128)}, f32[8,16,1024]{2,1,0:T(8,128)}, f32[8,16,256]{2,1,0:T(8,128)}, f32[8,16,1024]{2...) custom-call(s32[9]{0:T(128)} %pad_add_fusion.1.scalar_ref, ...), custom_call_target="tpu_custom_call" | custom-call | flops 1540096 | bytes 9240576 | tf_op jit(solution)/shard_map/place_sums/pallas_call | solution.py:951
  423.1 14.3 %collective-permute-done.20.refs_6_ = bf16[512,1024]{1,0:T(8,128)(2,1)} collective-permute-done((bf16[512,1024]{1,0:T(8,128)(2,1)}, bf16[512,1024]{1,0:T(8,128)(2,1)}, u32[]{:S(2)}, u32[]{:S(2)}) %collective-permute-start.20) | collective-permute-done | bytes 1048608 | tf_op jit(solution)/shard_map/ppermute | solution.py:916
  437.3 1.9 reshape.178
  439.2 8.4 %roll_rows.7 = f32[2048,1024]{1,0:T(8,128)} custom-call(s32[3]{0:T(128)} %add_add_fusion.scalar_ref, bf16[512,1024]{1,0:T(8,128)(2,1)} %copy-done.5, bf16[512,1024]{1,0:T(8,128)(2,1)} %copy-done.10, bf16[512,1024]{1,0:T(8,128)(2,1)} %copy-done.9, bf16[512,1024]{1,0:T(8,128)(2,1)} %copy-done.11, bf16[512,1024]{1,0:T(8,128)(2,1)} %collective-permute-done.18.refs_4_, ...), custom_call_target="tpu_custom_call" | custom-call | flops 1073741824 | bytes 12582912 | tf_op jit(solution)/shard_map/roll_rows/pallas_call | solution.py:71
  (139 shorter events, 28.4 us)
Async XLA Ops:
  7.2 77.1 %copy-start = (bf16[8,48,1024]{2,1,0:T(8,128)(2,1)S(1)}, bf16[8,48,1024]{2,1,0:T(8,128)(2,1)}, u32[]{:S(2)}) copy-start(bf16[8,48,1024]{2,1,0:T(8,128)(2,1)} %param.35) | copy-start | bytes 2359300
  7.2 203.8 %all-gather.6.cloned.1.call-start = ((), (), s32[]{:S(2)}) async-start(), calls=%async_computation | async-start | bytes 25952256 | tf_op jit(solution)/shard_map/all_gather | solution.py:774
  10.3 1.6 copy-start.14
  10.3 335.5 %all-gather.8.cloned.1.call-start = ((), (), s32[]{:S(2)}) async-start(), calls=%async_computation.1 | async-start | bytes 5242880 | tf_op jit(solution)/shard_map/all_gather | solution.py:1097
  12.0 3.6 copy-start.3
  12.3 13.2 %copy-start.19 = (s32[1,2048]{1,0:T(1,128)S(1)}, s32[1,2048]{1,0:T(1,128)}, u32[]{:S(2)}) copy-start(s32[1,2048]{1,0:T(1,128)} %param.27) | copy-start | bytes 24580
  19.5 56.8 %collective-permute-start.2 = (bf16[768,256]{1,0:T(8,128)(2,1)}, bf16[768,256]{1,0:T(8,128)(2,1)}, u32[]{:S(2)}, u32[]{:S(2)}) collective-permute-start(bf16[768,256]{1,0:T(8,128)(2,1)} %constant_dynamic-update-slice_fusion), channel_id=1, source_target_pairs={{0,3},{1,0},{2,1},{3,2},{4,7},{5,4},{6,5},{7,6},{8,11},{9,8},{10,9... | collective-permute-start | bytes 1179656 | tf_op jit(solution)/shard_map/ppermute | solution.py:788
  24.6 50.7 %collective-permute-start.1 = (bf16[768,256]{1,0:T(8,128)(2,1)}, bf16[768,256]{1,0:T(8,128)(2,1)}, u32[]{:S(2)}, u32[]{:S(2)}) collective-permute-start(bf16[768,256]{1,0:T(8,128)(2,1)} %constant_dynamic-update-slice_fusion), channel_id=1, source_target_pairs={{0,2},{1,3},{2,0},{3,1},{4,6},{5,7},{6,4},{7,5},{8,10},{9,11},{10,... | collective-permute-start | bytes 1179656 | tf_op jit(solution)/shard_map/ppermute | solution.py:788
  24.6 43.3 %collective-permute-start = (bf16[768,256]{1,0:T(8,128)(2,1)}, bf16[768,256]{1,0:T(8,128)(2,1)}, u32[]{:S(2)}, u32[]{:S(2)}) collective-permute-start(bf16[768,256]{1,0:T(8,128)(2,1)} %constant_dynamic-update-slice_fusion), channel_id=1, source_target_pairs={{0,1},{1,2},{2,3},{3,0},{4,5},{5,6},{6,7},{7,4},{8,9},{9,10},{10,1... | collective-permute-start | bytes 1179656 | tf_op jit(solution)/shard_map/ppermute | solution.py:788
  39.9 44.4 %copy-start.2 = (bf16[1024,1024]{1,0:T(8,128)(2,1)S(1)}, bf16[1024,1024]{1,0:T(8,128)(2,1)}, u32[]{:S(2)}) copy-start(bf16[1024,1024]{1,0:T(8,128)(2,1)} %roll_rows.4.x_ref) | copy-start | bytes 6291460
  78.2 36.6 %collective-permute-start.3 = (bf16[1536,256]{1,0:T(8,128)(2,1)}, bf16[1536,256]{1,0:T(8,128)(2,1)}, u32[]{:S(2)}, u32[]{:S(2)}) collective-permute-start(bf16[1536,256]{1,0:T(8,128)(2,1)} %pad_maximum_fusion.3), channel_id=1, source_target_pairs={{0,8},{8,0},{16,24},{24,16},{1,9},{9,1},{17,25},{25,17},{2,10},{10... | collective-permute-start | bytes 2359304 | tf_op jit(solution)/shard_map/ppermute | solution.py:792
  79.7 37.7 %collective-permute-start.4 = (bf16[1536,256]{1,0:T(8,128)(2,1)}, bf16[1536,256]{1,0:T(8,128)(2,1)}, u32[]{:S(2)}, u32[]{:S(2)}) collective-permute-start(bf16[1536,256]{1,0:T(8,128)(2,1)} %pad_maximum_fusion.3), channel_id=1, source_target_pairs={{0,16},{8,24},{16,0},{24,8},{1,17},{9,25},{17,1},{25,9},{2,18},{10... | collective-permute-start | bytes 2359304 | tf_op jit(solution)/shard_map/ppermute | solution.py:792
  84.3 34.0 %copy-start.12 = (bf16[48,1024]{1,0:T(8,128)(2,1)}, bf16[48,1024]{1,0:T(8,128)(2,1)S(1)}, u32[]{:S(2)}) copy-start(bf16[48,1024]{1,0:T(8,128)(2,1)S(1)} %dynamic-slice_bitcast_fusion.3.a_ref) | copy-start | bytes 294916
  84.3 35.3 %copy-start.20 = (f32[64,128]{1,0:T(8,128)S(1)}, f32[64,128]{1,0:T(8,128)}, u32[]{:S(2)}) copy-start(f32[64,128]{1,0:T(8,128)} %constant.239.clone) | copy-start | bytes 98308
  84.3 35.3 %copy-start.21 = (f32[64,128]{1,0:T(8,128)S(1)}, f32[64,128]{1,0:T(8,128)}, u32[]{:S(2)}) copy-start(f32[64,128]{1,0:T(8,128)} %constant.240.clone) | copy-start | bytes 98308
  84.3 35.3 %copy-start.22 = (f32[48,128]{1,0:T(8,128)S(1)}, f32[48,128]{1,0:T(8,128)}, u32[]{:S(2)}) copy-start(f32[48,128]{1,0:T(8,128)} %constant.237.clone) | copy-start | bytes 73732
  84.4 35.2 %copy-start.23 = (f32[48,128]{1,0:T(8,128)S(1)}, f32[48,128]{1,0:T(8,128)}, u32[]{:S(2)}) copy-start(f32[48,128]{1,0:T(8,128)} %constant.238.clone) | copy-start | bytes 73732
  85.1 35.0 %copy-start.7 = (bf16[1024,48]{1,0:T(8,128)(2,1)}, bf16[1024,48]{1,0:T(8,128)(2,1)S(1)}, u32[]{:S(2)}) copy-start(bf16[1024,48]{1,0:T(8,128)(2,1)S(1)} %convolution_convert_fusion.l_ref) | copy-start | bytes 294916
  115.8 9.7 %collective-permute-start.5 = (bf16[768,256]{1,0:T(8,128)(2,1)S(1)}, bf16[768,256]{1,0:T(8,128)(2,1)S(1)}, u32[]{:S(2)}, u32[]{:S(2)}) collective-permute-start(bf16[768,256]{1,0:T(8,128)(2,1)S(1)} %slice.108), channel_id=1, source_target_pairs={{0,16},{8,24},{16,0},{24,8},{1,17},{9,25},{17,1},{25,9},{2,18},{10... | collective-permute-start | bytes 1179656 | tf_op jit(solution)/shard_map/ppermute | solution.py:798
  118.4 9.5 %collective-permute-start.6 = (bf16[768,256]{1,0:T(8,128)(2,1)S(1)}, bf16[768,256]{1,0:T(8,128)(2,1)S(1)}, u32[]{:S(2)}, u32[]{:S(2)}) collective-permute-start(bf16[768,256]{1,0:T(8,128)(2,1)S(1)} %slice.109), channel_id=1, source_target_pairs={{0,8},{8,0},{16,24},{24,16},{1,9},{9,1},{17,25},{25,17},{2,10},{10... | collective-permute-start | bytes 1179656 | tf_op jit(solution)/shard_map/ppermute | solution.py:799
  127.9 3.3 copy-start.26
  131.2 11.2 %collective-permute-start.7 = (bf16[4,3,512,256]{3,2,1,0:T(8,128)(2,1)}, bf16[4,3,512,256]{3,2,1,0:T(8,128)(2,1)}, u32[]{:S(2)}, u32[]{:S(2)}) collective-permute-start(bf16[4,3,512,256]{3,2,1,0:T(8,128)(2,1)} %pad_maximum_fusion.near_ref), channel_id=1, source_target_pairs={{0,4},{4,0},{1,5},{5,1},{2,6},{6,2},{3,7},{7,3},{8,12},{12,8},{9,1... | collective-permute-start | bytes 9437192 | tf_op jit(solution)/shard_map/ppermute | solution.py:804
  132.2 2.1 copy-start.4
  134.3 1.5 copy-start.24
  134.3 1.5 copy-start.25
  139.6 11.3 %copy-start.8 = (bf16[4,16,1024]{2,1,0:T(8,128)(2,1)}, bf16[4,16,1024]{2,1,0:T(8,128)(2,1)S(1)}, u32[]{:S(2)}) copy-start(bf16[4,16,1024]{2,1,0:T(8,128)(2,1)S(1)} %reshape.171.da_ref) | copy-start | bytes 393220
  139.9 11.1 %copy-start.6 = (bf16[4,32,1024]{2,1,0:T(8,128)(2,1)}, bf16[4,32,1024]{2,1,0:T(8,128)(2,1)S(1)}, u32[]{:S(2)}) copy-start(bf16[4,32,1024]{2,1,0:T(8,128)(2,1)S(1)} %reshape.170.fb_ref) | copy-start | bytes 786436
  230.9 183.7 %all-gather.10.cloned.1.call-start = ((), (), s32[]{:S(2)}) async-start(), calls=%async_computation.2 | async-start | bytes 3833856 | tf_op jit(solution)/shard_map/all_gather | solution.py:1156
  287.1 8.7 %copy-start.16 = (bf16[4,48,1024]{2,1,0:T(8,128)(2,1)S(1)}, bf16[4,48,1024]{2,1,0:T(8,128)(2,1)}, u32[]{:S(2)}) copy-start(bf16[4,48,1024]{2,1,0:T(8,128)(2,1)} %get-tuple-element.120) | copy-start | bytes 1179652
  287.1 8.7 %copy-start.13 = (bf16[80,1024]{1,0:T(8,128)(2,1)S(1)}, bf16[80,1024]{1,0:T(8,128)(2,1)}, u32[]{:S(2)}) copy-start(bf16[80,1024]{1,0:T(8,128)(2,1)} %get-tuple-element.119) | copy-start | bytes 491524
  295.7 45.7 %collective-permute-start.8 = (bf16[512,1024]{1,0:T(8,128)(2,1)}, bf16[512,1024]{1,0:T(8,128)(2,1)S(1)}, u32[]{:S(2)}, u32[]{:S(2)}) collective-permute-start(bf16[512,1024]{1,0:T(8,128)(2,1)} %get-tuple-element.115), channel_id=1, source_target_pairs={{0,1},{1,0},{2,3},{3,2},{4,5},{5,4},{6,7},{7,6},{8,9},{9,8},{10,11... | collective-permute-start | bytes 3145736 | tf_op jit(solution)/shard_map/ppermute | solution.py:1124
  296.7 44.8 %collective-permute-start.9 = (bf16[128,1024]{1,0:T(8,128)(2,1)S(1)}, bf16[128,1024]{1,0:T(8,128)(2,1)S(1)}, u32[]{:S(2)}, u32[]{:S(2)}) collective-permute-start(bf16[128,1024]{1,0:T(8,128)(2,1)S(1)} %get-tuple-element.156), channel_id=1, source_target_pairs={{0,1},{1,2},{2,3},{3,0},{4,5},{5,6},{6,7},{7,4},{8,9},{9,10},{10,1... | collective-permute-start | bytes 786440 | tf_op jit(solution)/shard_map/ppermute | solution.py:898
  298.7 52.9 %collective-permute-start.10 = (bf16[128,1024]{1,0:T(8,128)(2,1)}, bf16[128,1024]{1,0:T(8,128)(2,1)S(1)}, u32[]{:S(2)}, u32[]{:S(2)}) collective-permute-start(bf16[128,1024]{1,0:T(8,128)(2,1)} %get-tuple-element.157), channel_id=1, source_target_pairs={{0,2},{1,3},{2,0},{3,1},{4,6},{5,7},{6,4},{7,5},{8,10},{9,11},{10,... | collective-permute-start | bytes 786440 | tf_op jit(solution)/shard_map/ppermute | solution.py:898
  300.0 52.7 %collective-permute-start.11 = (bf16[128,1024]{1,0:T(8,128)(2,1)}, bf16[128,1024]{1,0:T(8,128)(2,1)S(1)}, u32[]{:S(2)}, u32[]{:S(2)}) collective-permute-start(bf16[128,1024]{1,0:T(8,128)(2,1)} %get-tuple-element.158), channel_id=1, source_target_pairs={{0,3},{1,0},{2,1},{3,2},{4,7},{5,4},{6,5},{7,6},{8,11},{9,8},{10,9... | collective-permute-start | bytes 786440 | tf_op jit(solution)/shard_map/ppermute | solution.py:898
  332.7 20.0 %collective-permute-start.12 = (bf16[60,1024]{1,0:T(8,128)(2,1)}, bf16[60,1024]{1,0:T(8,128)(2,1)S(1)}, u32[]{:S(2)}, u32[]{:S(2)}) collective-permute-start(bf16[60,1024]{1,0:T(8,128)(2,1)} %get-tuple-element.165), channel_id=1, source_target_pairs={{0,1},{1,2},{2,3},{3,0},{4,5},{5,6},{6,7},{7,4},{8,9},{9,10},{10,1... | collective-permute-start | bytes 368648 | tf_op jit(solution)/shard_map/ppermute | solution.py:898
  341.4 11.2 %collective-permute-start.13 = (bf16[60,1024]{1,0:T(8,128)(2,1)}, bf16[60,1024]{1,0:T(8,128)(2,1)S(1)}, u32[]{:S(2)}, u32[]{:S(2)}) collective-permute-start(bf16[60,1024]{1,0:T(8,128)(2,1)} %get-tuple-element.166), channel_id=1, source_target_pairs={{0,2},{1,3},{2,0},{3,1},{4,6},{5,7},{6,4},{7,5},{8,10},{9,11},{10,... | collective-permute-start | bytes 368648 | tf_op jit(solution)/shard_map/ppermute | solution.py:898
  341.5 14.0 %collective-permute-start.14 = (bf16[60,1024]{1,0:T(8,128)(2,1)}, bf16[60,1024]{1,0:T(8,128)(2,1)}, u32[]{:S(2)}, u32[]{:S(2)}) collective-permute-start(bf16[60,1024]{1,0:T(8,128)(2,1)} %get-tuple-element.167), channel_id=1, source_target_pairs={{0,3},{1,0},{2,1},{3,2},{4,7},{5,4},{6,5},{7,6},{8,11},{9,8},{10,9... | collective-permute-start | bytes 368648 | tf_op jit(solution)/shard_map/ppermute | solution.py:898
  345.8 13.9 %copy-start.5 = (bf16[512,1024]{1,0:T(8,128)(2,1)}, bf16[512,1024]{1,0:T(8,128)(2,1)S(1)}, u32[]{:S(2)}) copy-start(bf16[512,1024]{1,0:T(8,128)(2,1)S(1)} %add_convert_fusion.refs_0_) | copy-start | bytes 3145732
  345.8 10.8 %copy-start.15 = (bf16[48,1024]{1,0:T(8,128)(2,1)S(1)}, bf16[48,1024]{1,0:T(8,128)(2,1)}, u32[]{:S(2)}) copy-start(bf16[48,1024]{1,0:T(8,128)(2,1)} %get-tuple-element.124) | copy-start | bytes 294916
  345.8 11.8 %copy-start.18 = (bf16[16,1024]{1,0:T(8,128)(2,1)S(1)}, bf16[16,1024]{1,0:T(8,128)(2,1)}, u32[]{:S(2)}) copy-start(bf16[16,1024]{1,0:T(8,128)(2,1)} %pad_convert_fusion) | copy-start | bytes 98308
  352.7 2.8 copy-start.17
  358.4 26.9 %collective-permute-start.16 = (bf16[512,1024]{1,0:T(8,128)(2,1)S(1)}, bf16[512,1024]{1,0:T(8,128)(2,1)S(1)}, u32[]{:S(2)}, u32[]{:S(2)}) collective-permute-start(bf16[512,1024]{1,0:T(8,128)(2,1)S(1)} %add_convert_fusion.refs_0_), channel_id=1, source_target_pairs={{3,2},{2,1},{1,0},{7,6},{6,5},{5,4},{11,10},{10,9},{9,8},{15,14},{... | collective-permute-start | bytes 3145736 | tf_op jit(solution)/shard_map/ppermute | solution.py:916
  359.7 26.9 %collective-permute-start.15 = (bf16[512,1024]{1,0:T(8,128)(2,1)S(1)}, bf16[512,1024]{1,0:T(8,128)(2,1)S(1)}, u32[]{:S(2)}, u32[]{:S(2)}) collective-permute-start(bf16[512,1024]{1,0:T(8,128)(2,1)S(1)} %add_convert_fusion.refs_0_), channel_id=1, source_target_pairs={{0,1},{1,2},{2,3},{4,5},{5,6},{6,7},{8,9},{9,10},{10,11},{12,13},{... | collective-permute-start | bytes 3145736 | tf_op jit(solution)/shard_map/ppermute | solution.py:915
  385.4 53.9 %copy-start.9 = (bf16[512,1024]{1,0:T(8,128)(2,1)}, bf16[512,1024]{1,0:T(8,128)(2,1)S(1)}, u32[]{:S(2)}) copy-start(bf16[512,1024]{1,0:T(8,128)(2,1)S(1)} %collective-permute-done.16.refs_2_) | copy-start | bytes 3145732
  385.4 26.3 %collective-permute-start.18 = (bf16[512,1024]{1,0:T(8,128)(2,1)S(1)}, bf16[512,1024]{1,0:T(8,128)(2,1)}, u32[]{:S(2)}, u32[]{:S(2)}) collective-permute-start(bf16[512,1024]{1,0:T(8,128)(2,1)S(1)} %collective-permute-done.16.refs_2_), channel_id=1, source_target_pairs={{2,1},{1,0},{6,5},{5,4},{10,9},{9,8},{14,13},{13,12},{18,17},{17,1... | collective-permute-start | bytes 3145736 | tf_op jit(solution)/shard_map/ppermute | solution.py:916
  386.7 25.0 %copy-start.10 = (bf16[512,1024]{1,0:T(8,128)(2,1)}, bf16[512,1024]{1,0:T(8,128)(2,1)S(1)}, u32[]{:S(2)}) copy-start(bf16[512,1024]{1,0:T(8,128)(2,1)S(1)} %collective-permute-done.15.refs_1_) | copy-start | bytes 3145732
  386.7 26.3 %collective-permute-start.17 = (bf16[512,1024]{1,0:T(8,128)(2,1)S(1)}, bf16[512,1024]{1,0:T(8,128)(2,1)S(1)}, u32[]{:S(2)}, u32[]{:S(2)}) collective-permute-start(bf16[512,1024]{1,0:T(8,128)(2,1)S(1)} %collective-permute-done.15.refs_1_), channel_id=1, source_target_pairs={{1,2},{2,3},{5,6},{6,7},{9,10},{10,11},{13,14},{14,15},{17,18},{18... | collective-permute-start | bytes 3145736 | tf_op jit(solution)/shard_map/ppermute | solution.py:915
  411.7 25.6 %collective-permute-start.20 = (bf16[512,1024]{1,0:T(8,128)(2,1)}, bf16[512,1024]{1,0:T(8,128)(2,1)}, u32[]{:S(2)}, u32[]{:S(2)}) collective-permute-start(bf16[512,1024]{1,0:T(8,128)(2,1)} %collective-permute-done.18.refs_4_), channel_id=1, source_target_pairs={{1,0},{5,4},{9,8},{13,12},{17,16},{21,20},{25,24},{29,28}} | collective-permute-start | bytes 3145736 | tf_op jit(solution)/shard_map/ppermute | solution.py:916
  413.0 26.3 %copy-start.11 = (bf16[512,1024]{1,0:T(8,128)(2,1)}, bf16[512,1024]{1,0:T(8,128)(2,1)S(1)}, u32[]{:S(2)}) copy-start(bf16[512,1024]{1,0:T(8,128)(2,1)S(1)} %collective-permute-done.17.refs_3_) | copy-start | bytes 3145732
  413.0 24.3 %collective-permute-start.19 = (bf16[512,1024]{1,0:T(8,128)(2,1)S(1)}, bf16[512,1024]{1,0:T(8,128)(2,1)}, u32[]{:S(2)}, u32[]{:S(2)}) collective-permute-start(bf16[512,1024]{1,0:T(8,128)(2,1)S(1)} %collective-permute-done.17.refs_3_), channel_id=1, source_target_pairs={{2,3},{6,7},{10,11},{14,15},{18,19},{22,23},{26,27},{30,31}} | collective-permute-start | bytes 3145736 | tf_op jit(solution)/shard_map/ppermute | solution.py:915
  439.2 8.4 %copy-start.1 = (bf16[8,48,1024]{2,1,0:T(8,128)(2,1)S(1)}, bf16[8,48,1024]{2,1,0:T(8,128)(2,1)}, u32[]{:S(2)}) copy-start(bf16[8,48,1024]{2,1,0:T(8,128)(2,1)} %param.35) | copy-start | bytes 2359300
Sparse Core Ops, SparseCore 0:
  10.9 200.0 all-gather.5
  231.1 85.9 all-gather.7
  358.5 34.2 all-gather.9
